TPU v7x, 256 devices: a whole 4x4x8 slice. The times are simulated.
256 devices in a mesh: inst: 8 (over x, core), lab: 32 (over z, y).
Axes of the slice: x: 4, y: 4, z: 8, core: 2. Of those that a mesh axis runs over, the one named last changes fastest.
Arguments:
- features: bfloat16 [4096, 768], P('inst'), may hold values from -6 to 6
- tile_rows: int32 [2048], P(('inst', 'lab')), may hold values from 0 to 1, as said below
- tile_labels: int32 [2048], P(('inst', 'lab')), may hold values from 0 to 7
- tile_values: bfloat16 [2048, 256, 256], P(('inst', 'lab')), may hold values from 0 to 1
- cluster_ids: int32 [65536], P(('lab', 'inst')), may hold values from 0 to 8191, as said below
Outputs:
- label_embed: float32 [65536, 768], P(('lab', 'inst'))
- centroids: float32 [8192, 768], P(('inst', 'lab'))
Inputs may be any that keep to these rules, and one draw needn't show every extreme that they name: Within each block of 8 entries the pairs (tile_rows, tile_labels) are distinct. Within each aligned block of 256 labels, at most 2 labels have clusters with the same value of cluster_ids // 32, and that many is reached in every block.
All inputs are finite; a program needn't handle non-finite values.
Results may differ from a plain program's by a relative error of at most 0.01.
Values may be sent and summed in bfloat16 or wider, within the bound.
No kernel may reach another device: no remote copies, remote signals or barrier semaphores. Data moves between devices by JAX's collectives and lax.ppermute only.
A program may use at most 128 MiB of HBM per device.

v0:
```python
import jax
import jax.numpy as jnp
from jax import lax
from jax.sharding import PartitionSpec as P

CL_OWN = 32


def unit_rows(matrix):
    return matrix * lax.rsqrt(jnp.sum(matrix * matrix, axis=-1, keepdims=True) + 1e-06)


def shards(features, tile_rows, tile_labels, tile_values, cluster_ids):
    tile = tile_values.shape[1]
    width = features.shape[1]
    normed = unit_rows(features.astype(jnp.float32)).astype(jnp.bfloat16)
    row_tiles = features.shape[0] // tile
    lab_tiles = cluster_ids.shape[0] * lax.axis_size("inst") // tile
    place = tile_rows * lab_tiles + tile_labels
    dense = jnp.zeros((row_tiles * lab_tiles, tile, tile), jnp.bfloat16).at[place].set(tile_values)
    dense = dense.reshape(row_tiles, lab_tiles, tile, tile)
    shaped = normed.reshape(row_tiles, tile, width)
    partial_value = jnp.einsum("ijrl,ird->jld", dense, shaped, preferred_element_type=jnp.float32)
    partial_value = (
        partial_value.reshape(lab_tiles * tile, width).astype(jnp.bfloat16).astype(jnp.float32)
    )
    summed = lax.psum_scatter(
        partial_value.astype(jnp.bfloat16), "inst", scatter_dimension=0, tiled=True
    ).astype(jnp.float32)
    label_embed = unit_rows(summed)
    wanted = lax.iota(jnp.int32, CL_OWN * lax.axis_size(("inst", "lab")))
    member = (cluster_ids[None, :] == wanted[:, None]).astype(jnp.float32)
    cluster_sums = lax.psum_scatter(
        jnp.dot(
            member, label_embed, precision=lax.Precision.HIGHEST, preferred_element_type=jnp.float32
        ),
        ("inst", "lab"),
        scatter_dimension=0,
        tiled=True,
    )
    return (label_embed, unit_rows(cluster_sums))


def solution(mesh):
    return jax.shard_map(
        shards,
        mesh=mesh,
        in_specs=(
            P("inst", None),
            P(("inst", "lab")),
            P(("inst", "lab")),
            P(("inst", "lab"), None, None),
            P(("lab", "inst")),
        ),
        out_specs=(P(("lab", "inst"), None), P(("inst", "lab"), None)),
        check_vma=False,
    )
```

profile of v0, /device:TPU:1, one launch (start us, length us, event | category | flops | bytes accessed | tf_op | source)
XLA Modules:
  0.0 527.9 jit_solution(15909780711480469488)
XLA Ops:
  7.2 0.0 copy-start.4
  7.2 0.0 copy-start.5
  7.2 0.0 copy-start.1
  7.2 0.0 reduce-scatter.3.cloned.1.call-start
  7.2 1.4 fusion.2
  8.7 2.2 fusion.3
  10.9 0.0 copy-done.4
  10.9 0.0 copy-done.5
  10.9 0.2 broadcast_in_dim.4
  11.1 0.0 copy-done.1
  11.1 0.9 scatter_fusion
  12.0 0.0 copy-start.2
  12.0 2.4 copy.7
  14.4 0.0 copy-done.2
  14.4 5.1 bitcast_convert_fusion
  19.5 0.0 copy-start.3
  19.5 0.0 reduce-scatter.3.cloned.1.call-update
  19.5 0.0 reduce-scatter.5.cloned.1.call-start
  19.6 39.5 %reduce-scatter.3.cloned.1.call-done = bf16[256,768]{1,0:T(8,128)(2,1)} async-done(((bf16[2048,768]{1,0:T(8,128)(2,1)}), bf16[256,768]{1,0:T(8,128)(2,1)}) %reduce-scatter.3.cloned.1.call-update) | async-done | bytes 393232 | tf_op jit(solution)/shard_map/reduce_scatter | solution.py:27
  59.0 1.2 fusion.4
  60.2 1.1 convert_multiply_fusion.2
  61.3 0.0 copy-done.3
  61.3 0.0 copy-start
  61.4 13.8 %fusion = f32[8192,768]{1,0:T(8,128)} fusion(f32[256,768]{1,0:T(8,128)S(1)} %convert_multiply_fusion.2, s32[256]{0:T(256)S(1)} %copy-done.3), kind=kOutput, calls=%fused_computation.2 | convolution fusion | flops 19329449984 | bytes 25953280 | tf_op jit(solution)/shard_map/dot_general | solution.py:34
  75.2 0.0 copy-done
  75.2 0.0 reduce-scatter.5.cloned.1.call-update
  75.2 443.3 %reduce-scatter.5.cloned.1.call-done = f32[32,768]{1,0:T(8,128)} async-done(((f32[8192,768]{1,0:T(8,128)}), f32[32,768]{1,0:T(8,128)}) %reduce-scatter.5.cloned.1.call-update) | async-done | bytes 98320 | tf_op jit(solution)/shard_map/reduce_scatter | solution.py:33
  518.5 1.0 multiply_reduce_fusion
  519.5 1.6 broadcast_multiply_fusion
  (4 shorter events, 0.0 us)
Async XLA Ops:
  7.2 3.7 copy-start.4
  7.2 3.7 copy-start.5
  7.2 3.9 copy-start.1
  7.2 51.8 %reduce-scatter.3.cloned.1.call-start = ((), (), s32[]{:S(2)}) async-start(), calls=%async_computation.2 | async-start | bytes 3538944 | tf_op jit(solution)/shard_map/reduce_scatter | solution.py:27
  12.0 2.4 copy-start.2
  19.5 41.8 %copy-start.3 = (s32[256]{0:T(256)S(1)}, s32[256]{0:T(256)}, u32[]{:S(2)}) copy-start(s32[256]{0:T(256)} %param.9) | copy-start | bytes 3076
  19.5 498.9 %reduce-scatter.5.cloned.1.call-start = ((), (), s32[]{:S(2)}) async-start(), calls=%async_computation.3 | async-start | bytes 25264128 | tf_op jit(solution)/shard_map/reduce_scatter | solution.py:33
  61.3 13.8 %copy-start = (f32[256,768]{1,0:T(8,128)}, f32[256,768]{1,0:T(8,128)S(1)}, u32[]{:S(2)}) copy-start(f32[256,768]{1,0:T(8,128)S(1)} %convert_multiply_fusion.2) | copy-start | bytes 2359300
Sparse Core Ops, SparseCore 0:
  19.6 39.3 reduce-scatter.2
  75.3 443.1 reduce-scatter.4
where the time goes:
time: 532 us; the launch traced here: 528 us
  waiting for transfers between devices  483 us (91%)
  matrix products  18.9 us (4%)
  between operations  14.1 us (3%)
  other arithmetic  8.58 us (2%)
    reduce_scatter x1, waiting for transfers between devices, shards(): lax.psum_scatter(jnp.dot(member, label_embed, precision=lax.Precision.HIG...  443 us
    reduce_scatter x1, waiting for transfers between devices, shards(): lax.psum_scatter(partial_value.astype(jnp.bfloat16), 'inst', scatter_dime...  39.5 us
    dot_general x1, matrix products, shards(): jnp.dot(member, label_embed, precision=lax.Precision.HIGHEST, preferred_e...  13.8 us
  transfers between devices with their start and end apart: 2, of which 2 were waited for; matrix products, arithmetic and copies ran while one was open for 0% of the time, Pallas kernels for 0%

commit v1 on v0

v1 whole, which is shorter than its diff:
```python
import functools

import jax
import jax.numpy as jnp
from jax import lax
from jax.experimental import pallas as pl
from jax.experimental.pallas import tpu as pltpu
from jax.sharding import PartitionSpec as P

CL_OWN = 32
TILE = 256
SLOTS = 2
LANES = 128
BF = jnp.bfloat16
F32 = jnp.float32


def full(shape):
    return pl.BlockSpec(shape, lambda *_: (0,) * len(shape))


def tiles_in(rows_hbm, labs_hbm, vals_hbm, rows_ref, labs_ref, vals_ref, sems):
    pairs = ((rows_hbm, rows_ref), (labs_hbm, labs_ref), (vals_hbm, vals_ref))
    return [pltpu.make_async_copy(src, dst, sems.at[k]) for k, (src, dst) in enumerate(pairs)]


def half_product(other, chips, rows_ref, labs_ref, vals_ref, x_ref, out_ref, acc_ref):
    tiles, tile = vals_ref.shape[0], vals_ref.shape[1]
    me = lax.axis_index("inst")
    core = lax.rem(me, 2)
    chip = lax.div(me, 2)
    if other:
        core = 1 - core
    for d in range(chips):
        lab = lax.rem(chip + d, chips) * 2 + core
        acc_ref[...] = jnp.zeros_like(acc_ref)
        for r in range(x_ref.shape[0] // tile):
            n = jnp.int32(-1)
            for t in range(tiles):
                n = jnp.where((rows_ref[t] == r) & (labs_ref[t] == lab), t, n)

            @pl.when(n >= 0)
            def _(n=n, r=r):
                acc_ref[...] += lax.dot_general(
                    vals_ref[n],
                    x_ref[r * tile : (r + 1) * tile, :],
                    (((0,), (0,)), ((), ())),
                    preferred_element_type=F32,
                )

        out_ref[d * tile : (d + 1) * tile, :] = acc_ref[...].astype(BF)


def first_kernel(
    chips, rows_hbm, labs_hbm, vals_hbm, feat_hbm, out_ref, x_ref, rows_ref, labs_ref, vals_ref, feat_ref, acc_ref, sems
):
    feat_in = pltpu.make_async_copy(feat_hbm, feat_ref, sems.at[3])
    copies = tiles_in(rows_hbm, labs_hbm, vals_hbm, rows_ref, labs_ref, vals_ref, sems)
    feat_in.start()
    for copy in copies:
        copy.start()
    feat_in.wait()
    f = feat_ref[...].astype(F32)
    x_ref[...] = (f * lax.rsqrt(jnp.sum(f * f, axis=-1, keepdims=True) + 1e-06)).astype(BF)
    for copy in copies:
        copy.wait()
    half_product(True, chips, rows_ref, labs_ref, vals_ref, x_ref, out_ref, acc_ref)


def second_kernel(chips, rows_hbm, labs_hbm, vals_hbm, x_ref, out_ref, rows_ref, labs_ref, vals_ref, acc_ref, sems):
    copies = tiles_in(rows_hbm, labs_hbm, vals_hbm, rows_ref, labs_ref, vals_ref, sems)
    for copy in copies:
        copy.start()
    for copy in copies:
        copy.wait()
    half_product(False, chips, rows_ref, labs_ref, vals_ref, x_ref, out_ref, acc_ref)


def pack_kernel(own_ref, mate_ref, a_ref, b_ref, c_ref, ids_ref, emb_ref, out_ref, stage_ref):
    labs, width = emb_ref.shape
    cols = width // LANES
    step = (cols + 1) * SLOTS
    summed = own_ref[...].astype(F32) + mate_ref[...].astype(F32)
    summed = summed + a_ref[...].astype(F32) + b_ref[...].astype(F32) + c_ref[...].astype(F32)
    unit = summed * lax.rsqrt(jnp.sum(summed * summed, axis=-1, keepdims=True) + 1e-06)
    emb_ref[...] = unit
    unit = unit.astype(BF)
    ids = ids_ref[...]
    down = lax.broadcasted_iota(jnp.int32, (labs, labs), 0)
    across = lax.broadcasted_iota(jnp.int32, (labs, labs), 1)
    ids_down = jnp.sum(jnp.where(down == across, ids, 0), axis=1, keepdims=True)
    owner = ids // CL_OWN
    earlier = (ids_down // CL_OWN == owner) & (down < across)
    rank = jnp.sum(earlier.astype(jnp.int32), axis=0, keepdims=True)
    inside = jnp.broadcast_to((ids_down % CL_OWN).astype(F32), (labs, LANES)).astype(BF)
    for slot in range(SLOTS):
        pick = jnp.where((down == owner) & (rank == slot), 1.0, 0.0).astype(BF)
        moved = jnp.dot(pick, unit, preferred_element_type=F32)
        for col in range(cols):
            stage_ref[pl.ds(col * SLOTS + slot, labs, stride=step), :] = moved[:, col * LANES : (col + 1) * LANES]
        stage_ref[pl.ds(cols * SLOTS + slot, labs, stride=step), :] = jnp.dot(
            pick, inside, preferred_element_type=F32
        )
    out_ref.reshape(labs * step, LANES)[...] = stage_ref[...].astype(BF)


def combine_kernel(got_ref, out_ref, stage_ref):
    owners, cols = got_ref.shape[0], got_ref.shape[1] - 1
    step = (cols + 1) * SLOTS
    stage_ref[...] = got_ref.reshape(owners * step, LANES)[...].astype(F32)
    lane = lax.broadcasted_iota(jnp.int32, (owners, LANES), 1).astype(F32)
    total = jnp.zeros((LANES, cols * LANES), F32)
    for slot in range(SLOTS):
        inside = stage_ref[pl.ds(cols * SLOTS + slot, owners, stride=step), :]
        member = jnp.where(inside == lane, 1.0, 0.0).astype(BF)
        rows = jnp.concatenate(
            [stage_ref[pl.ds(col * SLOTS + slot, owners, stride=step), :].astype(BF) for col in range(cols)], axis=1
        )
        total = total + lax.dot_general(member, rows, (((0,), (0,)), ((), ())), preferred_element_type=F32)
    sums = total[:CL_OWN]
    out_ref[...] = sums * lax.rsqrt(jnp.sum(sums * sums, axis=-1, keepdims=True) + 1e-06)


def shards(features, tile_rows, tile_labels, tile_values, cluster_ids):
    tiles, tile = tile_values.shape[:2]
    insts, width = features.shape
    labs = cluster_ids.shape[0]
    n_inst = lax.axis_size("inst")
    owners = lax.axis_size(("inst", "lab"))
    chips = n_inst // 2
    cols = width // LANES
    hbm = pl.BlockSpec(memory_space=pltpu.MemorySpace.HBM)
    features, tile_rows, tile_labels, tile_values = (
        pltpu.with_memory_space_constraint(a, pltpu.MemorySpace.HBM)
        for a in (features, tile_rows, tile_labels, tile_values)
    )
    half = jax.ShapeDtypeStruct((chips * tile, width), BF)
    cost = pl.CostEstimate(
        flops=tiles * tile * tile * width, bytes_accessed=2 * (chips + 2) * tile * width, transcendentals=0
    )
    tile_scratch = [pltpu.SMEM((tiles,), jnp.int32)] * 2 + [pltpu.VMEM(tile_values.shape, BF)]
    away, normed = pl.pallas_call(
        functools.partial(first_kernel, chips),
        grid=(1,),
        out_shape=(half, jax.ShapeDtypeStruct((insts, width), BF)),
        in_specs=[hbm] * 4,
        out_specs=(full(half.shape), full((insts, width))),
        scratch_shapes=tile_scratch
        + [pltpu.VMEM((insts, width), BF), pltpu.VMEM((tile, width), F32), pltpu.SemaphoreType.DMA((4,))],
        compiler_params=pltpu.CompilerParams(vmem_limit_bytes=24 << 20),
        cost_estimate=cost,
        name="away_half",
    )(tile_rows, tile_labels, tile_values, features)
    mate = lax.ppermute(away, "inst", [(i, i ^ 1) for i in range(n_inst)])
    own = pl.pallas_call(
        functools.partial(second_kernel, chips),
        grid=(1,),
        out_shape=half,
        in_specs=[hbm] * 3 + [full((insts, width))],
        out_specs=full(half.shape),
        scratch_shapes=tile_scratch + [pltpu.VMEM((tile, width), F32), pltpu.SemaphoreType.DMA((3,))],
        compiler_params=pltpu.CompilerParams(vmem_limit_bytes=24 << 20),
        cost_estimate=cost,
        name="own_half",
    )(tile_rows, tile_labels, tile_values, normed)
    arrived = []
    for d in (1, 3, 2):
        part = slice(d * tile, (d + 1) * tile)
        block = (own[part].astype(F32) + mate[part].astype(F32)).astype(BF)
        arrived.append(lax.ppermute(block, "inst", [(i, (i + 2 * d) % n_inst) for i in range(n_inst)]))
    block = full((tile, width))
    message = (owners, cols + 1, SLOTS, LANES)
    label_embed, packed = pl.pallas_call(
        pack_kernel,
        grid=(1,),
        out_shape=(jax.ShapeDtypeStruct((labs, width), F32), jax.ShapeDtypeStruct(message, BF)),
        in_specs=[block] * 5 + [full((1, labs))],
        out_specs=(full((labs, width)), full(message)),
        scratch_shapes=[pltpu.VMEM((owners * (cols + 1) * SLOTS, LANES), F32)],
        compiler_params=pltpu.CompilerParams(vmem_limit_bytes=24 << 20),
        name="pack",
    )(own, mate, *arrived, cluster_ids.reshape(1, labs))
    got = lax.all_to_all(packed, ("inst", "lab"), 0, 0, tiled=True)
    centroids = pl.pallas_call(
        combine_kernel,
        grid=(1,),
        out_shape=jax.ShapeDtypeStruct((CL_OWN, width), F32),
        in_specs=[full(message)],
        out_specs=full((CL_OWN, width)),
        scratch_shapes=[pltpu.VMEM((owners * (cols + 1) * SLOTS, LANES), F32)],
        compiler_params=pltpu.CompilerParams(vmem_limit_bytes=24 << 20),
        name="combine",
    )(got)
    return label_embed, centroids


def solution(mesh):
    return jax.shard_map(
        shards,
        mesh=mesh,
        in_specs=(
            P("inst", None),
            P(("inst", "lab")),
            P(("inst", "lab")),
            P(("inst", "lab"), None, None),
            P(("lab", "inst")),
        ),
        out_specs=(P(("lab", "inst"), None), P(("inst", "lab"), None)),
        check_vma=False,
    )
```

time: 532 us -> 76 us (0.14)
  waiting for transfers between devices: 483 us -> 19 us
  blocking collectives: 0 us -> 41.7 us
  matrix products: 18.9 us -> 0 us
  between operations: 14.1 us -> 0.66 us
  Pallas kernels: 0 us -> 9.03 us
  other arithmetic: 8.58 us -> 0.28 us
  starting transfers between devices: 0.08 us -> 5.58 us
    reduce_scatter x2 -> x0, waiting for transfers between devices: 483 us -> none  [the longest x1 443 us: shards(): lax.psum_scatter(jnp.dot(member, label_embed, precision=lax.Precision.HIG...]
    all_to_all x0 -> x1, blocking collectives: none -> 41.7 us  [shards(): got = lax.all_to_all(packed, ('inst', 'lab'), 0, 0, tiled=True)]
    ppermute x0 -> x4, waiting for transfers between devices: none -> 19 us  [the longest x3 18.5 us: shards(): lax.ppermute(block, 'inst', [(i, (i + 2 * d) % n_inst) for i in range(n_i...]
    dot_general x2 -> x0, matrix products: 18.9 us -> none  [the longest x1 13.8 us: shards(): jnp.dot(member, label_embed, precision=lax.Precision.HIGHEST, preferred_e...]
    pallas_call x0 -> x4, Pallas kernels: none -> 9.03 us  [the longest x1 3.39 us: shards(): pl.pallas_call(functools.partial(first_kernel, chips), grid=(1,), out_sha...]
    ppermute x0 -> x4, starting transfers between devices: none -> 5.58 us  [the longest x1 3.03 us: shards(): mate = lax.ppermute(away, 'inst', [(i, i ^ 1) for i in range(n_inst)])]
  transfers between devices with their start and end apart: 2 -> 4, of which waited for: 2 -> 4; matrix products, arithmetic and copies ran while one was open for 0% -> 0% of each run, Pallas kernels for 0% -> 3%
where the time goes in v1:
time: 76 us; the launch traced here: 76.2 us
  blocking collectives  41.7 us (55%)
  waiting for transfers between devices  19 us (25%)
  Pallas kernels  9.03 us (12%)
  starting transfers between devices  5.58 us (7%)
    all_to_all x1, blocking collectives, shards(): got = lax.all_to_all(packed, ('inst', 'lab'), 0, 0, tiled=True)  41.7 us
    ppermute x3, waiting for transfers between devices, shards(): lax.ppermute(block, 'inst', [(i, (i + 2 * d) % n_inst) for i in range(n_i...  18.5 us
    pallas_call x1, Pallas kernels, shards(): pl.pallas_call(functools.partial(first_kernel, chips), grid=(1,), out_sha...  3.39 us
    ppermute x1, starting transfers between devices, shards(): mate = lax.ppermute(away, 'inst', [(i, i ^ 1) for i in range(n_inst)])  3.03 us
    ppermute x3, starting transfers between devices, shards(): lax.ppermute(block, 'inst', [(i, (i + 2 * d) % n_inst) for i in range(n_i...  2.55 us
    pallas_call x1, Pallas kernels, shards(): pl.pallas_call(functools.partial(second_kernel, chips), grid=(1,), out_sh...  2.53 us
    pallas_call x1, Pallas kernels, shards(): pl.pallas_call(combine_kernel, grid=(1,), out_shape=jax.ShapeDtypeStruct(...  1.69 us
  transfers between devices with their start and end apart: 4, of which 4 were waited for; matrix products, arithmetic and copies ran while one was open for 0% of the time, Pallas kernels for 3%

profile of v1, /device:TPU:1, one launch (start us, length us, event | category | flops | bytes accessed | tf_op | source)
XLA Modules:
  0.0 76.2 jit_solution(11597323520081615288)
XLA Ops:
  0.6 3.4 %away_half.1 = (bf16[1024,768]{1,0:T(8,128)(2,1)S(1)}, bf16[512,768]{1,0:T(8,128)(2,1)S(1)}) custom-call(s32[8]{0:T(128)} %rows_hbm.3, s32[8]{0:T(128)} %labs_hbm.3, bf16[8,256,256]{2,1,0:T(8,128)(2,1)} %vals_hbm.3, bf16[512,768]{1,0:T(8,128)(2,1)} %feat_hbm.1), custom_call_target="tpu_custom_call" | custom-call | flops 402653184 | bytes 2359296 | tf_op jit(solution)/shard_map/away_half/pallas_call | solution.py:142
  4.0 3.0 %collective-permute-start = (bf16[1024,768]{1,0:T(8,128)(2,1)S(1)}, bf16[1024,768]{1,0:T(8,128)(2,1)S(1)}, u32[]{:S(2)}, u32[]{:S(2)}) collective-permute-start(bf16[1024,768]{1,0:T(8,128)(2,1)S(1)} %get-tuple-element.7), channel_id=1, source_target_pairs={{0,32},{32,0},{64,96},{96,64},{128,160},{160,128},{192,224},{224,1... | collective-permute-start | bytes 4718600 | tf_op jit(solution)/shard_map/ppermute | solution.py:154
  7.1 2.5 %own_half.1.own_ref = bf16[1024,768]{1,0:T(8,128)(2,1)S(1)} custom-call(s32[8]{0:T(128)} %rows_hbm.3, s32[8]{0:T(128)} %labs_hbm.3, bf16[8,256,256]{2,1,0:T(8,128)(2,1)} %vals_hbm.3, bf16[512,768]{1,0:T(8,128)(2,1)S(1)} %get-tuple-element.6.x_ref), custom_call_target="tpu_custom_call" | custom-call | flops 402653184 | bytes 2359296 | tf_op jit(solution)/shard_map/own_half/pallas_call | solution.py:155
  9.6 0.0 copy-start
  9.6 0.5 collective-permute-done.mate_ref
  10.1 0.3 add_convert_fusion
  10.4 1.1 %collective-permute-start.3 = (bf16[256,768]{1,0:T(8,128)(2,1)S(1)}, bf16[256,768]{1,0:T(8,128)(2,1)S(1)}, u32[]{:S(2)}, u32[]{:S(2)}) collective-permute-start(bf16[256,768]{1,0:T(8,128)(2,1)S(1)} %get-tuple-element.10), channel_id=1, source_target_pairs={{0,128},{32,160},{64,192},{96,224},{128,0},{160,32},{192,64},{224,... | collective-permute-start | bytes 1179656 | tf_op jit(solution)/shard_map/ppermute | solution.py:170
  11.5 1.2 %collective-permute-start.2 = (bf16[256,768]{1,0:T(8,128)(2,1)S(1)}, bf16[256,768]{1,0:T(8,128)(2,1)S(1)}, u32[]{:S(2)}, u32[]{:S(2)}) collective-permute-start(bf16[256,768]{1,0:T(8,128)(2,1)S(1)} %get-tuple-element.11), channel_id=1, source_target_pairs={{0,192},{32,224},{64,0},{96,32},{128,64},{160,96},{192,128},{224,1... | collective-permute-start | bytes 1179656 | tf_op jit(solution)/shard_map/ppermute | solution.py:170
  12.6 0.3 collective-permute-start.1
  12.9 9.4 %collective-permute-done.3.c_ref = bf16[256,768]{1,0:T(8,128)(2,1)S(1)} collective-permute-done((bf16[256,768]{1,0:T(8,128)(2,1)S(1)}, bf16[256,768]{1,0:T(8,128)(2,1)S(1)}, u32[]{:S(2)}, u32[]{:S(2)}) %collective-permute-start.3) | collective-permute-done | bytes 393248 | tf_op jit(solution)/shard_map/ppermute | solution.py:170
  22.3 6.9 %collective-permute-done.2.b_ref = bf16[256,768]{1,0:T(8,128)(2,1)S(1)} collective-permute-done((bf16[256,768]{1,0:T(8,128)(2,1)S(1)}, bf16[256,768]{1,0:T(8,128)(2,1)S(1)}, u32[]{:S(2)}, u32[]{:S(2)}) %collective-permute-start.2) | collective-permute-done | bytes 393248 | tf_op jit(solution)/shard_map/ppermute | solution.py:170
  29.2 2.2 %collective-permute-done.1.a_ref = bf16[256,768]{1,0:T(8,128)(2,1)S(1)} collective-permute-done((bf16[256,768]{1,0:T(8,128)(2,1)S(1)}, bf16[256,768]{1,0:T(8,128)(2,1)S(1)}, u32[]{:S(2)}, u32[]{:S(2)}) %collective-permute-start.1) | collective-permute-done | bytes 393248 | tf_op jit(solution)/shard_map/ppermute | solution.py:170
  31.4 0.0 copy-done
  31.4 1.4 %pack.1 = (f32[256,768]{1,0:T(8,128)}, bf16[256,7,2,128]{3,2,1,0:T(2,128)(2,1)S(1)}) custom-call(bf16[1024,768]{1,0:T(8,128)(2,1)S(1)} %own_half.1.own_ref, bf16[1024,768]{1,0:T(8,128)(2,1)S(1)} %collective-permute-done.mate_ref, bf16[256,768]{1,0:T(8,128)(2,1)S(1)} %collective-permute-done.1.a_ref, bf16[256,768]{1,0:T(8,128)(2,1)S(1)} %collective-permute-done.2.b_ref, ...), custom_call_target="tpu_custom_call" | custom-call | tf_op jit(solution)/shard_map/pack/pallas_call | solution.py:173
  32.9 41.7 %all_to_all.5.got_ref = bf16[256,7,2,128]{3,2,1,0:T(2,128)(2,1)S(1)} all-to-all(bf16[256,7,2,128]{3,2,1,0:T(2,128)(2,1)S(1)} %get-tuple-element.9), channel_id=1, replica_groups=mesh['inst'=8,'lab'=32] {'inst','lab'}, dimensions={0} | all-to-all | bytes 1835008 | tf_op jit(solution)/shard_map/all_to_all | solution.py:183
  74.5 1.7 %combine.1 = f32[32,768]{1,0:T(8,128)} custom-call(bf16[256,7,2,128]{3,2,1,0:T(2,128)(2,1)S(1)} %all_to_all.5.got_ref), custom_call_target="tpu_custom_call" | custom-call | tf_op jit(solution)/shard_map/combine/pallas_call | solution.py:184
Async XLA Ops:
  4.0 6.1 %collective-permute-start = (bf16[1024,768]{1,0:T(8,128)(2,1)S(1)}, bf16[1024,768]{1,0:T(8,128)(2,1)S(1)}, u32[]{:S(2)}, u32[]{:S(2)}) collective-permute-start(bf16[1024,768]{1,0:T(8,128)(2,1)S(1)} %get-tuple-element.7), channel_id=1, source_target_pairs={{0,32},{32,0},{64,96},{96,64},{128,160},{160,128},{192,224},{224,1... | collective-permute-start | bytes 4718600 | tf_op jit(solution)/shard_map/ppermute | solution.py:154
  9.6 21.8 %copy-start = (s32[256]{0:T(256)S(1)}, s32[256]{0:T(256)}, u32[]{:S(2)}) copy-start(s32[256]{0:T(256)} %param.9) | copy-start | bytes 3076
  10.4 12.0 %collective-permute-start.3 = (bf16[256,768]{1,0:T(8,128)(2,1)S(1)}, bf16[256,768]{1,0:T(8,128)(2,1)S(1)}, u32[]{:S(2)}, u32[]{:S(2)}) collective-permute-start(bf16[256,768]{1,0:T(8,128)(2,1)S(1)} %get-tuple-element.10), channel_id=1, source_target_pairs={{0,128},{32,160},{64,192},{96,224},{128,0},{160,32},{192,64},{224,... | collective-permute-start | bytes 1179656 | tf_op jit(solution)/shard_map/ppermute | solution.py:170
  11.5 17.7 %collective-permute-start.2 = (bf16[256,768]{1,0:T(8,128)(2,1)S(1)}, bf16[256,768]{1,0:T(8,128)(2,1)S(1)}, u32[]{:S(2)}, u32[]{:S(2)}) collective-permute-start(bf16[256,768]{1,0:T(8,128)(2,1)S(1)} %get-tuple-element.11), channel_id=1, source_target_pairs={{0,192},{32,224},{64,0},{96,32},{128,64},{160,96},{192,128},{224,1... | collective-permute-start | bytes 1179656 | tf_op jit(solution)/shard_map/ppermute | solution.py:170
  12.6 18.8 %collective-permute-start.1 = (bf16[256,768]{1,0:T(8,128)(2,1)S(1)}, bf16[256,768]{1,0:T(8,128)(2,1)S(1)}, u32[]{:S(2)}, u32[]{:S(2)}) collective-permute-start(bf16[256,768]{1,0:T(8,128)(2,1)S(1)} %get-tuple-element.12), channel_id=1, source_target_pairs={{0,64},{32,96},{64,128},{96,160},{128,192},{160,224},{192,0},{224,... | collective-permute-start | bytes 1179656 | tf_op jit(solution)/shard_map/ppermute | solution.py:170

commit v2 on v1

v2 whole, which is shorter than its diff:
```python
import functools

import jax
import jax.numpy as jnp
from jax import lax
from jax.experimental import pallas as pl
from jax.experimental.pallas import tpu as pltpu
from jax.sharding import Mesh
from jax.sharding import PartitionSpec as P

CL_OWN = 32
SLOTS = 2
LANES = 128
CORES = 2
Y_CHIPS = 4
INST = ("x", "c")
LAB = ("z", "y")
BF = jnp.bfloat16
F32 = jnp.float32


def full(shape):
    return pl.BlockSpec(shape, lambda *_: (0,) * len(shape))


def params(**kwargs):
    return pltpu.CompilerParams(vmem_limit_bytes=24 << 20, **kwargs)


def in_hbm(array):
    return pltpu.with_memory_space_constraint(array, pltpu.MemorySpace.HBM)


def tiles_in(rows_hbm, labs_hbm, vals_hbm, rows_ref, labs_ref, vals_ref, sems):
    pairs = ((rows_hbm, rows_ref), (labs_hbm, labs_ref), (vals_hbm, vals_ref))
    return [pltpu.make_async_copy(src, dst, sems.at[k]) for k, (src, dst) in enumerate(pairs)]


def product(other, steps, rows_ref, labs_ref, vals_ref, x_ref, out_ref, acc_ref):
    tiles, tile = vals_ref.shape[0], vals_ref.shape[1]
    core = lax.axis_index("c")
    if other:
        core = 1 - core
    for k, step in enumerate(steps):
        lab = lax.rem(lax.axis_index("x") + step, lax.axis_size("x")) * CORES + core
        acc_ref[...] = jnp.zeros_like(acc_ref)
        for r in range(x_ref.shape[0] // tile):
            n = jnp.int32(-1)
            for t in range(tiles):
                n = jnp.where((rows_ref[t] == r) & (labs_ref[t] == lab), t, n)

            @pl.when(n >= 0)
            def _(n=n, r=r):
                acc_ref[...] += lax.dot_general(
                    vals_ref[n],
                    x_ref[r * tile : (r + 1) * tile, :],
                    (((0,), (0,)), ((), ())),
                    preferred_element_type=F32,
                )

        out_ref[k * tile : (k + 1) * tile, :] = acc_ref[...].astype(BF)


def first_kernel(
    steps, rows_hbm, labs_hbm, vals_hbm, feat_hbm, out_ref, x_ref, rows_ref, labs_ref, vals_ref, feat_ref, acc_ref, sems
):
    feat_in = pltpu.make_async_copy(feat_hbm, feat_ref, sems.at[3])
    copies = tiles_in(rows_hbm, labs_hbm, vals_hbm, rows_ref, labs_ref, vals_ref, sems)
    feat_in.start()
    for copy in copies:
        copy.start()
    feat_in.wait()
    f = feat_ref[...].astype(F32)
    x_ref[...] = (f * lax.rsqrt(jnp.sum(f * f, axis=-1, keepdims=True) + 1e-06)).astype(BF)
    for copy in copies:
        copy.wait()
    product(True, steps, rows_ref, labs_ref, vals_ref, x_ref, out_ref, acc_ref)


def later_kernel(jobs, rows_hbm, labs_hbm, vals_hbm, x_ref, *refs):
    out_refs, (rows_ref, labs_ref, vals_ref, acc_ref, sems) = refs[: len(jobs)], refs[len(jobs) :]
    copies = tiles_in(rows_hbm, labs_hbm, vals_hbm, rows_ref, labs_ref, vals_ref, sems)
    for copy in copies:
        copy.start()
    for copy in copies:
        copy.wait()
    for (other, steps), out_ref in zip(jobs, out_refs):
        product(other, steps, rows_ref, labs_ref, vals_ref, x_ref, out_ref, acc_ref)


def route_kernel(ids_ref, place_ref, inside_ref):
    slots, owners, labs = place_ref.shape
    ids = ids_ref[...]
    down = lax.broadcasted_iota(jnp.int32, (labs, labs), 0)
    across = lax.broadcasted_iota(jnp.int32, (labs, labs), 1)
    ids_down = jnp.sum(jnp.where(down == across, ids, 0), axis=1, keepdims=True)
    owner = ids // CL_OWN
    earlier = (ids_down // CL_OWN == owner) & (down < across)
    rank = jnp.sum(earlier.astype(jnp.int32), axis=0, keepdims=True)
    here = lax.broadcasted_iota(jnp.int32, (owners, labs), 0) == owner
    for slot in range(slots):
        place_ref[slot] = jnp.where(here & (rank == slot), 1.0, 0.0).astype(BF)
    inside_ref[...] = jnp.broadcast_to((ids_down % CL_OWN).astype(F32), inside_ref.shape).astype(BF)


def ring_kernel(own_ref, mate_ref, up_ref, down_ref, plus_ref, minus_ref):
    tile = plus_ref.shape[0]
    half = tile // 2

    def pair(start):
        return own_ref[start : start + half].astype(F32) + mate_ref[start : start + half].astype(F32)

    plus_ref[:half] = (pair(tile) + up_ref[...].astype(F32)).astype(BF)
    plus_ref[half:] = pair(tile + half).astype(BF)
    minus_ref[:half] = pair(2 * tile).astype(BF)
    minus_ref[half:] = (pair(2 * tile + half) + down_ref[...].astype(F32)).astype(BF)


def pack_kernel(own_ref, mate_ref, a_ref, b_ref, place_ref, inside_ref, emb_ref, out_ref, stage_ref):
    width = emb_ref.shape[1]
    slots, owners = place_ref.shape[:2]
    cols = width // LANES
    step = (cols + 1) * slots
    summed = own_ref[...].astype(F32) + mate_ref[...].astype(F32)
    summed = summed + a_ref[...].astype(F32) + b_ref[...].astype(F32)
    unit = summed * lax.rsqrt(jnp.sum(summed * summed, axis=-1, keepdims=True) + 1e-06)
    emb_ref[...] = unit
    unit = unit.astype(BF)
    for slot in range(slots):
        moved = jnp.dot(place_ref[slot], unit, preferred_element_type=F32)
        for col in range(cols):
            stage_ref[pl.ds(col * slots + slot, owners, stride=step), :] = moved[:, col * LANES : (col + 1) * LANES]
        stage_ref[pl.ds(cols * slots + slot, owners, stride=step), :] = jnp.dot(
            place_ref[slot], inside_ref[...], preferred_element_type=F32
        )
    out_ref.reshape(owners * step, LANES)[...] = stage_ref[...].astype(BF)


def combine_kernel(got_ref, out_ref, stage_ref):
    owners, cols = got_ref.shape[0], got_ref.shape[1] - 1
    step = (cols + 1) * SLOTS
    stage_ref[...] = got_ref.reshape(owners * step, LANES)[...].astype(F32)
    lane = lax.broadcasted_iota(jnp.int32, (owners, LANES), 1).astype(F32)
    total = jnp.zeros((LANES, cols * LANES), F32)
    for slot in range(SLOTS):
        inside = stage_ref[pl.ds(cols * SLOTS + slot, owners, stride=step), :]
        member = jnp.where(inside == lane, 1.0, 0.0).astype(BF)
        rows = jnp.concatenate(
            [stage_ref[pl.ds(col * SLOTS + slot, owners, stride=step), :].astype(BF) for col in range(cols)], axis=1
        )
        total = total + lax.dot_general(member, rows, (((0,), (0,)), ((), ())), preferred_element_type=F32)
    sums = total[:CL_OWN]
    out_ref[...] = sums * lax.rsqrt(jnp.sum(sums * sums, axis=-1, keepdims=True) + 1e-06)


def shards(features, tile_rows, tile_labels, tile_values, cluster_ids):
    features, tile_rows, tile_labels, tile_values = (
        in_hbm(a) for a in (features, tile_rows, tile_labels, tile_values)
    )
    tiles, tile = tile_values.shape[:2]
    insts, width = features.shape
    labs = cluster_ids.shape[0]
    chips = lax.axis_size("x")
    owners = lax.axis_size(INST + LAB)
    cols = width // LANES
    hbm = pl.BlockSpec(memory_space=pltpu.MemorySpace.HBM)
    tile_scratch = [pltpu.SMEM((tiles,), jnp.int32)] * 2 + [pltpu.VMEM(tile_values.shape, BF)]
    far_steps, near_steps = (2,), (0, 1, 3)

    def product_cost(steps):
        return pl.CostEstimate(
            flops=len(steps) * tile * tile * width * 2,
            bytes_accessed=2 * (tiles * tile * tile + insts * width + len(steps) * tile * width),
            transcendentals=0,
        )

    far_away, normed = pl.pallas_call(
        functools.partial(first_kernel, far_steps),
        grid=(1,),
        out_shape=(jax.ShapeDtypeStruct((tile, width), BF), jax.ShapeDtypeStruct((insts, width), BF)),
        in_specs=[hbm] * 4,
        out_specs=(full((tile, width)), full((insts, width))),
        scratch_shapes=tile_scratch
        + [pltpu.VMEM((insts, width), BF), pltpu.VMEM((tile, width), F32), pltpu.SemaphoreType.DMA((4,))],
        compiler_params=params(),
        cost_estimate=product_cost(far_steps),
        name="far_away",
    )(tile_rows, tile_labels, tile_values, features)

    def later(name, x, *jobs):
        shapes = [(len(steps) * tile, width) for _, steps in jobs]
        return pl.pallas_call(
            functools.partial(later_kernel, jobs),
            grid=(1,),
            out_shape=[jax.ShapeDtypeStruct(shape, BF) for shape in shapes],
            in_specs=[hbm] * 3 + [full((insts, width))],
            out_specs=[full(shape) for shape in shapes],
            scratch_shapes=tile_scratch + [pltpu.VMEM((tile, width), F32), pltpu.SemaphoreType.DMA((3,))],
            compiler_params=params(),
            cost_estimate=product_cost(sum((steps for _, steps in jobs), ())),
            name=name,
        )(tile_rows, tile_labels, tile_values, x)

    def across(block):
        return lax.ppermute(block, "c", [(0, 1), (1, 0)])

    def along(block, step):
        return lax.ppermute(block, "x", [(i, (i + step) % chips) for i in range(chips)])

    far_mate = across(far_away)
    far_own, near_away = later("far_own", normed, (False, far_steps), (True, near_steps))
    cut = tile // 2
    far = [(far_own[h].astype(F32) + far_mate[h].astype(F32)).astype(BF) for h in (slice(0, cut), slice(cut, tile))]
    ids, normed, near_away, far = lax.optimization_barrier((cluster_ids, normed, near_away, far))
    up = along(far[0], 1)
    down = along(far[1], -1)
    mate = across(near_away)
    (own,) = later("near_own", normed, (False, near_steps))
    place, inside = pl.pallas_call(
        route_kernel,
        grid=(1,),
        out_shape=(jax.ShapeDtypeStruct((SLOTS, owners, labs), BF), jax.ShapeDtypeStruct((labs, LANES), BF)),
        in_specs=[full((1, labs))],
        out_specs=(full((SLOTS, owners, labs)), full((labs, LANES))),
        compiler_params=params(),
        name="route",
    )(ids.reshape(1, labs))
    block = full((tile, width))
    plus, minus = pl.pallas_call(
        ring_kernel,
        grid=(1,),
        out_shape=[jax.ShapeDtypeStruct((tile, width), BF)] * 2,
        in_specs=[full(own.shape)] * 2 + [full((tile // 2, width))] * 2,
        out_specs=[block] * 2,
        compiler_params=params(),
        name="ring",
    )(own, mate, up, down)
    message = (owners, cols + 1, SLOTS, LANES)
    stage = pltpu.VMEM((owners * (cols + 1) * SLOTS, LANES), F32)
    label_embed, rows = pl.pallas_call(
        pack_kernel,
        grid=(1,),
        out_shape=(jax.ShapeDtypeStruct((labs, width), F32), jax.ShapeDtypeStruct(message, BF)),
        in_specs=[block] * 4 + [full((SLOTS, owners, labs)), full((labs, LANES))],
        out_specs=(full((labs, width)), full(message)),
        scratch_shapes=[stage],
        compiler_params=params(),
        name="pack",
    )(own, mate, along(plus, 1), along(minus, -1), place, inside)
    got = lax.all_to_all(rows, INST + LAB, 0, 0, tiled=True)
    centroids = pl.pallas_call(
        combine_kernel,
        grid=(1,),
        out_shape=jax.ShapeDtypeStruct((CL_OWN, width), F32),
        in_specs=[full(message)],
        out_specs=full((CL_OWN, width)),
        scratch_shapes=[stage],
        compiler_params=params(),
        name="combine",
    )(got)
    return label_embed, centroids


def solution(mesh):
    insts, labs = mesh.devices.shape
    cut = (insts // CORES, CORES, labs // Y_CHIPS, Y_CHIPS)
    return jax.shard_map(
        shards,
        mesh=Mesh(mesh.devices.reshape(cut), INST + LAB),
        in_specs=(P(INST, None), P(INST + LAB), P(INST + LAB), P(INST + LAB, None, None), P(LAB + INST)),
        out_specs=(P(LAB + INST, None), P(INST + LAB, None)),
        check_vma=False,
    )
```

time: 76 us -> 73.9 us (0.972)
  waiting for transfers between devices: 19 us -> 10.2 us
  starting transfers between devices: 5.58 us -> 9.16 us
  Pallas kernels: 9.03 us -> 10.9 us
  blocking collectives: 41.7 us -> 42.5 us
    ppermute x4 -> x6, waiting for transfers between devices: 19 us -> 10.2 us  [the longest x4 10.2 us: along(): lax.ppermute(block, 'x', [(i, (i + step) % chips) for i in range(chips)])]
    ppermute x4 -> x6, starting transfers between devices: 5.58 us -> 9.16 us  [the longest x4 5.42 us: along(): lax.ppermute(block, 'x', [(i, (i + step) % chips) for i in range(chips)])]
    pallas_call x2 -> x5, Pallas kernels: 5.92 us -> 7.68 us  [the longest x2 5.26 us: later(): pl.pallas_call(functools.partial(later_kernel, jobs), grid=(1,), out_shap...]
    all_to_all x1, blocking collectives: 41.7 us -> 42.5 us  [shards(): got = lax.all_to_all(rows, INST + LAB, 0, 0, tiled=True)]
  transfers between devices with their start and end apart: 4 -> 6, of which waited for: 4 -> 2; matrix products, arithmetic and copies ran while one was open for 0% -> 0% of each run, Pallas kernels for 3% -> 8%
where the time goes in v2:
time: 73.9 us; the launch traced here: 73.6 us
  blocking collectives  42.5 us (58%)
  Pallas kernels  10.9 us (15%)
  waiting for transfers between devices  10.2 us (14%)
  starting transfers between devices  9.16 us (12%)
    all_to_all x1, blocking collectives, shards(): got = lax.all_to_all(rows, INST + LAB, 0, 0, tiled=True)  42.5 us
    ppermute x4, waiting for transfers between devices, along(): lax.ppermute(block, 'x', [(i, (i + step) % chips) for i in range(chips)])  10.2 us
    ppermute x4, starting transfers between devices, along(): lax.ppermute(block, 'x', [(i, (i + step) % chips) for i in range(chips)])  5.42 us
    pallas_call x2, Pallas kernels, later(): pl.pallas_call(functools.partial(later_kernel, jobs), grid=(1,), out_shap...  5.26 us
    ppermute x2, starting transfers between devices, across(): return lax.ppermute(block, 'c', [(0, 1), (1, 0)])  3.74 us
    pallas_call x1, Pallas kernels, shards(): pl.pallas_call(functools.partial(first_kernel, far_steps), grid=(1,), out...  1.89 us
    pallas_call x1, Pallas kernels, shards(): pl.pallas_call(combine_kernel, grid=(1,), out_shape=jax.ShapeDtypeStruct(...  1.7 us
    pallas_call x1, Pallas kernels, shards(): pl.pallas_call(pack_kernel, grid=(1,), out_shape=(jax.ShapeDtypeStruct((l...  1.51 us
  transfers between devices with their start and end apart: 6, of which 2 were waited for; matrix products, arithmetic and copies ran while one was open for 0% of the time, Pallas kernels for 8%

profile of v2, /device:TPU:1, one launch (start us, length us, event | category | flops | bytes accessed | tf_op | source)
XLA Modules:
  0.0 73.6 jit_solution(747401357800749402)
XLA Ops:
  0.6 1.9 %far_away.1 = (bf16[256,768]{1,0:T(8,128)(2,1)S(1)}, bf16[512,768]{1,0:T(8,128)(2,1)S(1)}) custom-call(s32[8]{0:T(128)} %rows_hbm.5, s32[8]{0:T(128)} %labs_hbm.5, bf16[8,256,256]{2,1,0:T(8,128)(2,1)} %vals_hbm.5, bf16[512,768]{1,0:T(8,128)(2,1)} %feat_hbm.1), custom_call_target="tpu_custom_call" | custom-call | flops 100663296 | bytes 2228224 | tf_op jit(solution)/shard_map/far_away/pallas_call | solution.py:177
  2.5 3.3 %collective-permute-start = (bf16[256,768]{1,0:T(8,128)(2,1)S(1)}, bf16[256,768]{1,0:T(8,128)(2,1)S(1)}, u32[]{:S(2)}, u32[]{:S(2)}) collective-permute-start(bf16[256,768]{1,0:T(8,128)(2,1)S(1)} %get-tuple-element.20), channel_id=1, source_target_pairs={{0,32},{32,0},{1,33},{33,1},{2,34},{34,2},{3,35},{35,3},{4,36},{36... | collective-permute-start | bytes 1179656 | tf_op jit(solution)/shard_map/ppermute | solution.py:205
  5.9 2.8 %far_own.1 = (bf16[256,768]{1,0:T(8,128)(2,1)S(1)}, bf16[768,768]{1,0:T(8,128)(2,1)S(1)}) custom-call(s32[8]{0:T(128)} %rows_hbm.5, s32[8]{0:T(128)} %labs_hbm.5, bf16[8,256,256]{2,1,0:T(8,128)(2,1)} %vals_hbm.5, bf16[512,768]{1,0:T(8,128)(2,1)S(1)} %get-tuple-element.21.x_ref), custom_call_target="tpu_custom_call" | custom-call | flops 402653184 | bytes 3407872 | tf_op jit(solution)/shard_map/far_own/pallas_call | solution.py:192
  8.7 0.0 collective-permute-done
  8.7 0.1 add_convert_fusion
  8.8 0.4 collective-permute-start.1
  9.2 0.0 collective-permute-start.2
  9.2 2.7 %collective-permute-start.3 = (bf16[128,768]{1,0:T(8,128)(2,1)S(1)}, bf16[128,768]{1,0:T(8,128)(2,1)S(1)}, u32[]{:S(2)}, u32[]{:S(2)}) collective-permute-start(bf16[128,768]{1,0:T(8,128)(2,1)S(1)} %get-tuple-element.24), channel_id=1, source_target_pairs={{0,192},{64,0},{128,64},{192,128},{1,193},{65,1},{129,65},{193,129... | collective-permute-start | bytes 589832 | tf_op jit(solution)/shard_map/ppermute | solution.py:208
  11.9 2.4 %near_own.1.own_ref = bf16[768,768]{1,0:T(8,128)(2,1)S(1)} custom-call(s32[8]{0:T(128)} %rows_hbm.5, s32[8]{0:T(128)} %labs_hbm.5, bf16[8,256,256]{2,1,0:T(8,128)(2,1)} %vals_hbm.5, bf16[512,768]{1,0:T(8,128)(2,1)S(1)} %get-tuple-element.21.x_ref), custom_call_target="tpu_custom_call" | custom-call | flops 301989888 | bytes 3014656 | tf_op jit(solution)/shard_map/near_own/pallas_call | solution.py:192
  14.3 0.0 copy-start
  14.3 2.4 %collective-permute-done.2.up_ref = bf16[128,768]{1,0:T(8,128)(2,1)S(1)} collective-permute-done((bf16[128,768]{1,0:T(8,128)(2,1)S(1)}, bf16[128,768]{1,0:T(8,128)(2,1)S(1)}, u32[]{:S(2)}, u32[]{:S(2)}) %collective-permute-start.2) | collective-permute-done | bytes 196640 | tf_op jit(solution)/shard_map/ppermute | solution.py:208
  16.7 0.0 collective-permute-done.3.down_ref
  16.7 0.0 collective-permute-done.1.mate_ref
  16.7 0.2 ring.1
  17.0 0.1 collective-permute-start.4
  17.1 2.7 %collective-permute-start.5 = (bf16[256,768]{1,0:T(8,128)(2,1)S(1)}, bf16[256,768]{1,0:T(8,128)(2,1)S(1)}, u32[]{:S(2)}, u32[]{:S(2)}) collective-permute-start(bf16[256,768]{1,0:T(8,128)(2,1)S(1)} %get-tuple-element.26), channel_id=1, source_target_pairs={{0,192},{64,0},{128,64},{192,128},{1,193},{65,1},{129,65},{193,129... | collective-permute-start | bytes 1179656 | tf_op jit(solution)/shard_map/ppermute | solution.py:208
  19.7 0.0 copy-done
  19.7 0.3 route.1
  20.1 7.8 %collective-permute-done.4.a_ref = bf16[256,768]{1,0:T(8,128)(2,1)S(1)} collective-permute-done((bf16[256,768]{1,0:T(8,128)(2,1)S(1)}, bf16[256,768]{1,0:T(8,128)(2,1)S(1)}, u32[]{:S(2)}, u32[]{:S(2)}) %collective-permute-start.4) | collective-permute-done | bytes 393248 | tf_op jit(solution)/shard_map/ppermute | solution.py:208
  27.9 0.0 collective-permute-done.5.b_ref
  27.9 1.5 %pack.1 = (f32[256,768]{1,0:T(8,128)}, bf16[256,7,2,128]{3,2,1,0:T(2,128)(2,1)S(1)}) custom-call(bf16[768,768]{1,0:T(8,128)(2,1)S(1)} %near_own.1.own_ref, bf16[768,768]{1,0:T(8,128)(2,1)S(1)} %collective-permute-done.1.mate_ref, bf16[256,768]{1,0:T(8,128)(2,1)S(1)} %collective-permute-done.4.a_ref, bf16[256,768]{1,0:T(8,128)(2,1)S(1)} %collective-permute-done.5.b_ref, ...), custom_call_target="tpu_custom_call" | custom-call | tf_op jit(solution)/shard_map/pack/pallas_call | solution.py:240
  29.4 42.5 %all_to_all.5.got_ref = bf16[256,7,2,128]{3,2,1,0:T(2,128)(2,1)S(1)} all-to-all(bf16[256,7,2,128]{3,2,1,0:T(2,128)(2,1)S(1)} %get-tuple-element.31), channel_id=1, replica_groups=mesh['x'=4,'c'=2,'z'=8,'y'=4] {'x','c','z','y'}, dimensions={0} | all-to-all | bytes 1835008 | tf_op jit(solution)/shard_map/all_to_all | solution.py:250
  71.9 1.7 %combine.1 = f32[32,768]{1,0:T(8,128)} custom-call(bf16[256,7,2,128]{3,2,1,0:T(2,128)(2,1)S(1)} %all_to_all.5.got_ref), custom_call_target="tpu_custom_call" | custom-call | tf_op jit(solution)/shard_map/combine/pallas_call | solution.py:251
Async XLA Ops:
  2.5 6.2 %collective-permute-start = (bf16[256,768]{1,0:T(8,128)(2,1)S(1)}, bf16[256,768]{1,0:T(8,128)(2,1)S(1)}, u32[]{:S(2)}, u32[]{:S(2)}) collective-permute-start(bf16[256,768]{1,0:T(8,128)(2,1)S(1)} %get-tuple-element.20), channel_id=1, source_target_pairs={{0,32},{32,0},{1,33},{33,1},{2,34},{34,2},{3,35},{35,3},{4,36},{36... | collective-permute-start | bytes 1179656 | tf_op jit(solution)/shard_map/ppermute | solution.py:205
  8.8 8.0 %collective-permute-start.1 = (bf16[768,768]{1,0:T(8,128)(2,1)S(1)}, bf16[768,768]{1,0:T(8,128)(2,1)S(1)}, u32[]{:S(2)}, u32[]{:S(2)}) collective-permute-start(bf16[768,768]{1,0:T(8,128)(2,1)S(1)} %get-tuple-element.22), channel_id=1, source_target_pairs={{0,32},{32,0},{1,33},{33,1},{2,34},{34,2},{3,35},{35,3},{4,36},{36... | collective-permute-start | bytes 3538952 | tf_op jit(solution)/shard_map/ppermute | solution.py:205
  9.2 7.5 %collective-permute-start.2 = (bf16[128,768]{1,0:T(8,128)(2,1)S(1)}, bf16[128,768]{1,0:T(8,128)(2,1)S(1)}, u32[]{:S(2)}, u32[]{:S(2)}) collective-permute-start(bf16[128,768]{1,0:T(8,128)(2,1)S(1)} %get-tuple-element.23), channel_id=1, source_target_pairs={{0,64},{64,128},{128,192},{192,0},{1,65},{65,129},{129,193},{193,1... | collective-permute-start | bytes 589832 | tf_op jit(solution)/shard_map/ppermute | solution.py:208
  9.2 7.5 %collective-permute-start.3 = (bf16[128,768]{1,0:T(8,128)(2,1)S(1)}, bf16[128,768]{1,0:T(8,128)(2,1)S(1)}, u32[]{:S(2)}, u32[]{:S(2)}) collective-permute-start(bf16[128,768]{1,0:T(8,128)(2,1)S(1)} %get-tuple-element.24), channel_id=1, source_target_pairs={{0,192},{64,0},{128,64},{192,128},{1,193},{65,1},{129,65},{193,129... | collective-permute-start | bytes 589832 | tf_op jit(solution)/shard_map/ppermute | solution.py:208
  14.3 5.4 %copy-start = (s32[256]{0:T(256)S(1)}, s32[256]{0:T(256)}, u32[]{:S(2)}) copy-start(s32[256]{0:T(256)} %param.9) | copy-start | bytes 3076
  17.0 10.9 %collective-permute-start.4 = (bf16[256,768]{1,0:T(8,128)(2,1)S(1)}, bf16[256,768]{1,0:T(8,128)(2,1)S(1)}, u32[]{:S(2)}, u32[]{:S(2)}) collective-permute-start(bf16[256,768]{1,0:T(8,128)(2,1)S(1)} %get-tuple-element.25), channel_id=1, source_target_pairs={{0,64},{64,128},{128,192},{192,0},{1,65},{65,129},{129,193},{193,1... | collective-permute-start | bytes 1179656 | tf_op jit(solution)/shard_map/ppermute | solution.py:208
  17.1 10.8 %collective-permute-start.5 = (bf16[256,768]{1,0:T(8,128)(2,1)S(1)}, bf16[256,768]{1,0:T(8,128)(2,1)S(1)}, u32[]{:S(2)}, u32[]{:S(2)}) collective-permute-start(bf16[256,768]{1,0:T(8,128)(2,1)S(1)} %get-tuple-element.26), channel_id=1, source_target_pairs={{0,192},{64,0},{128,64},{192,128},{1,193},{65,1},{129,65},{193,129... | collective-permute-start | bytes 1179656 | tf_op jit(solution)/shard_map/ppermute | solution.py:208

commit v3 on v2

--- a/solution.py
+++ b/solution.py
@@ -38,11 +38,12 @@
 
 def product(other, steps, rows_ref, labs_ref, vals_ref, x_ref, out_ref, acc_ref):
     tiles, tile = vals_ref.shape[0], vals_ref.shape[1]
+    chips = lax.axis_size("x")
     core = lax.axis_index("c")
     if other:
         core = 1 - core
     for k, step in enumerate(steps):
-        lab = lax.rem(lax.axis_index("x") + step, lax.axis_size("x")) * CORES + core
+        lab = lax.rem(lax.axis_index("x") + step * (1 - 2 * core) + chips, chips) * CORES + core
         acc_ref[...] = jnp.zeros_like(acc_ref)
         for r in range(x_ref.shape[0] // tile):
             n = jnp.int32(-1)
@@ -77,13 +78,8 @@
     product(True, steps, rows_ref, labs_ref, vals_ref, x_ref, out_ref, acc_ref)
 
 
-def later_kernel(jobs, rows_hbm, labs_hbm, vals_hbm, x_ref, *refs):
-    out_refs, (rows_ref, labs_ref, vals_ref, acc_ref, sems) = refs[: len(jobs)], refs[len(jobs) :]
-    copies = tiles_in(rows_hbm, labs_hbm, vals_hbm, rows_ref, labs_ref, vals_ref, sems)
-    for copy in copies:
-        copy.start()
-    for copy in copies:
-        copy.wait()
+def later_kernel(jobs, rows_ref, labs_ref, vals_ref, x_ref, *refs):
+    out_refs, acc_ref = refs[: len(jobs)], refs[len(jobs)]
     for (other, steps), out_ref in zip(jobs, out_refs):
         product(other, steps, rows_ref, labs_ref, vals_ref, x_ref, out_ref, acc_ref)
 
@@ -103,26 +99,16 @@
     inside_ref[...] = jnp.broadcast_to((ids_down % CL_OWN).astype(F32), inside_ref.shape).astype(BF)
 
 
-def ring_kernel(own_ref, mate_ref, up_ref, down_ref, plus_ref, minus_ref):
-    tile = plus_ref.shape[0]
-    half = tile // 2
-
-    def pair(start):
-        return own_ref[start : start + half].astype(F32) + mate_ref[start : start + half].astype(F32)
-
-    plus_ref[:half] = (pair(tile) + up_ref[...].astype(F32)).astype(BF)
-    plus_ref[half:] = pair(tile + half).astype(BF)
-    minus_ref[:half] = pair(2 * tile).astype(BF)
-    minus_ref[half:] = (pair(2 * tile + half) + down_ref[...].astype(F32)).astype(BF)
-
-
-def pack_kernel(own_ref, mate_ref, a_ref, b_ref, place_ref, inside_ref, emb_ref, out_ref, stage_ref):
+def load_kernel(own_ref, mate_ref, far_ref, out_ref):
+    out_ref[...] = (own_ref[...].astype(F32) + mate_ref[...].astype(F32) + far_ref[...].astype(F32)).astype(BF)
+
+
+def pack_kernel(most_ref, came_ref, place_ref, inside_ref, emb_ref, out_ref, stage_ref):
     width = emb_ref.shape[1]
     slots, owners = place_ref.shape[:2]
     cols = width // LANES
     step = (cols + 1) * slots
-    summed = own_ref[...].astype(F32) + mate_ref[...].astype(F32)
-    summed = summed + a_ref[...].astype(F32) + b_ref[...].astype(F32)
+    summed = most_ref[...] + came_ref[...].astype(F32)
     unit = summed * lax.rsqrt(jnp.sum(summed * summed, axis=-1, keepdims=True) + 1e-06)
     emb_ref[...] = unit
     unit = unit.astype(BF)
@@ -154,18 +140,16 @@
 
 
 def shards(features, tile_rows, tile_labels, tile_values, cluster_ids):
-    features, tile_rows, tile_labels, tile_values = (
-        in_hbm(a) for a in (features, tile_rows, tile_labels, tile_values)
-    )
     tiles, tile = tile_values.shape[:2]
     insts, width = features.shape
     labs = cluster_ids.shape[0]
     chips = lax.axis_size("x")
     owners = lax.axis_size(INST + LAB)
     cols = width // LANES
+    smem = pl.BlockSpec(memory_space=pltpu.MemorySpace.SMEM)
     hbm = pl.BlockSpec(memory_space=pltpu.MemorySpace.HBM)
     tile_scratch = [pltpu.SMEM((tiles,), jnp.int32)] * 2 + [pltpu.VMEM(tile_values.shape, BF)]
-    far_steps, near_steps = (2,), (0, 1, 3)
+    far_steps, near_steps = (2,), (0, 1, -1)
 
     def product_cost(steps):
         return pl.CostEstimate(
@@ -185,7 +169,7 @@
         compiler_params=params(),
         cost_estimate=product_cost(far_steps),
         name="far_away",
-    )(tile_rows, tile_labels, tile_values, features)
+    )(*(in_hbm(a) for a in (tile_rows, tile_labels, tile_values, features)))
 
     def later(name, x, *jobs):
         shapes = [(len(steps) * tile, width) for _, steps in jobs]
@@ -193,9 +177,9 @@
             functools.partial(later_kernel, jobs),
             grid=(1,),
             out_shape=[jax.ShapeDtypeStruct(shape, BF) for shape in shapes],
-            in_specs=[hbm] * 3 + [full((insts, width))],
+            in_specs=[smem] * 2 + [full(tile_values.shape), full((insts, width))],
             out_specs=[full(shape) for shape in shapes],
-            scratch_shapes=tile_scratch + [pltpu.VMEM((tile, width), F32), pltpu.SemaphoreType.DMA((3,))],
+            scratch_shapes=[pltpu.VMEM((tile, width), F32)],
             compiler_params=params(),
             cost_estimate=product_cost(sum((steps for _, steps in jobs), ())),
             name=name,
@@ -205,17 +189,34 @@
         return lax.ppermute(block, "c", [(0, 1), (1, 0)])
 
     def along(block, step):
-        return lax.ppermute(block, "x", [(i, (i + step) % chips) for i in range(chips)])
+        pairs = [(i, i + step * (1 - 2 * c)) for i in range(chips) for c in range(CORES)]
+        pairs = [(i * CORES + k % CORES, j % chips * CORES + k % CORES) for k, (i, j) in enumerate(pairs)]
+        return lax.ppermute(block, INST, pairs)
 
     far_mate = across(far_away)
     far_own, near_away = later("far_own", normed, (False, far_steps), (True, near_steps))
-    cut = tile // 2
-    far = [(far_own[h].astype(F32) + far_mate[h].astype(F32)).astype(BF) for h in (slice(0, cut), slice(cut, tile))]
+    far = (far_own.astype(F32) + far_mate.astype(F32)).astype(BF)
     ids, normed, near_away, far = lax.optimization_barrier((cluster_ids, normed, near_away, far))
-    up = along(far[0], 1)
-    down = along(far[1], -1)
+    far_came = along(far, 1)
     mate = across(near_away)
     (own,) = later("near_own", normed, (False, near_steps))
+
+    def pair(k):
+        return own[k * tile : (k + 1) * tile].astype(F32) + mate[k * tile : (k + 1) * tile].astype(F32)
+
+    free_came = along(pair(2).astype(BF), -1)
+    block = full((tile, width))
+    loaded = pl.pallas_call(
+        load_kernel,
+        grid=(1,),
+        out_shape=jax.ShapeDtypeStruct((tile, width), BF),
+        in_specs=[pl.BlockSpec((tile, width), lambda *_: (1, 0))] * 2 + [block],
+        out_specs=block,
+        compiler_params=params(),
+        name="load",
+    )(own, mate, far_came)
+    came = along(loaded, 1)
+    most = pair(0) + free_came.astype(F32)
     place, inside = pl.pallas_call(
         route_kernel,
         grid=(1,),
@@ -226,27 +227,18 @@
         name="route",
     )(ids.reshape(1, labs))
     block = full((tile, width))
-    plus, minus = pl.pallas_call(
-        ring_kernel,
-        grid=(1,),
-        out_shape=[jax.ShapeDtypeStruct((tile, width), BF)] * 2,
-        in_specs=[full(own.shape)] * 2 + [full((tile // 2, width))] * 2,
-        out_specs=[block] * 2,
-        compiler_params=params(),
-        name="ring",
-    )(own, mate, up, down)
     message = (owners, cols + 1, SLOTS, LANES)
     stage = pltpu.VMEM((owners * (cols + 1) * SLOTS, LANES), F32)
     label_embed, rows = pl.pallas_call(
         pack_kernel,
         grid=(1,),
         out_shape=(jax.ShapeDtypeStruct((labs, width), F32), jax.ShapeDtypeStruct(message, BF)),
-        in_specs=[block] * 4 + [full((SLOTS, owners, labs)), full((labs, LANES))],
+        in_specs=[block] * 2 + [full((SLOTS, owners, labs)), full((labs, LANES))],
         out_specs=(full((labs, width)), full(message)),
         scratch_shapes=[stage],
         compiler_params=params(),
         name="pack",
-    )(own, mate, along(plus, 1), along(minus, -1), place, inside)
+    )(most, came, place, inside)
     got = lax.all_to_all(rows, INST + LAB, 0, 0, tiled=True)
     centroids = pl.pallas_call(
         combine_kernel,

time: 73.9 us -> 70.9 us (0.959)
  starting transfers between devices: 9.16 us -> 5.7 us
  blocking collectives: 42.5 us -> 44.1 us
  Pallas kernels: 10.9 us -> 9.4 us
    ppermute x4 -> x3, starting transfers between devices: 5.42 us -> 2.56 us  [along(): return lax.ppermute(block, INST, pairs)]
    all_to_all x1, blocking collectives: 42.5 us -> 44.1 us  [shards(): got = lax.all_to_all(rows, INST + LAB, 0, 0, tiled=True)]
    pallas_call x2, Pallas kernels: 5.26 us -> 3.9 us  [later(): pl.pallas_call(functools.partial(later_kernel, jobs), grid=(1,), out_shap...]
    ppermute x4 -> x3, waiting for transfers between devices: 10.2 us -> 9.84 us  [along(): return lax.ppermute(block, INST, pairs)]
  transfers between devices with their start and end apart: 6 -> 5, of which waited for: 2 -> 4; matrix products, arithmetic and copies ran while one was open for 0% -> 0% of each run, Pallas kernels for 8% -> 6%
where the time goes in v3:
time: 70.9 us; the launch traced here: 70.4 us
  blocking collectives  44.1 us (62%)
  waiting for transfers between devices  10.1 us (14%)
  Pallas kernels  9.4 us (13%)
  starting transfers between devices  5.7 us (8%)
  between operations  0.73 us (1%)
    all_to_all x1, blocking collectives, shards(): got = lax.all_to_all(rows, INST + LAB, 0, 0, tiled=True)  44.1 us
    ppermute x3, waiting for transfers between devices, along(): return lax.ppermute(block, INST, pairs)  9.84 us
    pallas_call x2, Pallas kernels, later(): pl.pallas_call(functools.partial(later_kernel, jobs), grid=(1,), out_shap...  3.9 us
    ppermute x2, starting transfers between devices, across(): return lax.ppermute(block, 'c', [(0, 1), (1, 0)])  3.14 us
    ppermute x3, starting transfers between devices, along(): return lax.ppermute(block, INST, pairs)  2.56 us
    pallas_call x1, Pallas kernels, shards(): pl.pallas_call(functools.partial(first_kernel, far_steps), grid=(1,), out...  1.98 us
    pallas_call x1, Pallas kernels, shards(): pl.pallas_call(combine_kernel, grid=(1,), out_shape=jax.ShapeDtypeStruct(...  1.69 us
  transfers between devices with their start and end apart: 5, of which 4 were waited for; matrix products, arithmetic and copies ran while one was open for 0% of the time, Pallas kernels for 6%

profile of v3, /device:TPU:1, one launch (start us, length us, event | category | flops | bytes accessed | tf_op | source)
XLA Modules:
  0.0 70.4 jit_solution(4548069830135090258)
XLA Ops:
  0.6 0.0 copy-start.1
  0.6 0.0 copy-start.2
  0.7 0.0 copy-start
  0.7 2.0 %far_away.1 = (bf16[256,768]{1,0:T(8,128)(2,1)S(1)}, bf16[512,768]{1,0:T(8,128)(2,1)S(1)}) custom-call(s32[8]{0:T(128)} %rows_ref.3, s32[8]{0:T(128)} %labs_ref.3, bf16[8,256,256]{2,1,0:T(8,128)(2,1)} %vals_ref.3, bf16[512,768]{1,0:T(8,128)(2,1)} %feat_hbm.1), custom_call_target="tpu_custom_call" | custom-call | flops 100663296 | bytes 2228224 | tf_op jit(solution)/shard_map/far_away/pallas_call | solution.py:161
  2.6 3.0 %collective-permute-start = (bf16[256,768]{1,0:T(8,128)(2,1)S(1)}, bf16[256,768]{1,0:T(8,128)(2,1)S(1)}, u32[]{:S(2)}, u32[]{:S(2)}) collective-permute-start(bf16[256,768]{1,0:T(8,128)(2,1)S(1)} %get-tuple-element.17), channel_id=1, source_target_pairs={{0,32},{32,0},{1,33},{33,1},{2,34},{34,2},{3,35},{35,3},{4,36},{36... | collective-permute-start | bytes 1179656 | tf_op jit(solution)/shard_map/ppermute | solution.py:189
  5.7 0.0 copy-done.1
  5.7 0.0 copy-done.2
  5.7 0.0 copy-done
  5.7 2.1 %far_own.1 = (bf16[256,768]{1,0:T(8,128)(2,1)S(1)}, bf16[768,768]{1,0:T(8,128)(2,1)S(1)}) custom-call(s32[8]{0:T(128)S(1)} %copy-done.1, s32[8]{0:T(128)S(1)} %copy-done.2, bf16[8,256,256]{2,1,0:T(8,128)(2,1)S(1)} %copy-done, bf16[512,768]{1,0:T(8,128)(2,1)S(1)} %get-tuple-element.18.x_ref), custom_call_target="tpu_custom_call" | custom-call | flops 402653184 | bytes 3407872 | tf_op jit(solution)/shard_map/far_own/pallas_call | solution.py:176
  7.9 0.0 collective-permute-done
  7.9 0.1 add_convert_fusion.1
  8.0 0.1 collective-permute-start.1
  8.1 0.8 %collective-permute-start.3 = (bf16[256,768]{1,0:T(8,128)(2,1)S(1)}, bf16[256,768]{1,0:T(8,128)(2,1)S(1)}, u32[]{:S(2)}, u32[]{:S(2)}) collective-permute-start(bf16[256,768]{1,0:T(8,128)(2,1)S(1)} %add_convert_fusion.1), channel_id=1, source_target_pairs={{0,64},{32,224},{64,128},{96,32},{128,192},{160,96},{192,0},{224,1... | collective-permute-start | bytes 1179656 | tf_op jit(solution)/shard_map/ppermute | solution.py:194
  8.9 1.8 %near_own.1.own_ref = bf16[768,768]{1,0:T(8,128)(2,1)S(1)} custom-call(s32[8]{0:T(128)S(1)} %copy-done.1, s32[8]{0:T(128)S(1)} %copy-done.2, bf16[8,256,256]{2,1,0:T(8,128)(2,1)S(1)} %copy-done, bf16[512,768]{1,0:T(8,128)(2,1)S(1)} %get-tuple-element.18.x_ref), custom_call_target="tpu_custom_call" | custom-call | flops 301989888 | bytes 3014656 | tf_op jit(solution)/shard_map/near_own/pallas_call | solution.py:176
  10.7 0.2 collective-permute-done.1.mate_ref
  10.9 0.1 add_convert_fusion
  11.0 0.0 copy-start.3
  11.0 0.5 collective-permute-start.2
  11.6 4.1 %collective-permute-done.3.far_ref = bf16[256,768]{1,0:T(8,128)(2,1)S(1)} collective-permute-done((bf16[256,768]{1,0:T(8,128)(2,1)S(1)}, bf16[256,768]{1,0:T(8,128)(2,1)S(1)}, u32[]{:S(2)}, u32[]{:S(2)}) %collective-permute-start.3) | collective-permute-done | bytes 393248 | tf_op jit(solution)/shard_map/ppermute | solution.py:194
  15.7 0.1 load.1
  15.8 1.2 %collective-permute-start.4 = (bf16[256,768]{1,0:T(8,128)(2,1)S(1)}, bf16[256,768]{1,0:T(8,128)(2,1)S(1)}, u32[]{:S(2)}, u32[]{:S(2)}) collective-permute-start(bf16[256,768]{1,0:T(8,128)(2,1)S(1)} %load.1), channel_id=1, source_target_pairs={{0,64},{32,224},{64,128},{96,32},{128,192},{160,96},{192,0},{224,1... | collective-permute-start | bytes 1179656 | tf_op jit(solution)/shard_map/ppermute | solution.py:194
  17.0 0.0 copy-done.3
  17.0 0.3 route.1
  17.3 3.8 %collective-permute-done.2 = bf16[256,768]{1,0:T(8,128)(2,1)S(1)} collective-permute-done((bf16[256,768]{1,0:T(8,128)(2,1)S(1)}, bf16[256,768]{1,0:T(8,128)(2,1)S(1)}, u32[]{:S(2)}, u32[]{:S(2)}) %collective-permute-start.2) | collective-permute-done | bytes 393248 | tf_op jit(solution)/shard_map/ppermute | solution.py:194
  21.1 0.2 convert_add_fusion.most_ref
  21.3 1.9 %collective-permute-done.4.came_ref = bf16[256,768]{1,0:T(8,128)(2,1)S(1)} collective-permute-done((bf16[256,768]{1,0:T(8,128)(2,1)S(1)}, bf16[256,768]{1,0:T(8,128)(2,1)S(1)}, u32[]{:S(2)}, u32[]{:S(2)}) %collective-permute-start.4) | collective-permute-done | bytes 393248 | tf_op jit(solution)/shard_map/ppermute | solution.py:194
  23.2 1.4 %pack.1 = (f32[256,768]{1,0:T(8,128)}, bf16[256,7,2,128]{3,2,1,0:T(2,128)(2,1)S(1)}) custom-call(f32[256,768]{1,0:T(8,128)S(1)} %convert_add_fusion.most_ref, bf16[256,768]{1,0:T(8,128)(2,1)S(1)} %collective-permute-done.4.came_ref, bf16[2,256,256]{2,1,0:T(8,128)(2,1)S(1)} %get-tuple-element.22.place_ref, bf16[256,128]{1,0:T(8,128)(2,1)S(1)} %get-tuple-element.23.inside_ref), custom_call_target="tpu_custom_call" | custom-call | tf_op jit(solution)/shard_map/pack/pallas_call | solution.py:232
  24.6 44.1 %all_to_all.5.got_ref = bf16[256,7,2,128]{3,2,1,0:T(2,128)(2,1)S(1)} all-to-all(bf16[256,7,2,128]{3,2,1,0:T(2,128)(2,1)S(1)} %get-tuple-element.25), channel_id=1, replica_groups=mesh['x'=4,'c'=2,'z'=8,'y'=4] {'x','c','z','y'}, dimensions={0} | all-to-all | bytes 1835008 | tf_op jit(solution)/shard_map/all_to_all | solution.py:242
  68.7 1.7 %combine.1 = f32[32,768]{1,0:T(8,128)} custom-call(bf16[256,7,2,128]{3,2,1,0:T(2,128)(2,1)S(1)} %all_to_all.5.got_ref), custom_call_target="tpu_custom_call" | custom-call | tf_op jit(solution)/shard_map/combine/pallas_call | solution.py:243
Async XLA Ops:
  0.6 5.1 %copy-start.1 = (s32[8]{0:T(128)S(1)}, s32[8]{0:T(128)}, u32[]{:S(2)}) copy-start(s32[8]{0:T(128)} %rows_ref.3) | copy-start | bytes 100
  0.6 5.1 %copy-start.2 = (s32[8]{0:T(128)S(1)}, s32[8]{0:T(128)}, u32[]{:S(2)}) copy-start(s32[8]{0:T(128)} %labs_ref.3) | copy-start | bytes 100
  0.7 5.0 %copy-start = (bf16[8,256,256]{2,1,0:T(8,128)(2,1)S(1)}, bf16[8,256,256]{2,1,0:T(8,128)(2,1)}, u32[]{:S(2)}) copy-start(bf16[8,256,256]{2,1,0:T(8,128)(2,1)} %vals_ref.3) | copy-start | bytes 3145732
  2.6 5.2 %collective-permute-start = (bf16[256,768]{1,0:T(8,128)(2,1)S(1)}, bf16[256,768]{1,0:T(8,128)(2,1)S(1)}, u32[]{:S(2)}, u32[]{:S(2)}) collective-permute-start(bf16[256,768]{1,0:T(8,128)(2,1)S(1)} %get-tuple-element.17), channel_id=1, source_target_pairs={{0,32},{32,0},{1,33},{33,1},{2,34},{34,2},{3,35},{35,3},{4,36},{36... | collective-permute-start | bytes 1179656 | tf_op jit(solution)/shard_map/ppermute | solution.py:189
  8.0 2.9 %collective-permute-start.1 = (bf16[768,768]{1,0:T(8,128)(2,1)S(1)}, bf16[768,768]{1,0:T(8,128)(2,1)S(1)}, u32[]{:S(2)}, u32[]{:S(2)}) collective-permute-start(bf16[768,768]{1,0:T(8,128)(2,1)S(1)} %get-tuple-element.19), channel_id=1, source_target_pairs={{0,32},{32,0},{1,33},{33,1},{2,34},{34,2},{3,35},{35,3},{4,36},{36... | collective-permute-start | bytes 3538952 | tf_op jit(solution)/shard_map/ppermute | solution.py:189
  8.1 7.6 %collective-permute-start.3 = (bf16[256,768]{1,0:T(8,128)(2,1)S(1)}, bf16[256,768]{1,0:T(8,128)(2,1)S(1)}, u32[]{:S(2)}, u32[]{:S(2)}) collective-permute-start(bf16[256,768]{1,0:T(8,128)(2,1)S(1)} %add_convert_fusion.1), channel_id=1, source_target_pairs={{0,64},{32,224},{64,128},{96,32},{128,192},{160,96},{192,0},{224,1... | collective-permute-start | bytes 1179656 | tf_op jit(solution)/shard_map/ppermute | solution.py:194
  11.0 6.0 %copy-start.3 = (s32[256]{0:T(256)S(1)}, s32[256]{0:T(256)}, u32[]{:S(2)}) copy-start(s32[256]{0:T(256)} %param.9) | copy-start | bytes 3076
  11.0 10.1 %collective-permute-start.2 = (bf16[256,768]{1,0:T(8,128)(2,1)S(1)}, bf16[256,768]{1,0:T(8,128)(2,1)S(1)}, u32[]{:S(2)}, u32[]{:S(2)}) collective-permute-start(bf16[256,768]{1,0:T(8,128)(2,1)S(1)} %add_convert_fusion), channel_id=1, source_target_pairs={{0,192},{32,96},{64,0},{96,160},{128,64},{160,224},{192,128},{224,... | collective-permute-start | bytes 1179656 | tf_op jit(solution)/shard_map/ppermute | solution.py:194
  15.8 7.4 %collective-permute-start.4 = (bf16[256,768]{1,0:T(8,128)(2,1)S(1)}, bf16[256,768]{1,0:T(8,128)(2,1)S(1)}, u32[]{:S(2)}, u32[]{:S(2)}) collective-permute-start(bf16[256,768]{1,0:T(8,128)(2,1)S(1)} %load.1), channel_id=1, source_target_pairs={{0,64},{32,224},{64,128},{96,32},{128,192},{160,96},{192,0},{224,1... | collective-permute-start | bytes 1179656 | tf_op jit(solution)/shard_map/ppermute | solution.py:194

commit v4 on v3

--- a/solution.py
+++ b/solution.py
@@ -9,6 +9,7 @@
 from jax.sharding import PartitionSpec as P
 
 CL_OWN = 32
+RT = 2
 SLOTS = 2
 LANES = 128
 CORES = 2
@@ -36,7 +37,11 @@
     return [pltpu.make_async_copy(src, dst, sems.at[k]) for k, (src, dst) in enumerate(pairs)]
 
 
-def product(other, steps, rows_ref, labs_ref, vals_ref, x_ref, out_ref, acc_ref):
+def times(values, x):
+    return lax.dot_general(values, x, (((0,), (0,)), ((), ())), preferred_element_type=F32)
+
+
+def product(other, steps, rows_ref, labs_ref, vals_ref, x_ref, out_ref):
     tiles, tile = vals_ref.shape[0], vals_ref.shape[1]
     chips = lax.axis_size("x")
     core = lax.axis_index("c")
@@ -44,26 +49,34 @@
         core = 1 - core
     for k, step in enumerate(steps):
         lab = lax.rem(lax.axis_index("x") + step * (1 - 2 * core) + chips, chips) * CORES + core
-        acc_ref[...] = jnp.zeros_like(acc_ref)
-        for r in range(x_ref.shape[0] // tile):
+        held = []
+        for r in range(RT):
             n = jnp.int32(-1)
             for t in range(tiles):
                 n = jnp.where((rows_ref[t] == r) & (labs_ref[t] == lab), t, n)
-
-            @pl.when(n >= 0)
-            def _(n=n, r=r):
-                acc_ref[...] += lax.dot_general(
-                    vals_ref[n],
-                    x_ref[r * tile : (r + 1) * tile, :],
-                    (((0,), (0,)), ((), ())),
-                    preferred_element_type=F32,
-                )
-
-        out_ref[k * tile : (k + 1) * tile, :] = acc_ref[...].astype(BF)
+            held.append(n)
+        top, low = held
+        count = (top >= 0).astype(jnp.int32) + (low >= 0).astype(jnp.int32)
+        one = jnp.maximum(top, low)
+        where = jnp.where(top >= 0, 0, tile)
+        spot = pl.ds(k * tile, tile)
+
+        @pl.when(count == 0)
+        def _(spot=spot):
+            out_ref[spot, :] = jnp.zeros((tile, out_ref.shape[1]), BF)
+
+        @pl.when(count == 1)
+        def _(spot=spot, one=one, where=where):
+            out_ref[spot, :] = times(vals_ref[one], x_ref[pl.ds(pl.multiple_of(where, tile), tile), :]).astype(BF)
+
+        @pl.when(count == 2)
+        def _(spot=spot, top=top, low=low):
+            both = times(vals_ref[top], x_ref[:tile, :]) + times(vals_ref[low], x_ref[tile:, :])
+            out_ref[spot, :] = both.astype(BF)
 
 
 def first_kernel(
-    steps, rows_hbm, labs_hbm, vals_hbm, feat_hbm, out_ref, x_ref, rows_ref, labs_ref, vals_ref, feat_ref, acc_ref, sems
+    steps, rows_hbm, labs_hbm, vals_hbm, feat_hbm, out_ref, x_ref, rows_ref, labs_ref, vals_ref, feat_ref, sems
 ):
     feat_in = pltpu.make_async_copy(feat_hbm, feat_ref, sems.at[3])
     copies = tiles_in(rows_hbm, labs_hbm, vals_hbm, rows_ref, labs_ref, vals_ref, sems)
@@ -75,27 +88,24 @@
     x_ref[...] = (f * lax.rsqrt(jnp.sum(f * f, axis=-1, keepdims=True) + 1e-06)).astype(BF)
     for copy in copies:
         copy.wait()
-    product(True, steps, rows_ref, labs_ref, vals_ref, x_ref, out_ref, acc_ref)
-
-
-def later_kernel(jobs, rows_ref, labs_ref, vals_ref, x_ref, *refs):
-    out_refs, acc_ref = refs[: len(jobs)], refs[len(jobs)]
+    product(True, steps, rows_ref, labs_ref, vals_ref, x_ref, out_ref)
+
+
+def later_kernel(jobs, rows_ref, labs_ref, vals_ref, x_ref, *out_refs):
     for (other, steps), out_ref in zip(jobs, out_refs):
-        product(other, steps, rows_ref, labs_ref, vals_ref, x_ref, out_ref, acc_ref)
+        product(other, steps, rows_ref, labs_ref, vals_ref, x_ref, out_ref)
 
 
 def route_kernel(ids_ref, place_ref, inside_ref):
-    slots, owners, labs = place_ref.shape
+    rows, labs = place_ref.shape
     ids = ids_ref[...]
     down = lax.broadcasted_iota(jnp.int32, (labs, labs), 0)
     across = lax.broadcasted_iota(jnp.int32, (labs, labs), 1)
     ids_down = jnp.sum(jnp.where(down == across, ids, 0), axis=1, keepdims=True)
     owner = ids // CL_OWN
     earlier = (ids_down // CL_OWN == owner) & (down < across)
-    rank = jnp.sum(earlier.astype(jnp.int32), axis=0, keepdims=True)
-    here = lax.broadcasted_iota(jnp.int32, (owners, labs), 0) == owner
-    for slot in range(slots):
-        place_ref[slot] = jnp.where(here & (rank == slot), 1.0, 0.0).astype(BF)
+    row = owner * SLOTS + jnp.sum(earlier.astype(jnp.int32), axis=0, keepdims=True)
+    place_ref[...] = jnp.where(lax.broadcasted_iota(jnp.int32, (rows, labs), 0) == row, 1.0, 0.0).astype(BF)
     inside_ref[...] = jnp.broadcast_to((ids_down % CL_OWN).astype(F32), inside_ref.shape).astype(BF)
 
 
@@ -103,39 +113,30 @@
     out_ref[...] = (own_ref[...].astype(F32) + mate_ref[...].astype(F32) + far_ref[...].astype(F32)).astype(BF)
 
 
-def pack_kernel(most_ref, came_ref, place_ref, inside_ref, emb_ref, out_ref, stage_ref):
-    width = emb_ref.shape[1]
-    slots, owners = place_ref.shape[:2]
-    cols = width // LANES
-    step = (cols + 1) * slots
+def pack_kernel(most_ref, came_ref, place_ref, inside_ref, emb_hbm, out_ref, emb_ref, sem):
+    owners, cols = out_ref.shape[0], out_ref.shape[1] - 1
     summed = most_ref[...] + came_ref[...].astype(F32)
     unit = summed * lax.rsqrt(jnp.sum(summed * summed, axis=-1, keepdims=True) + 1e-06)
     emb_ref[...] = unit
-    unit = unit.astype(BF)
-    for slot in range(slots):
-        moved = jnp.dot(place_ref[slot], unit, preferred_element_type=F32)
-        for col in range(cols):
-            stage_ref[pl.ds(col * slots + slot, owners, stride=step), :] = moved[:, col * LANES : (col + 1) * LANES]
-        stage_ref[pl.ds(cols * slots + slot, owners, stride=step), :] = jnp.dot(
-            place_ref[slot], inside_ref[...], preferred_element_type=F32
-        )
-    out_ref.reshape(owners * step, LANES)[...] = stage_ref[...].astype(BF)
-
-
-def combine_kernel(got_ref, out_ref, stage_ref):
+    emb_out = pltpu.make_async_copy(emb_ref, emb_hbm, sem)
+    emb_out.start()
+    place = place_ref[...]
+    moved = jnp.dot(place, unit.astype(BF), preferred_element_type=F32).astype(BF)
+    for col in range(cols):
+        out_ref[:, col] = moved[:, col * LANES : (col + 1) * LANES].reshape(owners, SLOTS, LANES)
+    inside = jnp.dot(place, inside_ref[...], preferred_element_type=F32).astype(BF)
+    out_ref[:, cols] = inside.reshape(owners, SLOTS, LANES)
+    emb_out.wait()
+
+
+def combine_kernel(got_ref, out_ref):
     owners, cols = got_ref.shape[0], got_ref.shape[1] - 1
-    step = (cols + 1) * SLOTS
-    stage_ref[...] = got_ref.reshape(owners * step, LANES)[...].astype(F32)
-    lane = lax.broadcasted_iota(jnp.int32, (owners, LANES), 1).astype(F32)
-    total = jnp.zeros((LANES, cols * LANES), F32)
-    for slot in range(SLOTS):
-        inside = stage_ref[pl.ds(cols * SLOTS + slot, owners, stride=step), :]
-        member = jnp.where(inside == lane, 1.0, 0.0).astype(BF)
-        rows = jnp.concatenate(
-            [stage_ref[pl.ds(col * SLOTS + slot, owners, stride=step), :].astype(BF) for col in range(cols)], axis=1
-        )
-        total = total + lax.dot_general(member, rows, (((0,), (0,)), ((), ())), preferred_element_type=F32)
-    sums = total[:CL_OWN]
+    rows = owners * SLOTS
+    inside = got_ref[:, cols].reshape(rows, LANES).astype(F32)
+    lane = lax.broadcasted_iota(jnp.int32, (rows, LANES), 1).astype(F32)
+    member = jnp.where(inside == lane, 1.0, 0.0).astype(BF)
+    data = jnp.concatenate([got_ref[:, col].reshape(rows, LANES) for col in range(cols)], axis=1)
+    sums = lax.dot_general(member, data, (((0,), (0,)), ((), ())), preferred_element_type=F32)[:CL_OWN]
     out_ref[...] = sums * lax.rsqrt(jnp.sum(sums * sums, axis=-1, keepdims=True) + 1e-06)
 
 
@@ -165,7 +166,7 @@
         in_specs=[hbm] * 4,
         out_specs=(full((tile, width)), full((insts, width))),
         scratch_shapes=tile_scratch
-        + [pltpu.VMEM((insts, width), BF), pltpu.VMEM((tile, width), F32), pltpu.SemaphoreType.DMA((4,))],
+        + [pltpu.VMEM((insts, width), BF), pltpu.SemaphoreType.DMA((4,))],
         compiler_params=params(),
         cost_estimate=product_cost(far_steps),
         name="far_away",
@@ -179,7 +180,6 @@
             out_shape=[jax.ShapeDtypeStruct(shape, BF) for shape in shapes],
             in_specs=[smem] * 2 + [full(tile_values.shape), full((insts, width))],
             out_specs=[full(shape) for shape in shapes],
-            scratch_shapes=[pltpu.VMEM((tile, width), F32)],
             compiler_params=params(),
             cost_estimate=product_cost(sum((steps for _, steps in jobs), ())),
             name=name,
@@ -220,22 +220,21 @@
     place, inside = pl.pallas_call(
         route_kernel,
         grid=(1,),
-        out_shape=(jax.ShapeDtypeStruct((SLOTS, owners, labs), BF), jax.ShapeDtypeStruct((labs, LANES), BF)),
+        out_shape=(jax.ShapeDtypeStruct((SLOTS * owners, labs), BF), jax.ShapeDtypeStruct((labs, LANES), BF)),
         in_specs=[full((1, labs))],
-        out_specs=(full((SLOTS, owners, labs)), full((labs, LANES))),
+        out_specs=(full((SLOTS * owners, labs)), full((labs, LANES))),
         compiler_params=params(),
         name="route",
     )(ids.reshape(1, labs))
     block = full((tile, width))
     message = (owners, cols + 1, SLOTS, LANES)
-    stage = pltpu.VMEM((owners * (cols + 1) * SLOTS, LANES), F32)
     label_embed, rows = pl.pallas_call(
         pack_kernel,
         grid=(1,),
         out_shape=(jax.ShapeDtypeStruct((labs, width), F32), jax.ShapeDtypeStruct(message, BF)),
-        in_specs=[block] * 2 + [full((SLOTS, owners, labs)), full((labs, LANES))],
-        out_specs=(full((labs, width)), full(message)),
-        scratch_shapes=[stage],
+        in_specs=[block] * 2 + [full((SLOTS * owners, labs)), full((labs, LANES))],
+        out_specs=(hbm, full(message)),
+        scratch_shapes=[pltpu.VMEM((labs, width), F32), pltpu.SemaphoreType.DMA],
         compiler_params=params(),
         name="pack",
     )(most, came, place, inside)
@@ -246,7 +245,6 @@
         out_shape=jax.ShapeDtypeStruct((CL_OWN, width), F32),
         in_specs=[full(message)],
         out_specs=full((CL_OWN, width)),
-        scratch_shapes=[stage],
         compiler_params=params(),
         name="combine",
     )(got)

time: 70.9 us -> 69.8 us (0.984)
  Pallas kernels: 9.4 us -> 8 us
  transfers between devices with their start and end apart: 5 -> 5, of which waited for: 4 -> 4; matrix products, arithmetic and copies ran while one was open for 0% -> 0% of each run, Pallas kernels for 6% -> 5%
where the time goes in v4:
time: 69.8 us; the launch traced here: 69.7 us
  blocking collectives  44.5 us (64%)
  waiting for transfers between devices  10.1 us (14%)
  Pallas kernels  8 us (11%)
  starting transfers between devices  6 us (9%)
  between operations  0.74 us (1%)
    all_to_all x1, blocking collectives, shards(): got = lax.all_to_all(rows, INST + LAB, 0, 0, tiled=True)  44.5 us
    ppermute x3, waiting for transfers between devices, along(): return lax.ppermute(block, INST, pairs)  9.83 us
    pallas_call x2, Pallas kernels, later(): pl.pallas_call(functools.partial(later_kernel, jobs), grid=(1,), out_shap...  3.28 us
    ppermute x2, starting transfers between devices, across(): return lax.ppermute(block, 'c', [(0, 1), (1, 0)])  3.15 us
    ppermute x3, starting transfers between devices, along(): return lax.ppermute(block, INST, pairs)  2.86 us
    pallas_call x1, Pallas kernels, shards(): pl.pallas_call(functools.partial(first_kernel, far_steps), grid=(1,), out...  1.89 us
  transfers between devices with their start and end apart: 5, of which 4 were waited for; matrix products, arithmetic and copies ran while one was open for 0% of the time, Pallas kernels for 5%

profile of v4, /device:TPU:1, one launch (start us, length us, event | category | flops | bytes accessed | tf_op | source)
XLA Modules:
  0.0 69.7 jit_solution(11411481526193740458)
XLA Ops:
  0.6 0.0 copy-start.1
  0.6 0.0 copy-start.2
  0.7 0.0 copy-start
  0.7 1.9 %far_away.1 = (bf16[256,768]{1,0:T(8,128)(2,1)S(1)}, bf16[512,768]{1,0:T(8,128)(2,1)S(1)}) custom-call(s32[8]{0:T(128)} %rows_ref.3, s32[8]{0:T(128)} %labs_ref.3, bf16[8,256,256]{2,1,0:T(8,128)(2,1)} %vals_ref.3, bf16[512,768]{1,0:T(8,128)(2,1)} %feat_hbm.1), custom_call_target="tpu_custom_call" | custom-call | flops 100663296 | bytes 2228224 | tf_op jit(solution)/shard_map/far_away/pallas_call | solution.py:162
  2.6 3.1 %collective-permute-start = (bf16[256,768]{1,0:T(8,128)(2,1)S(1)}, bf16[256,768]{1,0:T(8,128)(2,1)S(1)}, u32[]{:S(2)}, u32[]{:S(2)}) collective-permute-start(bf16[256,768]{1,0:T(8,128)(2,1)S(1)} %get-tuple-element.17), channel_id=1, source_target_pairs={{0,32},{32,0},{1,33},{33,1},{2,34},{34,2},{3,35},{35,3},{4,36},{36... | collective-permute-start | bytes 1179656 | tf_op jit(solution)/shard_map/ppermute | solution.py:189
  5.6 0.0 copy-done.1
  5.6 0.0 copy-done.2
  5.6 0.0 copy-done
  5.6 1.9 %far_own.1 = (bf16[256,768]{1,0:T(8,128)(2,1)S(1)}, bf16[768,768]{1,0:T(8,128)(2,1)S(1)}) custom-call(s32[8]{0:T(128)S(1)} %copy-done.1, s32[8]{0:T(128)S(1)} %copy-done.2, bf16[8,256,256]{2,1,0:T(8,128)(2,1)S(1)} %copy-done, bf16[512,768]{1,0:T(8,128)(2,1)S(1)} %get-tuple-element.18.x_ref), custom_call_target="tpu_custom_call" | custom-call | flops 402653184 | bytes 3407872 | tf_op jit(solution)/shard_map/far_own/pallas_call | solution.py:177
  7.5 0.0 collective-permute-done
  7.5 0.1 add_convert_fusion.1
  7.7 0.1 collective-permute-start.1
  7.8 1.2 %collective-permute-start.3 = (bf16[256,768]{1,0:T(8,128)(2,1)S(1)}, bf16[256,768]{1,0:T(8,128)(2,1)S(1)}, u32[]{:S(2)}, u32[]{:S(2)}) collective-permute-start(bf16[256,768]{1,0:T(8,128)(2,1)S(1)} %add_convert_fusion.1), channel_id=1, source_target_pairs={{0,64},{32,224},{64,128},{96,32},{128,192},{160,96},{192,0},{224,1... | collective-permute-start | bytes 1179656 | tf_op jit(solution)/shard_map/ppermute | solution.py:194
  8.9 1.4 %near_own.1.own_ref = bf16[768,768]{1,0:T(8,128)(2,1)S(1)} custom-call(s32[8]{0:T(128)S(1)} %copy-done.1, s32[8]{0:T(128)S(1)} %copy-done.2, bf16[8,256,256]{2,1,0:T(8,128)(2,1)S(1)} %copy-done, bf16[512,768]{1,0:T(8,128)(2,1)S(1)} %get-tuple-element.18.x_ref), custom_call_target="tpu_custom_call" | custom-call | flops 301989888 | bytes 3014656 | tf_op jit(solution)/shard_map/near_own/pallas_call | solution.py:177
  10.3 0.3 collective-permute-done.1.mate_ref
  10.6 0.1 add_convert_fusion
  10.7 0.0 copy-start.3
  10.7 0.2 collective-permute-start.2
  10.9 4.5 %collective-permute-done.3.far_ref = bf16[256,768]{1,0:T(8,128)(2,1)S(1)} collective-permute-done((bf16[256,768]{1,0:T(8,128)(2,1)S(1)}, bf16[256,768]{1,0:T(8,128)(2,1)S(1)}, u32[]{:S(2)}, u32[]{:S(2)}) %collective-permute-start.3) | collective-permute-done | bytes 393248 | tf_op jit(solution)/shard_map/ppermute | solution.py:194
  15.4 0.1 load.1
  15.5 1.5 %collective-permute-start.4 = (bf16[256,768]{1,0:T(8,128)(2,1)S(1)}, bf16[256,768]{1,0:T(8,128)(2,1)S(1)}, u32[]{:S(2)}, u32[]{:S(2)}) collective-permute-start(bf16[256,768]{1,0:T(8,128)(2,1)S(1)} %load.1), channel_id=1, source_target_pairs={{0,64},{32,224},{64,128},{96,32},{128,192},{160,96},{192,0},{224,1... | collective-permute-start | bytes 1179656 | tf_op jit(solution)/shard_map/ppermute | solution.py:194
  17.0 0.0 copy-done.3
  17.0 0.3 route.1
  17.4 3.4 %collective-permute-done.2 = bf16[256,768]{1,0:T(8,128)(2,1)S(1)} collective-permute-done((bf16[256,768]{1,0:T(8,128)(2,1)S(1)}, bf16[256,768]{1,0:T(8,128)(2,1)S(1)}, u32[]{:S(2)}, u32[]{:S(2)}) %collective-permute-start.2) | collective-permute-done | bytes 393248 | tf_op jit(solution)/shard_map/ppermute | solution.py:194
  20.8 0.2 convert_add_fusion.most_ref
  20.9 1.9 %collective-permute-done.4.came_ref = bf16[256,768]{1,0:T(8,128)(2,1)S(1)} collective-permute-done((bf16[256,768]{1,0:T(8,128)(2,1)S(1)}, bf16[256,768]{1,0:T(8,128)(2,1)S(1)}, u32[]{:S(2)}, u32[]{:S(2)}) %collective-permute-start.4) | collective-permute-done | bytes 393248 | tf_op jit(solution)/shard_map/ppermute | solution.py:194
  22.9 1.1 %pack.1 = (f32[256,768]{1,0:T(8,128)}, bf16[256,7,2,128]{3,2,1,0:T(2,128)(2,1)S(1)}) custom-call(f32[256,768]{1,0:T(8,128)S(1)} %convert_add_fusion.most_ref, bf16[256,768]{1,0:T(8,128)(2,1)S(1)} %collective-permute-done.4.came_ref, bf16[512,256]{1,0:T(8,128)(2,1)S(1)} %get-tuple-element.22.place_ref, bf16[256,128]{1,0:T(8,128)(2,1)S(1)} %get-tuple-element.23.inside_ref), custom_call_target="tpu_custom_call" | custom-call | tf_op jit(solution)/shard_map/pack/pallas_call | solution.py:231
  24.0 44.5 %all_to_all.5.got_ref = bf16[256,7,2,128]{3,2,1,0:T(2,128)(2,1)S(1)} all-to-all(bf16[256,7,2,128]{3,2,1,0:T(2,128)(2,1)S(1)} %get-tuple-element.25), channel_id=1, replica_groups=mesh['x'=4,'c'=2,'z'=8,'y'=4] {'x','c','z','y'}, dimensions={0} | all-to-all | bytes 1835008 | tf_op jit(solution)/shard_map/all_to_all | solution.py:241
  68.4 1.3 %combine.1 = f32[32,768]{1,0:T(8,128)} custom-call(bf16[256,7,2,128]{3,2,1,0:T(2,128)(2,1)S(1)} %all_to_all.5.got_ref), custom_call_target="tpu_custom_call" | custom-call | tf_op jit(solution)/shard_map/combine/pallas_call | solution.py:242
Async XLA Ops:
  0.6 5.0 %copy-start.1 = (s32[8]{0:T(128)S(1)}, s32[8]{0:T(128)}, u32[]{:S(2)}) copy-start(s32[8]{0:T(128)} %rows_ref.3) | copy-start | bytes 100
  0.6 5.0 %copy-start.2 = (s32[8]{0:T(128)S(1)}, s32[8]{0:T(128)}, u32[]{:S(2)}) copy-start(s32[8]{0:T(128)} %labs_ref.3) | copy-start | bytes 100
  0.7 5.0 %copy-start = (bf16[8,256,256]{2,1,0:T(8,128)(2,1)S(1)}, bf16[8,256,256]{2,1,0:T(8,128)(2,1)}, u32[]{:S(2)}) copy-start(bf16[8,256,256]{2,1,0:T(8,128)(2,1)} %vals_ref.3) | copy-start | bytes 3145732
  2.6 5.0 %collective-permute-start = (bf16[256,768]{1,0:T(8,128)(2,1)S(1)}, bf16[256,768]{1,0:T(8,128)(2,1)S(1)}, u32[]{:S(2)}, u32[]{:S(2)}) collective-permute-start(bf16[256,768]{1,0:T(8,128)(2,1)S(1)} %get-tuple-element.17), channel_id=1, source_target_pairs={{0,32},{32,0},{1,33},{33,1},{2,34},{34,2},{3,35},{35,3},{4,36},{36... | collective-permute-start | bytes 1179656 | tf_op jit(solution)/shard_map/ppermute | solution.py:189
  7.7 2.9 %collective-permute-start.1 = (bf16[768,768]{1,0:T(8,128)(2,1)S(1)}, bf16[768,768]{1,0:T(8,128)(2,1)S(1)}, u32[]{:S(2)}, u32[]{:S(2)}) collective-permute-start(bf16[768,768]{1,0:T(8,128)(2,1)S(1)} %get-tuple-element.19), channel_id=1, source_target_pairs={{0,32},{32,0},{1,33},{33,1},{2,34},{34,2},{3,35},{35,3},{4,36},{36... | collective-permute-start | bytes 3538952 | tf_op jit(solution)/shard_map/ppermute | solution.py:189
  7.8 7.6 %collective-permute-start.3 = (bf16[256,768]{1,0:T(8,128)(2,1)S(1)}, bf16[256,768]{1,0:T(8,128)(2,1)S(1)}, u32[]{:S(2)}, u32[]{:S(2)}) collective-permute-start(bf16[256,768]{1,0:T(8,128)(2,1)S(1)} %add_convert_fusion.1), channel_id=1, source_target_pairs={{0,64},{32,224},{64,128},{96,32},{128,192},{160,96},{192,0},{224,1... | collective-permute-start | bytes 1179656 | tf_op jit(solution)/shard_map/ppermute | solution.py:194
  10.7 6.3 %copy-start.3 = (s32[256]{0:T(256)S(1)}, s32[256]{0:T(256)}, u32[]{:S(2)}) copy-start(s32[256]{0:T(256)} %param.9) | copy-start | bytes 3076
  10.7 10.1 %collective-permute-start.2 = (bf16[256,768]{1,0:T(8,128)(2,1)S(1)}, bf16[256,768]{1,0:T(8,128)(2,1)S(1)}, u32[]{:S(2)}, u32[]{:S(2)}) collective-permute-start(bf16[256,768]{1,0:T(8,128)(2,1)S(1)} %add_convert_fusion), channel_id=1, source_target_pairs={{0,192},{32,96},{64,0},{96,160},{128,64},{160,224},{192,128},{224,... | collective-permute-start | bytes 1179656 | tf_op jit(solution)/shard_map/ppermute | solution.py:194
  15.5 7.4 %collective-permute-start.4 = (bf16[256,768]{1,0:T(8,128)(2,1)S(1)}, bf16[256,768]{1,0:T(8,128)(2,1)S(1)}, u32[]{:S(2)}, u32[]{:S(2)}) collective-permute-start(bf16[256,768]{1,0:T(8,128)(2,1)S(1)} %load.1), channel_id=1, source_target_pairs={{0,64},{32,224},{64,128},{96,32},{128,192},{160,96},{192,0},{224,1... | collective-permute-start | bytes 1179656 | tf_op jit(solution)/shard_map/ppermute | solution.py:194

commit v5 on v4

--- a/solution.py
+++ b/solution.py
@@ -32,68 +32,79 @@
     return pltpu.with_memory_space_constraint(array, pltpu.MemorySpace.HBM)
 
 
-def tiles_in(rows_hbm, labs_hbm, vals_hbm, rows_ref, labs_ref, vals_ref, sems):
-    pairs = ((rows_hbm, rows_ref), (labs_hbm, labs_ref), (vals_hbm, vals_ref))
-    return [pltpu.make_async_copy(src, dst, sems.at[k]) for k, (src, dst) in enumerate(pairs)]
-
-
 def times(values, x):
     return lax.dot_general(values, x, (((0,), (0,)), ((), ())), preferred_element_type=F32)
 
 
-def product(other, steps, rows_ref, labs_ref, vals_ref, x_ref, out_ref):
-    tiles, tile = vals_ref.shape[0], vals_ref.shape[1]
+def tiles_of(other, step, rows_ref, labs_ref):
     chips = lax.axis_size("x")
     core = lax.axis_index("c")
     if other:
         core = 1 - core
-    for k, step in enumerate(steps):
-        lab = lax.rem(lax.axis_index("x") + step * (1 - 2 * core) + chips, chips) * CORES + core
-        held = []
-        for r in range(RT):
-            n = jnp.int32(-1)
-            for t in range(tiles):
-                n = jnp.where((rows_ref[t] == r) & (labs_ref[t] == lab), t, n)
-            held.append(n)
-        top, low = held
-        count = (top >= 0).astype(jnp.int32) + (low >= 0).astype(jnp.int32)
-        one = jnp.maximum(top, low)
-        where = jnp.where(top >= 0, 0, tile)
-        spot = pl.ds(k * tile, tile)
-
-        @pl.when(count == 0)
-        def _(spot=spot):
-            out_ref[spot, :] = jnp.zeros((tile, out_ref.shape[1]), BF)
-
-        @pl.when(count == 1)
-        def _(spot=spot, one=one, where=where):
-            out_ref[spot, :] = times(vals_ref[one], x_ref[pl.ds(pl.multiple_of(where, tile), tile), :]).astype(BF)
-
-        @pl.when(count == 2)
-        def _(spot=spot, top=top, low=low):
-            both = times(vals_ref[top], x_ref[:tile, :]) + times(vals_ref[low], x_ref[tile:, :])
-            out_ref[spot, :] = both.astype(BF)
-
-
-def first_kernel(
-    steps, rows_hbm, labs_hbm, vals_hbm, feat_hbm, out_ref, x_ref, rows_ref, labs_ref, vals_ref, feat_ref, sems
-):
-    feat_in = pltpu.make_async_copy(feat_hbm, feat_ref, sems.at[3])
-    copies = tiles_in(rows_hbm, labs_hbm, vals_hbm, rows_ref, labs_ref, vals_ref, sems)
-    feat_in.start()
-    for copy in copies:
+    lab = lax.rem(lax.axis_index("x") + step * (1 - 2 * core) + chips, chips) * CORES + core
+    held = []
+    for r in range(RT):
+        n = jnp.int32(-1)
+        for t in range(rows_ref.shape[0]):
+            n = jnp.where((rows_ref[t] == r) & (labs_ref[t] == lab), t, n)
+        held.append(n)
+    return held
+
+
+def product(top, low, pick, x_ref, out_ref, spot):
+    tile = x_ref.shape[0] // RT
+
+    @pl.when((top < 0) & (low < 0))
+    def _():
+        out_ref[spot, :] = jnp.zeros((tile, out_ref.shape[1]), BF)
+
+    @pl.when((top >= 0) & (low < 0))
+    def _():
+        out_ref[spot, :] = times(pick(top, 0), x_ref[:tile, :]).astype(BF)
+
+    @pl.when((top < 0) & (low >= 0))
+    def _():
+        out_ref[spot, :] = times(pick(low, 1), x_ref[tile:, :]).astype(BF)
+
+    @pl.when((top >= 0) & (low >= 0))
+    def _():
+        out_ref[spot, :] = (times(pick(top, 0), x_ref[:tile, :]) + times(pick(low, 1), x_ref[tile:, :])).astype(BF)
+
+
+def first_kernel(step, rows_hbm, labs_hbm, vals_hbm, feat_hbm, out_ref, x_ref, rows_ref, labs_ref, two_ref, feat_ref, sems):
+    tile = two_ref.shape[1]
+    halves = [slice(r * tile, (r + 1) * tile) for r in range(RT)]
+    lists = [
+        pltpu.make_async_copy(rows_hbm, rows_ref, sems.at[0]),
+        pltpu.make_async_copy(labs_hbm, labs_ref, sems.at[1]),
+    ]
+    feats = [pltpu.make_async_copy(feat_hbm.at[h], feat_ref.at[h], sems.at[2 + r]) for r, h in enumerate(halves)]
+    for copy in lists + feats:
         copy.start()
-    feat_in.wait()
-    f = feat_ref[...].astype(F32)
-    x_ref[...] = (f * lax.rsqrt(jnp.sum(f * f, axis=-1, keepdims=True) + 1e-06)).astype(BF)
-    for copy in copies:
+    for copy in lists:
         copy.wait()
-    product(True, steps, rows_ref, labs_ref, vals_ref, x_ref, out_ref)
+    held = tiles_of(True, step, rows_ref, labs_ref)
+    tiles = [
+        pltpu.make_async_copy(vals_hbm.at[jnp.maximum(n, 0)], two_ref.at[r], sems.at[2 + RT + r])
+        for r, n in enumerate(held)
+    ]
+    for copy in tiles:
+        copy.start()
+    for copy, h in zip(feats, halves):
+        copy.wait()
+        f = feat_ref[h, :].astype(F32)
+        x_ref[h, :] = (f * lax.rsqrt(jnp.sum(f * f, axis=-1, keepdims=True) + 1e-06)).astype(BF)
+    for copy in tiles:
+        copy.wait()
+    product(*held, lambda n, r: two_ref[r], x_ref, out_ref, slice(0, tile))
 
 
 def later_kernel(jobs, rows_ref, labs_ref, vals_ref, x_ref, *out_refs):
+    tile = vals_ref.shape[1]
     for (other, steps), out_ref in zip(jobs, out_refs):
-        product(other, steps, rows_ref, labs_ref, vals_ref, x_ref, out_ref)
+        for k, step in enumerate(steps):
+            held = tiles_of(other, step, rows_ref, labs_ref)
+            product(*held, lambda n, r: vals_ref[n], x_ref, out_ref, slice(k * tile, (k + 1) * tile))
 
 
 def route_kernel(ids_ref, place_ref, inside_ref):
@@ -113,23 +124,22 @@
     out_ref[...] = (own_ref[...].astype(F32) + mate_ref[...].astype(F32) + far_ref[...].astype(F32)).astype(BF)
 
 
-def pack_kernel(most_ref, came_ref, place_ref, inside_ref, emb_hbm, out_ref, emb_ref, sem):
+def pack_kernel(most_ref, came_ref, place_ref, inside_ref, emb_ref, out_ref):
     owners, cols = out_ref.shape[0], out_ref.shape[1] - 1
     summed = most_ref[...] + came_ref[...].astype(F32)
     unit = summed * lax.rsqrt(jnp.sum(summed * summed, axis=-1, keepdims=True) + 1e-06)
     emb_ref[...] = unit
-    emb_out = pltpu.make_async_copy(emb_ref, emb_hbm, sem)
-    emb_out.start()
     place = place_ref[...]
     moved = jnp.dot(place, unit.astype(BF), preferred_element_type=F32).astype(BF)
     for col in range(cols):
         out_ref[:, col] = moved[:, col * LANES : (col + 1) * LANES].reshape(owners, SLOTS, LANES)
     inside = jnp.dot(place, inside_ref[...], preferred_element_type=F32).astype(BF)
     out_ref[:, cols] = inside.reshape(owners, SLOTS, LANES)
-    emb_out.wait()
-
-
-def combine_kernel(got_ref, out_ref):
+
+
+def combine_kernel(got_ref, emb_ref, out_ref, emb_hbm, sem):
+    emb_out = pltpu.make_async_copy(emb_ref, emb_hbm, sem)
+    emb_out.start()
     owners, cols = got_ref.shape[0], got_ref.shape[1] - 1
     rows = owners * SLOTS
     inside = got_ref[:, cols].reshape(rows, LANES).astype(F32)
@@ -138,6 +148,7 @@
     data = jnp.concatenate([got_ref[:, col].reshape(rows, LANES) for col in range(cols)], axis=1)
     sums = lax.dot_general(member, data, (((0,), (0,)), ((), ())), preferred_element_type=F32)[:CL_OWN]
     out_ref[...] = sums * lax.rsqrt(jnp.sum(sums * sums, axis=-1, keepdims=True) + 1e-06)
+    emb_out.wait()
 
 
 def shards(features, tile_rows, tile_labels, tile_values, cluster_ids):
@@ -149,7 +160,6 @@
     cols = width // LANES
     smem = pl.BlockSpec(memory_space=pltpu.MemorySpace.SMEM)
     hbm = pl.BlockSpec(memory_space=pltpu.MemorySpace.HBM)
-    tile_scratch = [pltpu.SMEM((tiles,), jnp.int32)] * 2 + [pltpu.VMEM(tile_values.shape, BF)]
     far_steps, near_steps = (2,), (0, 1, -1)
 
     def product_cost(steps):
@@ -160,13 +170,18 @@
         )
 
     far_away, normed = pl.pallas_call(
-        functools.partial(first_kernel, far_steps),
+        functools.partial(first_kernel, *far_steps),
         grid=(1,),
         out_shape=(jax.ShapeDtypeStruct((tile, width), BF), jax.ShapeDtypeStruct((insts, width), BF)),
         in_specs=[hbm] * 4,
         out_specs=(full((tile, width)), full((insts, width))),
-        scratch_shapes=tile_scratch
-        + [pltpu.VMEM((insts, width), BF), pltpu.SemaphoreType.DMA((4,))],
+        scratch_shapes=[
+            pltpu.SMEM((tiles,), jnp.int32),
+            pltpu.SMEM((tiles,), jnp.int32),
+            pltpu.VMEM((RT, tile, tile), BF),
+            pltpu.VMEM((insts, width), BF),
+            pltpu.SemaphoreType.DMA((2 + 2 * RT,)),
+        ],
         compiler_params=params(),
         cost_estimate=product_cost(far_steps),
         name="far_away",
@@ -228,26 +243,27 @@
     )(ids.reshape(1, labs))
     block = full((tile, width))
     message = (owners, cols + 1, SLOTS, LANES)
-    label_embed, rows = pl.pallas_call(
+    embed = jax.ShapeDtypeStruct((labs, width), F32)
+    unit, rows = pl.pallas_call(
         pack_kernel,
         grid=(1,),
-        out_shape=(jax.ShapeDtypeStruct((labs, width), F32), jax.ShapeDtypeStruct(message, BF)),
+        out_shape=(embed, jax.ShapeDtypeStruct(message, BF)),
         in_specs=[block] * 2 + [full((SLOTS * owners, labs)), full((labs, LANES))],
-        out_specs=(hbm, full(message)),
-        scratch_shapes=[pltpu.VMEM((labs, width), F32), pltpu.SemaphoreType.DMA],
+        out_specs=(full((labs, width)), full(message)),
         compiler_params=params(),
         name="pack",
     )(most, came, place, inside)
     got = lax.all_to_all(rows, INST + LAB, 0, 0, tiled=True)
-    centroids = pl.pallas_call(
+    centroids, label_embed = pl.pallas_call(
         combine_kernel,
         grid=(1,),
-        out_shape=jax.ShapeDtypeStruct((CL_OWN, width), F32),
-        in_specs=[full(message)],
-        out_specs=full((CL_OWN, width)),
+        out_shape=(jax.ShapeDtypeStruct((CL_OWN, width), F32), embed),
+        in_specs=[full(message), full((labs, width))],
+        out_specs=(full((CL_OWN, width)), hbm),
+        scratch_shapes=[pltpu.SemaphoreType.DMA],
         compiler_params=params(),
         name="combine",
-    )(got)
+    )(got, unit)
     return label_embed, centroids
 
 

time: 69.8 us -> 70.2 us (level)
    pallas_call x3, Pallas kernels: 4.24 us -> 5.05 us  [the longest x1 2.2 us: shards(): pl.pallas_call(functools.partial(first_kernel, *far_steps), grid=(1,), ou...]
where the time goes in v5:
time: 70.2 us; the launch traced here: 69.9 us
  blocking collectives  43.9 us (63%)
  waiting for transfers between devices  10.4 us (15%)
  Pallas kernels  8.66 us (12%)
  starting transfers between devices  5.88 us (8%)
  between operations  0.73 us (1%)
    all_to_all x1, blocking collectives, shards(): got = lax.all_to_all(rows, INST + LAB, 0, 0, tiled=True)  43.9 us
    ppermute x3, waiting for transfers between devices, along(): return lax.ppermute(block, INST, pairs)  10 us
    ppermute x2, starting transfers between devices, across(): return lax.ppermute(block, 'c', [(0, 1), (1, 0)])  3.69 us
    pallas_call x2, Pallas kernels, later(): pl.pallas_call(functools.partial(later_kernel, jobs), grid=(1,), out_shap...  3.11 us
    pallas_call x1, Pallas kernels, shards(): pl.pallas_call(functools.partial(first_kernel, *far_steps), grid=(1,), ou...  2.2 us
    ppermute x3, starting transfers between devices, along(): return lax.ppermute(block, INST, pairs)  2.19 us
    pallas_call x1, Pallas kernels, shards(): pl.pallas_call(combine_kernel, grid=(1,), out_shape=(jax.ShapeDtypeStruct...  1.94 us
  transfers between devices with their start and end apart: 5, of which 4 were waited for; matrix products, arithmetic and copies ran while one was open for 0% of the time, Pallas kernels for 5%

profile of v5, /device:TPU:1, one launch (start us, length us, event | category | flops | bytes accessed | tf_op | source)
XLA Modules:
  0.0 69.9 jit_solution(12197327298654034168)
XLA Ops:
  0.6 0.0 copy-start.1
  0.6 0.0 copy-start.2
  0.7 0.0 copy-start
  0.7 2.2 %far_away.1 = (bf16[256,768]{1,0:T(8,128)(2,1)S(1)}, bf16[512,768]{1,0:T(8,128)(2,1)S(1)}) custom-call(s32[8]{0:T(128)} %rows_ref.3, s32[8]{0:T(128)} %labs_ref.3, bf16[8,256,256]{2,1,0:T(8,128)(2,1)} %vals_ref.3, bf16[512,768]{1,0:T(8,128)(2,1)} %feat_hbm.1), custom_call_target="tpu_custom_call" | custom-call | flops 100663296 | bytes 2228224 | tf_op jit(solution)/shard_map/far_away/pallas_call | solution.py:172
  2.9 3.4 %collective-permute-start = (bf16[256,768]{1,0:T(8,128)(2,1)S(1)}, bf16[256,768]{1,0:T(8,128)(2,1)S(1)}, u32[]{:S(2)}, u32[]{:S(2)}) collective-permute-start(bf16[256,768]{1,0:T(8,128)(2,1)S(1)} %get-tuple-element.19), channel_id=1, source_target_pairs={{0,32},{32,0},{1,33},{33,1},{2,34},{34,2},{3,35},{35,3},{4,36},{36... | collective-permute-start | bytes 1179656 | tf_op jit(solution)/shard_map/ppermute | solution.py:204
  6.2 0.0 copy-done.1
  6.2 0.0 copy-done.2
  6.2 0.0 copy-done
  6.2 1.5 %far_own.1 = (bf16[256,768]{1,0:T(8,128)(2,1)S(1)}, bf16[768,768]{1,0:T(8,128)(2,1)S(1)}) custom-call(s32[8]{0:T(128)S(1)} %copy-done.1, s32[8]{0:T(128)S(1)} %copy-done.2, bf16[8,256,256]{2,1,0:T(8,128)(2,1)S(1)} %copy-done, bf16[512,768]{1,0:T(8,128)(2,1)S(1)} %get-tuple-element.20.x_ref), custom_call_target="tpu_custom_call" | custom-call | flops 402653184 | bytes 3407872 | tf_op jit(solution)/shard_map/far_own/pallas_call | solution.py:192
  7.7 0.0 collective-permute-done
  7.7 0.1 add_convert_fusion.1
  7.8 0.3 collective-permute-start.1
  8.1 0.6 collective-permute-start.3
  8.7 1.7 %near_own.1.own_ref = bf16[768,768]{1,0:T(8,128)(2,1)S(1)} custom-call(s32[8]{0:T(128)S(1)} %copy-done.1, s32[8]{0:T(128)S(1)} %copy-done.2, bf16[8,256,256]{2,1,0:T(8,128)(2,1)S(1)} %copy-done, bf16[512,768]{1,0:T(8,128)(2,1)S(1)} %get-tuple-element.20.x_ref), custom_call_target="tpu_custom_call" | custom-call | flops 301989888 | bytes 3014656 | tf_op jit(solution)/shard_map/near_own/pallas_call | solution.py:192
  10.4 0.4 collective-permute-done.1.mate_ref
  10.8 0.1 add_convert_fusion
  10.9 0.0 copy-start.3
  10.9 0.7 %collective-permute-start.2 = (bf16[256,768]{1,0:T(8,128)(2,1)S(1)}, bf16[256,768]{1,0:T(8,128)(2,1)S(1)}, u32[]{:S(2)}, u32[]{:S(2)}) collective-permute-start(bf16[256,768]{1,0:T(8,128)(2,1)S(1)} %add_convert_fusion), channel_id=1, source_target_pairs={{0,192},{32,96},{64,0},{96,160},{128,64},{160,224},{192,128},{224,... | collective-permute-start | bytes 1179656 | tf_op jit(solution)/shard_map/ppermute | solution.py:209
  11.6 4.1 %collective-permute-done.3.far_ref = bf16[256,768]{1,0:T(8,128)(2,1)S(1)} collective-permute-done((bf16[256,768]{1,0:T(8,128)(2,1)S(1)}, bf16[256,768]{1,0:T(8,128)(2,1)S(1)}, u32[]{:S(2)}, u32[]{:S(2)}) %collective-permute-start.3) | collective-permute-done | bytes 393248 | tf_op jit(solution)/shard_map/ppermute | solution.py:209
  15.7 0.1 load.1
  15.9 0.9 %collective-permute-start.4 = (bf16[256,768]{1,0:T(8,128)(2,1)S(1)}, bf16[256,768]{1,0:T(8,128)(2,1)S(1)}, u32[]{:S(2)}, u32[]{:S(2)}) collective-permute-start(bf16[256,768]{1,0:T(8,128)(2,1)S(1)} %load.1), channel_id=1, source_target_pairs={{0,64},{32,224},{64,128},{96,32},{128,192},{160,96},{192,0},{224,1... | collective-permute-start | bytes 1179656 | tf_op jit(solution)/shard_map/ppermute | solution.py:209
  16.8 0.0 copy-done.3
  16.8 0.3 route.1
  17.1 3.8 %collective-permute-done.2 = bf16[256,768]{1,0:T(8,128)(2,1)S(1)} collective-permute-done((bf16[256,768]{1,0:T(8,128)(2,1)S(1)}, bf16[256,768]{1,0:T(8,128)(2,1)S(1)}, u32[]{:S(2)}, u32[]{:S(2)}) %collective-permute-start.2) | collective-permute-done | bytes 393248 | tf_op jit(solution)/shard_map/ppermute | solution.py:209
  20.9 0.2 convert_add_fusion.most_ref
  21.1 2.1 %collective-permute-done.4.came_ref = bf16[256,768]{1,0:T(8,128)(2,1)S(1)} collective-permute-done((bf16[256,768]{1,0:T(8,128)(2,1)S(1)}, bf16[256,768]{1,0:T(8,128)(2,1)S(1)}, u32[]{:S(2)}, u32[]{:S(2)}) %collective-permute-start.4) | collective-permute-done | bytes 393248 | tf_op jit(solution)/shard_map/ppermute | solution.py:209
  23.2 0.9 %pack.1 = (f32[256,768]{1,0:T(8,128)S(1)}, bf16[256,7,2,128]{3,2,1,0:T(2,128)(2,1)S(1)}) custom-call(f32[256,768]{1,0:T(8,128)S(1)} %convert_add_fusion.most_ref, bf16[256,768]{1,0:T(8,128)(2,1)S(1)} %collective-permute-done.4.came_ref, bf16[512,256]{1,0:T(8,128)(2,1)S(1)} %get-tuple-element.24.place_ref, bf16[256,128]{1,0:T(8,128)(2,1)S(1)} %get-tuple-element.25.inside_ref), custom_call_target="tpu_custom_call" | custom-call | tf_op jit(solution)/shard_map/pack/pallas_call | solution.py:247
  24.1 43.9 %all_to_all.5.got_ref = bf16[256,7,2,128]{3,2,1,0:T(2,128)(2,1)S(1)} all-to-all(bf16[256,7,2,128]{3,2,1,0:T(2,128)(2,1)S(1)} %get-tuple-element.26), channel_id=1, replica_groups=mesh['x'=4,'c'=2,'z'=8,'y'=4] {'x','c','z','y'}, dimensions={0} | all-to-all | bytes 1835008 | tf_op jit(solution)/shard_map/all_to_all | solution.py:256
  68.0 1.9 %combine.1 = (f32[32,768]{1,0:T(8,128)}, f32[256,768]{1,0:T(8,128)}) custom-call(bf16[256,7,2,128]{3,2,1,0:T(2,128)(2,1)S(1)} %all_to_all.5.got_ref, f32[256,768]{1,0:T(8,128)S(1)} %get-tuple-element.27.emb_ref), custom_call_target="tpu_custom_call" | custom-call | tf_op jit(solution)/shard_map/combine/pallas_call | solution.py:257
Async XLA Ops:
  0.6 5.6 %copy-start.1 = (s32[8]{0:T(128)S(1)}, s32[8]{0:T(128)}, u32[]{:S(2)}) copy-start(s32[8]{0:T(128)} %rows_ref.3) | copy-start | bytes 100
  0.6 5.6 %copy-start.2 = (s32[8]{0:T(128)S(1)}, s32[8]{0:T(128)}, u32[]{:S(2)}) copy-start(s32[8]{0:T(128)} %labs_ref.3) | copy-start | bytes 100
  0.7 5.6 %copy-start = (bf16[8,256,256]{2,1,0:T(8,128)(2,1)S(1)}, bf16[8,256,256]{2,1,0:T(8,128)(2,1)}, u32[]{:S(2)}) copy-start(bf16[8,256,256]{2,1,0:T(8,128)(2,1)} %vals_ref.3) | copy-start | bytes 3145732
  2.9 4.8 %collective-permute-start = (bf16[256,768]{1,0:T(8,128)(2,1)S(1)}, bf16[256,768]{1,0:T(8,128)(2,1)S(1)}, u32[]{:S(2)}, u32[]{:S(2)}) collective-permute-start(bf16[256,768]{1,0:T(8,128)(2,1)S(1)} %get-tuple-element.19), channel_id=1, source_target_pairs={{0,32},{32,0},{1,33},{33,1},{2,34},{34,2},{3,35},{35,3},{4,36},{36... | collective-permute-start | bytes 1179656 | tf_op jit(solution)/shard_map/ppermute | solution.py:204
  7.8 2.9 %collective-permute-start.1 = (bf16[768,768]{1,0:T(8,128)(2,1)S(1)}, bf16[768,768]{1,0:T(8,128)(2,1)S(1)}, u32[]{:S(2)}, u32[]{:S(2)}) collective-permute-start(bf16[768,768]{1,0:T(8,128)(2,1)S(1)} %get-tuple-element.21), channel_id=1, source_target_pairs={{0,32},{32,0},{1,33},{33,1},{2,34},{34,2},{3,35},{35,3},{4,36},{36... | collective-permute-start | bytes 3538952 | tf_op jit(solution)/shard_map/ppermute | solution.py:204
  8.1 7.6 %collective-permute-start.3 = (bf16[256,768]{1,0:T(8,128)(2,1)S(1)}, bf16[256,768]{1,0:T(8,128)(2,1)S(1)}, u32[]{:S(2)}, u32[]{:S(2)}) collective-permute-start(bf16[256,768]{1,0:T(8,128)(2,1)S(1)} %add_convert_fusion.1), channel_id=1, source_target_pairs={{0,64},{32,224},{64,128},{96,32},{128,192},{160,96},{192,0},{224,1... | collective-permute-start | bytes 1179656 | tf_op jit(solution)/shard_map/ppermute | solution.py:209
  10.9 5.9 %copy-start.3 = (s32[256]{0:T(256)S(1)}, s32[256]{0:T(256)}, u32[]{:S(2)}) copy-start(s32[256]{0:T(256)} %param.9) | copy-start | bytes 3076
  10.9 10.1 %collective-permute-start.2 = (bf16[256,768]{1,0:T(8,128)(2,1)S(1)}, bf16[256,768]{1,0:T(8,128)(2,1)S(1)}, u32[]{:S(2)}, u32[]{:S(2)}) collective-permute-start(bf16[256,768]{1,0:T(8,128)(2,1)S(1)} %add_convert_fusion), channel_id=1, source_target_pairs={{0,192},{32,96},{64,0},{96,160},{128,64},{160,224},{192,128},{224,... | collective-permute-start | bytes 1179656 | tf_op jit(solution)/shard_map/ppermute | solution.py:209
  15.9 7.3 %collective-permute-start.4 = (bf16[256,768]{1,0:T(8,128)(2,1)S(1)}, bf16[256,768]{1,0:T(8,128)(2,1)S(1)}, u32[]{:S(2)}, u32[]{:S(2)}) collective-permute-start(bf16[256,768]{1,0:T(8,128)(2,1)S(1)} %load.1), channel_id=1, source_target_pairs={{0,64},{32,224},{64,128},{96,32},{128,192},{160,96},{192,0},{224,1... | collective-permute-start | bytes 1179656 | tf_op jit(solution)/shard_map/ppermute | solution.py:209

commit v6 on v4

--- a/solution.py
+++ b/solution.py
@@ -96,7 +96,7 @@
         product(other, steps, rows_ref, labs_ref, vals_ref, x_ref, out_ref)
 
 
-def route_kernel(ids_ref, place_ref, inside_ref):
+def route_kernel(n_lab, ids_ref, place_ref, inside_ref):
     rows, labs = place_ref.shape
     ids = ids_ref[...]
     down = lax.broadcasted_iota(jnp.int32, (labs, labs), 0)
@@ -104,7 +104,10 @@
     ids_down = jnp.sum(jnp.where(down == across, ids, 0), axis=1, keepdims=True)
     owner = ids // CL_OWN
     earlier = (ids_down // CL_OWN == owner) & (down < across)
-    row = owner * SLOTS + jnp.sum(earlier.astype(jnp.int32), axis=0, keepdims=True)
+    rank = jnp.sum(earlier.astype(jnp.int32), axis=0, keepdims=True)
+    core = owner // n_lab % CORES
+    chip = owner // (n_lab * CORES) * n_lab + owner % n_lab
+    row = core * (rows // CORES) + chip * SLOTS + rank
     place_ref[...] = jnp.where(lax.broadcasted_iota(jnp.int32, (rows, labs), 0) == row, 1.0, 0.0).astype(BF)
     inside_ref[...] = jnp.broadcast_to((ids_down % CL_OWN).astype(F32), inside_ref.shape).astype(BF)
 
@@ -114,7 +117,8 @@
 
 
 def pack_kernel(most_ref, came_ref, place_ref, inside_ref, emb_hbm, out_ref, emb_ref, sem):
-    owners, cols = out_ref.shape[0], out_ref.shape[1] - 1
+    chips, cols = out_ref.shape[0], out_ref.shape[1] // CORES
+    rows = chips * SLOTS
     summed = most_ref[...] + came_ref[...].astype(F32)
     unit = summed * lax.rsqrt(jnp.sum(summed * summed, axis=-1, keepdims=True) + 1e-06)
     emb_ref[...] = unit
@@ -122,21 +126,38 @@
     emb_out.start()
     place = place_ref[...]
     moved = jnp.dot(place, unit.astype(BF), preferred_element_type=F32).astype(BF)
-    for col in range(cols):
-        out_ref[:, col] = moved[:, col * LANES : (col + 1) * LANES].reshape(owners, SLOTS, LANES)
-    inside = jnp.dot(place, inside_ref[...], preferred_element_type=F32).astype(BF)
-    out_ref[:, cols] = inside.reshape(owners, SLOTS, LANES)
+    for core in range(CORES):
+        for col in range(cols):
+            block = moved[core * rows : (core + 1) * rows, col * LANES : (col + 1) * LANES]
+            out_ref[:, core * cols + col] = block.reshape(chips, SLOTS, LANES)
+    inside = jnp.dot(place, inside_ref[...], preferred_element_type=F32)
+    lane = lax.broadcasted_iota(jnp.int32, (rows, LANES), 1)
+    beside = jnp.where(lane < LANES // CORES, inside[:rows], inside[rows:])
+    out_ref[:, CORES * cols] = beside.astype(BF).reshape(chips, SLOTS, LANES)
     emb_out.wait()
 
 
-def combine_kernel(got_ref, out_ref):
-    owners, cols = got_ref.shape[0], got_ref.shape[1] - 1
-    rows = owners * SLOTS
-    inside = got_ref[:, cols].reshape(rows, LANES).astype(F32)
-    lane = lax.broadcasted_iota(jnp.int32, (rows, LANES), 1).astype(F32)
+def combine_kernel(got_ref, mine_ref, other_ref):
+    chips, cols = got_ref.shape[0], got_ref.shape[1] // CORES
+    rows = chips * SLOTS
+    part = LANES // CORES
+    inside = got_ref[:, CORES * cols].reshape(rows, LANES).astype(F32)
+    lane = lax.rem(lax.broadcasted_iota(jnp.int32, (rows, LANES), 1), part).astype(F32)
     member = jnp.where(inside == lane, 1.0, 0.0).astype(BF)
-    data = jnp.concatenate([got_ref[:, col].reshape(rows, LANES) for col in range(cols)], axis=1)
-    sums = lax.dot_general(member, data, (((0,), (0,)), ((), ())), preferred_element_type=F32)[:CL_OWN]
+    sums = []
+    for core in range(CORES):
+        data = [got_ref[:, core * cols + col].reshape(rows, LANES) for col in range(cols)]
+        both = lax.dot_general(
+            member, jnp.concatenate(data, axis=1), (((0,), (0,)), ((), ())), preferred_element_type=F32
+        )
+        sums.append(both[core * part : core * part + CL_OWN])
+    first = lax.axis_index("c") == 0
+    mine_ref[...] = jnp.where(first, sums[0], sums[1])
+    other_ref[...] = jnp.where(first, sums[1], sums[0])
+
+
+def finish_kernel(mine_ref, mate_ref, out_ref):
+    sums = mine_ref[...] + mate_ref[...]
     out_ref[...] = sums * lax.rsqrt(jnp.sum(sums * sums, axis=-1, keepdims=True) + 1e-06)
 
 
@@ -218,7 +239,7 @@
     came = along(loaded, 1)
     most = pair(0) + free_came.astype(F32)
     place, inside = pl.pallas_call(
-        route_kernel,
+        functools.partial(route_kernel, lax.axis_size(LAB)),
         grid=(1,),
         out_shape=(jax.ShapeDtypeStruct((SLOTS * owners, labs), BF), jax.ShapeDtypeStruct((labs, LANES), BF)),
         in_specs=[full((1, labs))],
@@ -227,7 +248,7 @@
         name="route",
     )(ids.reshape(1, labs))
     block = full((tile, width))
-    message = (owners, cols + 1, SLOTS, LANES)
+    message = (owners // CORES, CORES * cols + 1, SLOTS, LANES)
     label_embed, rows = pl.pallas_call(
         pack_kernel,
         grid=(1,),
@@ -238,16 +259,26 @@
         compiler_params=params(),
         name="pack",
     )(most, came, place, inside)
-    got = lax.all_to_all(rows, INST + LAB, 0, 0, tiled=True)
-    centroids = pl.pallas_call(
+    got = lax.all_to_all(rows, ("x",) + LAB, 0, 0, tiled=True)
+    sums = jax.ShapeDtypeStruct((CL_OWN, width), F32)
+    mine, other = pl.pallas_call(
         combine_kernel,
         grid=(1,),
-        out_shape=jax.ShapeDtypeStruct((CL_OWN, width), F32),
+        out_shape=(sums, sums),
         in_specs=[full(message)],
-        out_specs=full((CL_OWN, width)),
+        out_specs=(full(sums.shape), full(sums.shape)),
         compiler_params=params(),
         name="combine",
     )(got)
+    centroids = pl.pallas_call(
+        finish_kernel,
+        grid=(1,),
+        out_shape=sums,
+        in_specs=[full(sums.shape)] * 2,
+        out_specs=full(sums.shape),
+        compiler_params=params(),
+        name="finish",
+    )(mine, across(other))
     return label_embed, centroids
 
 

time: 69.8 us -> 68.6 us (0.983)
  blocking collectives: 44.5 us -> 37.1 us
  starting transfers between devices: 6 us -> 11.4 us
  waiting for transfers between devices: 10.1 us -> 11 us
    all_to_all x1, blocking collectives: 44.5 us -> 37.1 us  [shards(): got = lax.all_to_all(rows, ('x',) + LAB, 0, 0, tiled=True)]
    ppermute x2 -> x3, starting transfers between devices: 3.15 us -> 8.87 us  [across(): return lax.ppermute(block, 'c', [(0, 1), (1, 0)])]
    ppermute x2 -> x3, waiting for transfers between devices: 0.27 us -> 1.11 us  [across(): return lax.ppermute(block, 'c', [(0, 1), (1, 0)])]
    pallas_call x2 -> x3, Pallas kernels: 1.61 us -> 1.6 us  [the longest x1 0.74 us: shards(): pl.pallas_call(finish_kernel, grid=(1,), out_shape=sums, in_specs=[full(s...]
  transfers between devices with their start and end apart: 5 -> 6, of which waited for: 4 -> 5; matrix products, arithmetic and copies ran while one was open for 0% -> 0% of each run, Pallas kernels for 5% -> 5%
where the time goes in v6:
time: 68.6 us; the launch traced here: 68.4 us
  blocking collectives  37.1 us (54%)
  starting transfers between devices  11.4 us (17%)
  waiting for transfers between devices  11 us (16%)
  Pallas kernels  7.81 us (11%)
  between operations  0.74 us (1%)
    all_to_all x1, blocking collectives, shards(): got = lax.all_to_all(rows, ('x',) + LAB, 0, 0, tiled=True)  37.1 us
    ppermute x3, waiting for transfers between devices, along(): return lax.ppermute(block, INST, pairs)  9.89 us
    ppermute x3, starting transfers between devices, across(): return lax.ppermute(block, 'c', [(0, 1), (1, 0)])  8.87 us
    pallas_call x2, Pallas kernels, later(): pl.pallas_call(functools.partial(later_kernel, jobs), grid=(1,), out_shap...  3.09 us
    ppermute x3, starting transfers between devices, along(): return lax.ppermute(block, INST, pairs)  2.55 us
    pallas_call x1, Pallas kernels, shards(): pl.pallas_call(functools.partial(first_kernel, far_steps), grid=(1,), out...  1.89 us
  transfers between devices with their start and end apart: 6, of which 5 were waited for; matrix products, arithmetic and copies ran while one was open for 0% of the time, Pallas kernels for 5%

profile of v6, /device:TPU:1, one launch (start us, length us, event | category | flops | bytes accessed | tf_op | source)
XLA Modules:
  0.0 68.4 jit_solution(15948252290474714175)
XLA Ops:
  0.6 0.0 copy-start.1
  0.6 0.0 copy-start.2
  0.7 0.0 copy-start
  0.7 1.9 %far_away.1 = (bf16[256,768]{1,0:T(8,128)(2,1)S(1)}, bf16[512,768]{1,0:T(8,128)(2,1)S(1)}) custom-call(s32[8]{0:T(128)} %rows_ref.3, s32[8]{0:T(128)} %labs_ref.3, bf16[8,256,256]{2,1,0:T(8,128)(2,1)} %vals_ref.3, bf16[512,768]{1,0:T(8,128)(2,1)} %feat_hbm.1), custom_call_target="tpu_custom_call" | custom-call | flops 100663296 | bytes 2228224 | tf_op jit(solution)/shard_map/far_away/pallas_call | solution.py:183
  2.6 3.3 %collective-permute-start = (bf16[256,768]{1,0:T(8,128)(2,1)S(1)}, bf16[256,768]{1,0:T(8,128)(2,1)S(1)}, u32[]{:S(2)}, u32[]{:S(2)}) collective-permute-start(bf16[256,768]{1,0:T(8,128)(2,1)S(1)} %get-tuple-element.19), channel_id=1, source_target_pairs={{0,32},{32,0},{1,33},{33,1},{2,34},{34,2},{3,35},{35,3},{4,36},{36... | collective-permute-start | bytes 1179656 | tf_op jit(solution)/shard_map/ppermute | solution.py:210
  5.9 0.0 copy-done.1
  5.9 0.0 copy-done.2
  5.9 0.0 copy-done
  5.9 1.4 %far_own.1 = (bf16[256,768]{1,0:T(8,128)(2,1)S(1)}, bf16[768,768]{1,0:T(8,128)(2,1)S(1)}) custom-call(s32[8]{0:T(128)S(1)} %copy-done.1, s32[8]{0:T(128)S(1)} %copy-done.2, bf16[8,256,256]{2,1,0:T(8,128)(2,1)S(1)} %copy-done, bf16[512,768]{1,0:T(8,128)(2,1)S(1)} %get-tuple-element.20.x_ref), custom_call_target="tpu_custom_call" | custom-call | flops 402653184 | bytes 3407872 | tf_op jit(solution)/shard_map/far_own/pallas_call | solution.py:198
  7.3 0.0 collective-permute-done
  7.4 0.1 add_convert_fusion.1
  7.5 0.4 collective-permute-start.1
  7.9 0.7 %collective-permute-start.3 = (bf16[256,768]{1,0:T(8,128)(2,1)S(1)}, bf16[256,768]{1,0:T(8,128)(2,1)S(1)}, u32[]{:S(2)}, u32[]{:S(2)}) collective-permute-start(bf16[256,768]{1,0:T(8,128)(2,1)S(1)} %add_convert_fusion.1), channel_id=1, source_target_pairs={{0,64},{32,224},{64,128},{96,32},{128,192},{160,96},{192,0},{224,1... | collective-permute-start | bytes 1179656 | tf_op jit(solution)/shard_map/ppermute | solution.py:215
  8.6 1.7 %near_own.1.own_ref = bf16[768,768]{1,0:T(8,128)(2,1)S(1)} custom-call(s32[8]{0:T(128)S(1)} %copy-done.1, s32[8]{0:T(128)S(1)} %copy-done.2, bf16[8,256,256]{2,1,0:T(8,128)(2,1)S(1)} %copy-done, bf16[512,768]{1,0:T(8,128)(2,1)S(1)} %get-tuple-element.20.x_ref), custom_call_target="tpu_custom_call" | custom-call | flops 301989888 | bytes 3014656 | tf_op jit(solution)/shard_map/near_own/pallas_call | solution.py:198
  10.2 0.2 collective-permute-done.1.mate_ref
  10.4 0.1 add_convert_fusion
  10.5 0.0 copy-start.3
  10.5 0.8 %collective-permute-start.2 = (bf16[256,768]{1,0:T(8,128)(2,1)S(1)}, bf16[256,768]{1,0:T(8,128)(2,1)S(1)}, u32[]{:S(2)}, u32[]{:S(2)}) collective-permute-start(bf16[256,768]{1,0:T(8,128)(2,1)S(1)} %add_convert_fusion), channel_id=1, source_target_pairs={{0,192},{32,96},{64,0},{96,160},{128,64},{160,224},{192,128},{224,... | collective-permute-start | bytes 1179656 | tf_op jit(solution)/shard_map/ppermute | solution.py:215
  11.3 4.2 %collective-permute-done.3.far_ref = bf16[256,768]{1,0:T(8,128)(2,1)S(1)} collective-permute-done((bf16[256,768]{1,0:T(8,128)(2,1)S(1)}, bf16[256,768]{1,0:T(8,128)(2,1)S(1)}, u32[]{:S(2)}, u32[]{:S(2)}) %collective-permute-start.3) | collective-permute-done | bytes 393248 | tf_op jit(solution)/shard_map/ppermute | solution.py:215
  15.4 0.1 load.1
  15.6 1.1 %collective-permute-start.4 = (bf16[256,768]{1,0:T(8,128)(2,1)S(1)}, bf16[256,768]{1,0:T(8,128)(2,1)S(1)}, u32[]{:S(2)}, u32[]{:S(2)}) collective-permute-start(bf16[256,768]{1,0:T(8,128)(2,1)S(1)} %load.1), channel_id=1, source_target_pairs={{0,64},{32,224},{64,128},{96,32},{128,192},{160,96},{192,0},{224,1... | collective-permute-start | bytes 1179656 | tf_op jit(solution)/shard_map/ppermute | solution.py:215
  16.6 0.0 copy-done.3
  16.6 0.4 route.1
  17.0 3.6 %collective-permute-done.2 = bf16[256,768]{1,0:T(8,128)(2,1)S(1)} collective-permute-done((bf16[256,768]{1,0:T(8,128)(2,1)S(1)}, bf16[256,768]{1,0:T(8,128)(2,1)S(1)}, u32[]{:S(2)}, u32[]{:S(2)}) %collective-permute-start.2) | collective-permute-done | bytes 393248 | tf_op jit(solution)/shard_map/ppermute | solution.py:215
  20.6 0.2 convert_add_fusion.most_ref
  20.8 2.2 %collective-permute-done.4.came_ref = bf16[256,768]{1,0:T(8,128)(2,1)S(1)} collective-permute-done((bf16[256,768]{1,0:T(8,128)(2,1)S(1)}, bf16[256,768]{1,0:T(8,128)(2,1)S(1)}, u32[]{:S(2)}, u32[]{:S(2)}) %collective-permute-start.4) | collective-permute-done | bytes 393248 | tf_op jit(solution)/shard_map/ppermute | solution.py:215
  22.9 1.1 %pack.1 = (f32[256,768]{1,0:T(8,128)}, bf16[128,13,2,128]{3,2,1,0:T(2,128)(2,1)S(1)}) custom-call(f32[256,768]{1,0:T(8,128)S(1)} %convert_add_fusion.most_ref, bf16[256,768]{1,0:T(8,128)(2,1)S(1)} %collective-permute-done.4.came_ref, bf16[512,256]{1,0:T(8,128)(2,1)S(1)} %get-tuple-element.24.place_ref, bf16[256,128]{1,0:T(8,128)(2,1)S(1)} %get-tuple-element.25.inside_ref), custom_call_target="tpu_custom_call" | custom-call | tf_op jit(solution)/shard_map/pack/pallas_call | solution.py:252
  24.0 37.1 %all_to_all.5.got_ref = bf16[128,13,2,128]{3,2,1,0:T(2,128)(2,1)S(1)} all-to-all(bf16[128,13,2,128]{3,2,1,0:T(2,128)(2,1)S(1)} %get-tuple-element.27), channel_id=1, replica_groups=mesh['x'=4,'c'=2,'z'=8,'y'=4] {'x','z','y'}, dimensions={0} | all-to-all | bytes 1703936 | tf_op jit(solution)/shard_map/all_to_all | solution.py:262
  61.1 0.5 combine.1
  61.6 5.1 %collective-permute-start.5 = (f32[32,768]{1,0:T(8,128)S(1)}, f32[32,768]{1,0:T(8,128)S(1)}, u32[]{:S(2)}, u32[]{:S(2)}) collective-permute-start(f32[32,768]{1,0:T(8,128)S(1)} %get-tuple-element.29), channel_id=1, source_target_pairs={{0,32},{32,0},{1,33},{33,1},{2,34},{34,2},{3,35},{35,3},{4,36},{36... | collective-permute-start | bytes 294920 | tf_op jit(solution)/shard_map/ppermute | solution.py:210
  66.8 0.9 %collective-permute-done.5.mate_ref = f32[32,768]{1,0:T(8,128)S(1)} collective-permute-done((f32[32,768]{1,0:T(8,128)S(1)}, f32[32,768]{1,0:T(8,128)S(1)}, u32[]{:S(2)}, u32[]{:S(2)}) %collective-permute-start.5) | collective-permute-done | bytes 98336 | tf_op jit(solution)/shard_map/ppermute | solution.py:210
  67.7 0.7 %finish.1 = f32[32,768]{1,0:T(8,128)} custom-call(f32[32,768]{1,0:T(8,128)S(1)} %get-tuple-element.28.mine_ref, f32[32,768]{1,0:T(8,128)S(1)} %collective-permute-done.5.mate_ref), custom_call_target="tpu_custom_call" | custom-call | tf_op jit(solution)/shard_map/finish/pallas_call | solution.py:273
Async XLA Ops:
  0.6 5.3 %copy-start.1 = (s32[8]{0:T(128)S(1)}, s32[8]{0:T(128)}, u32[]{:S(2)}) copy-start(s32[8]{0:T(128)} %rows_ref.3) | copy-start | bytes 100
  0.6 5.3 %copy-start.2 = (s32[8]{0:T(128)S(1)}, s32[8]{0:T(128)}, u32[]{:S(2)}) copy-start(s32[8]{0:T(128)} %labs_ref.3) | copy-start | bytes 100
  0.7 5.2 %copy-start = (bf16[8,256,256]{2,1,0:T(8,128)(2,1)S(1)}, bf16[8,256,256]{2,1,0:T(8,128)(2,1)}, u32[]{:S(2)}) copy-start(bf16[8,256,256]{2,1,0:T(8,128)(2,1)} %vals_ref.3) | copy-start | bytes 3145732
  2.6 4.8 %collective-permute-start = (bf16[256,768]{1,0:T(8,128)(2,1)S(1)}, bf16[256,768]{1,0:T(8,128)(2,1)S(1)}, u32[]{:S(2)}, u32[]{:S(2)}) collective-permute-start(bf16[256,768]{1,0:T(8,128)(2,1)S(1)} %get-tuple-element.19), channel_id=1, source_target_pairs={{0,32},{32,0},{1,33},{33,1},{2,34},{34,2},{3,35},{35,3},{4,36},{36... | collective-permute-start | bytes 1179656 | tf_op jit(solution)/shard_map/ppermute | solution.py:210
  7.5 2.9 %collective-permute-start.1 = (bf16[768,768]{1,0:T(8,128)(2,1)S(1)}, bf16[768,768]{1,0:T(8,128)(2,1)S(1)}, u32[]{:S(2)}, u32[]{:S(2)}) collective-permute-start(bf16[768,768]{1,0:T(8,128)(2,1)S(1)} %get-tuple-element.21), channel_id=1, source_target_pairs={{0,32},{32,0},{1,33},{33,1},{2,34},{34,2},{3,35},{35,3},{4,36},{36... | collective-permute-start | bytes 3538952 | tf_op jit(solution)/shard_map/ppermute | solution.py:210
  7.9 7.6 %collective-permute-start.3 = (bf16[256,768]{1,0:T(8,128)(2,1)S(1)}, bf16[256,768]{1,0:T(8,128)(2,1)S(1)}, u32[]{:S(2)}, u32[]{:S(2)}) collective-permute-start(bf16[256,768]{1,0:T(8,128)(2,1)S(1)} %add_convert_fusion.1), channel_id=1, source_target_pairs={{0,64},{32,224},{64,128},{96,32},{128,192},{160,96},{192,0},{224,1... | collective-permute-start | bytes 1179656 | tf_op jit(solution)/shard_map/ppermute | solution.py:215
  10.5 6.1 %copy-start.3 = (s32[256]{0:T(256)S(1)}, s32[256]{0:T(256)}, u32[]{:S(2)}) copy-start(s32[256]{0:T(256)} %param.9) | copy-start | bytes 3076
  10.5 10.1 %collective-permute-start.2 = (bf16[256,768]{1,0:T(8,128)(2,1)S(1)}, bf16[256,768]{1,0:T(8,128)(2,1)S(1)}, u32[]{:S(2)}, u32[]{:S(2)}) collective-permute-start(bf16[256,768]{1,0:T(8,128)(2,1)S(1)} %add_convert_fusion), channel_id=1, source_target_pairs={{0,192},{32,96},{64,0},{96,160},{128,64},{160,224},{192,128},{224,... | collective-permute-start | bytes 1179656 | tf_op jit(solution)/shard_map/ppermute | solution.py:215
  15.6 7.3 %collective-permute-start.4 = (bf16[256,768]{1,0:T(8,128)(2,1)S(1)}, bf16[256,768]{1,0:T(8,128)(2,1)S(1)}, u32[]{:S(2)}, u32[]{:S(2)}) collective-permute-start(bf16[256,768]{1,0:T(8,128)(2,1)S(1)} %load.1), channel_id=1, source_target_pairs={{0,64},{32,224},{64,128},{96,32},{128,192},{160,96},{192,0},{224,1... | collective-permute-start | bytes 1179656 | tf_op jit(solution)/shard_map/ppermute | solution.py:215
  61.6 6.1 %collective-permute-start.5 = (f32[32,768]{1,0:T(8,128)S(1)}, f32[32,768]{1,0:T(8,128)S(1)}, u32[]{:S(2)}, u32[]{:S(2)}) collective-permute-start(f32[32,768]{1,0:T(8,128)S(1)} %get-tuple-element.29), channel_id=1, source_target_pairs={{0,32},{32,0},{1,33},{33,1},{2,34},{34,2},{3,35},{35,3},{4,36},{36... | collective-permute-start | bytes 294920 | tf_op jit(solution)/shard_map/ppermute | solution.py:210

commit v7 on v4

--- a/solution.py
+++ b/solution.py
@@ -96,15 +96,20 @@
         product(other, steps, rows_ref, labs_ref, vals_ref, x_ref, out_ref)
 
 
-def route_kernel(ids_ref, place_ref, inside_ref):
+def route_kernel(n_lab, ids_ref, place_ref, inside_ref):
     rows, labs = place_ref.shape
+    chips = lax.axis_size("x")
     ids = ids_ref[...]
     down = lax.broadcasted_iota(jnp.int32, (labs, labs), 0)
     across = lax.broadcasted_iota(jnp.int32, (labs, labs), 1)
     ids_down = jnp.sum(jnp.where(down == across, ids, 0), axis=1, keepdims=True)
     owner = ids // CL_OWN
     earlier = (ids_down // CL_OWN == owner) & (down < across)
-    row = owner * SLOTS + jnp.sum(earlier.astype(jnp.int32), axis=0, keepdims=True)
+    rank = jnp.sum(earlier.astype(jnp.int32), axis=0, keepdims=True)
+    inst = owner // n_lab
+    core = (inst + lax.axis_index("c")) % CORES
+    chip = (inst // CORES + chips - lax.axis_index("x")) % chips
+    row = ((core * chips + chip) * n_lab + owner % n_lab) * SLOTS + rank
     place_ref[...] = jnp.where(lax.broadcasted_iota(jnp.int32, (rows, labs), 0) == row, 1.0, 0.0).astype(BF)
     inside_ref[...] = jnp.broadcast_to((ids_down % CL_OWN).astype(F32), inside_ref.shape).astype(BF)
 
@@ -114,7 +119,10 @@
 
 
 def pack_kernel(most_ref, came_ref, place_ref, inside_ref, emb_hbm, out_ref, emb_ref, sem):
-    owners, cols = out_ref.shape[0], out_ref.shape[1] - 1
+    dests, width = out_ref.shape[0], emb_ref.shape[1]
+    cols = width // LANES
+    owners = out_ref.shape[1] // cols
+    rows = dests * SLOTS
     summed = most_ref[...] + came_ref[...].astype(F32)
     unit = summed * lax.rsqrt(jnp.sum(summed * summed, axis=-1, keepdims=True) + 1e-06)
     emb_ref[...] = unit
@@ -122,21 +130,40 @@
     emb_out.start()
     place = place_ref[...]
     moved = jnp.dot(place, unit.astype(BF), preferred_element_type=F32).astype(BF)
-    for col in range(cols):
-        out_ref[:, col] = moved[:, col * LANES : (col + 1) * LANES].reshape(owners, SLOTS, LANES)
-    inside = jnp.dot(place, inside_ref[...], preferred_element_type=F32).astype(BF)
-    out_ref[:, cols] = inside.reshape(owners, SLOTS, LANES)
+    inside = jnp.dot(place, inside_ref[...], preferred_element_type=F32)
+    spot = lax.broadcasted_iota(jnp.int32, (rows, LANES), 1) // (LANES // owners)
+    beside = jnp.zeros((rows, LANES), F32)
+    for q in range(owners):
+        mine = slice(q * rows, (q + 1) * rows)
+        for col in range(cols):
+            block = moved[mine, col * LANES : (col + 1) * LANES]
+            out_ref[:, q * cols + col] = block.reshape(dests, SLOTS, LANES)
+        beside = jnp.where(spot == q, inside[mine], beside)
+    out_ref[:, owners * cols] = beside.astype(BF).reshape(dests, SLOTS, LANES)
     emb_out.wait()
 
 
-def combine_kernel(got_ref, out_ref):
-    owners, cols = got_ref.shape[0], got_ref.shape[1] - 1
-    rows = owners * SLOTS
-    inside = got_ref[:, cols].reshape(rows, LANES).astype(F32)
+def combine_kernel(got_ref, keep_ref, away_ref):
+    sources, width = got_ref.shape[0], keep_ref.shape[1]
+    cols = width // LANES
+    owners = got_ref.shape[1] // cols
+    rows = sources * SLOTS
+    inside = got_ref[:, owners * cols].reshape(rows, LANES).astype(F32)
     lane = lax.broadcasted_iota(jnp.int32, (rows, LANES), 1).astype(F32)
-    member = jnp.where(inside == lane, 1.0, 0.0).astype(BF)
-    data = jnp.concatenate([got_ref[:, col].reshape(rows, LANES) for col in range(cols)], axis=1)
-    sums = lax.dot_general(member, data, (((0,), (0,)), ((), ())), preferred_element_type=F32)[:CL_OWN]
+    for q in range(owners):
+        at = q * (LANES // owners)
+        member = jnp.where(inside[:, at : at + 1] == lane, 1.0, 0.0).astype(BF)
+        data = jnp.concatenate([got_ref[:, q * cols + col].reshape(rows, LANES) for col in range(cols)], axis=1)
+        sums = lax.dot_general(member, data, (((0,), (0,)), ((), ())), preferred_element_type=F32)[:CL_OWN]
+        core, k = divmod(q, owners // CORES)
+        if core == 0:
+            keep_ref[k * CL_OWN : (k + 1) * CL_OWN, :] = sums
+        else:
+            away_ref[k * CL_OWN : (k + 1) * CL_OWN, :] = sums.astype(BF)
+
+
+def finish_kernel(own_ref, a_ref, b_ref, c_ref, out_ref):
+    sums = own_ref[...] + a_ref[...].astype(F32) + b_ref[...].astype(F32) + c_ref[...].astype(F32)
     out_ref[...] = sums * lax.rsqrt(jnp.sum(sums * sums, axis=-1, keepdims=True) + 1e-06)
 
 
@@ -218,7 +245,7 @@
     came = along(loaded, 1)
     most = pair(0) + free_came.astype(F32)
     place, inside = pl.pallas_call(
-        route_kernel,
+        functools.partial(route_kernel, lax.axis_size(LAB)),
         grid=(1,),
         out_shape=(jax.ShapeDtypeStruct((SLOTS * owners, labs), BF), jax.ShapeDtypeStruct((labs, LANES), BF)),
         in_specs=[full((1, labs))],
@@ -227,7 +254,7 @@
         name="route",
     )(ids.reshape(1, labs))
     block = full((tile, width))
-    message = (owners, cols + 1, SLOTS, LANES)
+    message = (lax.axis_size(LAB), lax.axis_size(INST) * cols + 1, SLOTS, LANES)
     label_embed, rows = pl.pallas_call(
         pack_kernel,
         grid=(1,),
@@ -238,16 +265,37 @@
         compiler_params=params(),
         name="pack",
     )(most, came, place, inside)
-    got = lax.all_to_all(rows, INST + LAB, 0, 0, tiled=True)
-    centroids = pl.pallas_call(
+    got = lax.all_to_all(rows, LAB, 0, 0, tiled=True)
+    held = (chips * CL_OWN, width)
+    keep, away = pl.pallas_call(
         combine_kernel,
         grid=(1,),
-        out_shape=jax.ShapeDtypeStruct((CL_OWN, width), F32),
+        out_shape=(jax.ShapeDtypeStruct(held, F32), jax.ShapeDtypeStruct(held, BF)),
         in_specs=[full(message)],
-        out_specs=full((CL_OWN, width)),
+        out_specs=(full(held), full(held)),
         compiler_params=params(),
         name="combine",
     )(got)
+    mate_sums = across(away)
+
+    def cluster_sums(step):
+        part = slice(step * CL_OWN, (step + 1) * CL_OWN)
+        return keep[part] + mate_sums[part].astype(F32)
+
+    sums_came = [
+        lax.ppermute(cluster_sums(step).astype(BF), "x", [(i, (i + step) % chips) for i in range(chips)])
+        for step in (2, 1, 3)
+    ]
+    block = full((CL_OWN, width))
+    centroids = pl.pallas_call(
+        finish_kernel,
+        grid=(1,),
+        out_shape=jax.ShapeDtypeStruct((CL_OWN, width), F32),
+        in_specs=[block] * 4,
+        out_specs=block,
+        compiler_params=params(),
+        name="finish",
+    )(cluster_sums(0), *sums_came)
     return label_embed, centroids
 
 

time: 69.8 us -> 69 us (0.989); the launches traced: 69.7 us -> 68 us
  blocking collectives: 44.5 us -> 29.1 us
  starting transfers between devices: 6 us -> 15.9 us
  waiting for transfers between devices: 10.1 us -> 13.5 us
    all_to_all x1, blocking collectives: 44.5 us -> 29.1 us  [shards(): got = lax.all_to_all(rows, LAB, 0, 0, tiled=True)]
    ppermute x2 -> x3, starting transfers between devices: 3.15 us -> 9.11 us  [across(): return lax.ppermute(block, 'c', [(0, 1), (1, 0)])]
    ppermute x0 -> x3, starting transfers between devices: none -> 4.78 us  [shards(): lax.ppermute(cluster_sums(step).astype(BF), 'x', [(i, (i + step) % chips)...]
    ppermute x2 -> x3, waiting for transfers between devices: 0.27 us -> 1.79 us  [across(): return lax.ppermute(block, 'c', [(0, 1), (1, 0)])]
    ppermute x0 -> x3, waiting for transfers between devices: none -> 1.48 us  [shards(): lax.ppermute(cluster_sums(step).astype(BF), 'x', [(i, (i + step) % chips)...]
    ppermute x3, starting transfers between devices: 2.86 us -> 2.04 us  [along(): return lax.ppermute(block, INST, pairs)]
    pallas_call x2 -> x3, Pallas kernels: 1.61 us -> 2.04 us  [the longest x1 0.93 us: shards(): pl.pallas_call(combine_kernel, grid=(1,), out_shape=(jax.ShapeDtypeStruct...]
  transfers between devices with their start and end apart: 5 -> 9, of which waited for: 4 -> 6; matrix products, arithmetic and copies ran while one was open for 0% -> 0% of each run, Pallas kernels for 5% -> 5%
where the time goes in v7:
time: 69 us; the launch traced here: 68 us
  blocking collectives  29.1 us (42%)
  starting transfers between devices  15.9 us (23%)
  waiting for transfers between devices  13.5 us (20%)
  Pallas kernels  8.24 us (12%)
  between operations  0.76 us (1%)
    all_to_all x1, blocking collectives, shards(): got = lax.all_to_all(rows, LAB, 0, 0, tiled=True)  29.1 us
    ppermute x3, waiting for transfers between devices, along(): return lax.ppermute(block, INST, pairs)  10.3 us
    ppermute x3, starting transfers between devices, across(): return lax.ppermute(block, 'c', [(0, 1), (1, 0)])  9.11 us
    ppermute x3, starting transfers between devices, shards(): lax.ppermute(cluster_sums(step).astype(BF), 'x', [(i, (i + step) % chips)...  4.78 us
    pallas_call x2, Pallas kernels, later(): pl.pallas_call(functools.partial(later_kernel, jobs), grid=(1,), out_shap...  3.09 us
    ppermute x3, starting transfers between devices, along(): return lax.ppermute(block, INST, pairs)  2.04 us
    pallas_call x1, Pallas kernels, shards(): pl.pallas_call(functools.partial(first_kernel, far_steps), grid=(1,), out...  1.89 us
    ppermute x3, waiting for transfers between devices, across(): return lax.ppermute(block, 'c', [(0, 1), (1, 0)])  1.79 us
  transfers between devices with their start and end apart: 9, of which 6 were waited for; matrix products, arithmetic and copies ran while one was open for 0% of the time, Pallas kernels for 5%

profile of v7, /device:TPU:1, one launch (start us, length us, event | category | flops | bytes accessed | tf_op | source)
XLA Modules:
  0.0 68.0 jit_solution(3494080665013339887)
XLA Ops:
  0.7 1.9 %far_away.1 = (bf16[256,768]{1,0:T(8,128)(2,1)S(1)}, bf16[512,768]{1,0:T(8,128)(2,1)S(1)}) custom-call(s32[8]{0:T(128)} %rows_ref.3, s32[8]{0:T(128)} %labs_ref.3, bf16[8,256,256]{2,1,0:T(8,128)(2,1)} %vals_ref.3, bf16[512,768]{1,0:T(8,128)(2,1)} %feat_hbm.1), custom_call_target="tpu_custom_call" | custom-call | flops 100663296 | bytes 2228224 | tf_op jit(solution)/shard_map/far_away/pallas_call | solution.py:189
  2.6 3.3 %collective-permute-start = (bf16[256,768]{1,0:T(8,128)(2,1)S(1)}, bf16[256,768]{1,0:T(8,128)(2,1)S(1)}, u32[]{:S(2)}, u32[]{:S(2)}) collective-permute-start(bf16[256,768]{1,0:T(8,128)(2,1)S(1)} %get-tuple-element.19), channel_id=1, source_target_pairs={{0,32},{32,0},{1,33},{33,1},{2,34},{34,2},{3,35},{35,3},{4,36},{36... | collective-permute-start | bytes 1179656 | tf_op jit(solution)/shard_map/ppermute | solution.py:216
  5.9 0.0 copy-done.2
  5.9 1.8 %far_own.1 = (bf16[256,768]{1,0:T(8,128)(2,1)S(1)}, bf16[768,768]{1,0:T(8,128)(2,1)S(1)}) custom-call(s32[8]{0:T(128)S(1)} %copy-done.1, s32[8]{0:T(128)S(1)} %copy-done.2, bf16[8,256,256]{2,1,0:T(8,128)(2,1)S(1)} %copy-done, bf16[512,768]{1,0:T(8,128)(2,1)S(1)} %get-tuple-element.20.x_ref), custom_call_target="tpu_custom_call" | custom-call | flops 402653184 | bytes 3407872 | tf_op jit(solution)/shard_map/far_own/pallas_call | solution.py:204
  7.7 0.0 collective-permute-done
  7.7 0.1 add_convert_fusion.1
  7.8 0.1 collective-permute-start.1
  7.9 0.8 %collective-permute-start.3 = (bf16[256,768]{1,0:T(8,128)(2,1)S(1)}, bf16[256,768]{1,0:T(8,128)(2,1)S(1)}, u32[]{:S(2)}, u32[]{:S(2)}) collective-permute-start(bf16[256,768]{1,0:T(8,128)(2,1)S(1)} %add_convert_fusion.1), channel_id=1, source_target_pairs={{0,64},{32,224},{64,128},{96,32},{128,192},{160,96},{192,0},{224,1... | collective-permute-start | bytes 1179656 | tf_op jit(solution)/shard_map/ppermute | solution.py:221
  8.8 1.3 %near_own.1.own_ref = bf16[768,768]{1,0:T(8,128)(2,1)S(1)} custom-call(s32[8]{0:T(128)S(1)} %copy-done.1, s32[8]{0:T(128)S(1)} %copy-done.2, bf16[8,256,256]{2,1,0:T(8,128)(2,1)S(1)} %copy-done, bf16[512,768]{1,0:T(8,128)(2,1)S(1)} %get-tuple-element.20.x_ref), custom_call_target="tpu_custom_call" | custom-call | flops 301989888 | bytes 3014656 | tf_op jit(solution)/shard_map/near_own/pallas_call | solution.py:204
  10.0 0.7 %collective-permute-done.1.mate_ref = bf16[768,768]{1,0:T(8,128)(2,1)S(1)} collective-permute-done((bf16[768,768]{1,0:T(8,128)(2,1)S(1)}, bf16[768,768]{1,0:T(8,128)(2,1)S(1)}, u32[]{:S(2)}, u32[]{:S(2)}) %collective-permute-start.1) | collective-permute-done | bytes 1179680 | tf_op jit(solution)/shard_map/ppermute | solution.py:216
  10.8 0.1 add_convert_fusion
  10.9 0.0 copy-start.3
  10.9 0.1 collective-permute-start.2
  11.0 4.6 %collective-permute-done.3.far_ref = bf16[256,768]{1,0:T(8,128)(2,1)S(1)} collective-permute-done((bf16[256,768]{1,0:T(8,128)(2,1)S(1)}, bf16[256,768]{1,0:T(8,128)(2,1)S(1)}, u32[]{:S(2)}, u32[]{:S(2)}) %collective-permute-start.3) | collective-permute-done | bytes 393248 | tf_op jit(solution)/shard_map/ppermute | solution.py:221
  15.5 0.1 load.1
  15.7 1.1 %collective-permute-start.4 = (bf16[256,768]{1,0:T(8,128)(2,1)S(1)}, bf16[256,768]{1,0:T(8,128)(2,1)S(1)}, u32[]{:S(2)}, u32[]{:S(2)}) collective-permute-start(bf16[256,768]{1,0:T(8,128)(2,1)S(1)} %load.1), channel_id=1, source_target_pairs={{0,64},{32,224},{64,128},{96,32},{128,192},{160,96},{192,0},{224,1... | collective-permute-start | bytes 1179656 | tf_op jit(solution)/shard_map/ppermute | solution.py:221
  16.8 0.4 route.1
  17.2 3.8 %collective-permute-done.2 = bf16[256,768]{1,0:T(8,128)(2,1)S(1)} collective-permute-done((bf16[256,768]{1,0:T(8,128)(2,1)S(1)}, bf16[256,768]{1,0:T(8,128)(2,1)S(1)}, u32[]{:S(2)}, u32[]{:S(2)}) %collective-permute-start.2) | collective-permute-done | bytes 393248 | tf_op jit(solution)/shard_map/ppermute | solution.py:221
  20.9 0.2 convert_add_fusion.most_ref
  21.1 1.9 %collective-permute-done.4.came_ref = bf16[256,768]{1,0:T(8,128)(2,1)S(1)} collective-permute-done((bf16[256,768]{1,0:T(8,128)(2,1)S(1)}, bf16[256,768]{1,0:T(8,128)(2,1)S(1)}, u32[]{:S(2)}, u32[]{:S(2)}) %collective-permute-start.4) | collective-permute-done | bytes 393248 | tf_op jit(solution)/shard_map/ppermute | solution.py:221
  23.1 1.1 %pack.1 = (f32[256,768]{1,0:T(8,128)}, bf16[32,49,2,128]{3,2,1,0:T(2,128)(2,1)S(1)}) custom-call(f32[256,768]{1,0:T(8,128)S(1)} %convert_add_fusion.most_ref, bf16[256,768]{1,0:T(8,128)(2,1)S(1)} %collective-permute-done.4.came_ref, bf16[512,256]{1,0:T(8,128)(2,1)S(1)} %get-tuple-element.24.place_ref, bf16[256,128]{1,0:T(8,128)(2,1)S(1)} %get-tuple-element.25.inside_ref), custom_call_target="tpu_custom_call" | custom-call | tf_op jit(solution)/shard_map/pack/pallas_call | solution.py:258
  24.1 29.1 %all_to_all.5.got_ref = bf16[32,49,2,128]{3,2,1,0:T(2,128)(2,1)S(1)} all-to-all(bf16[32,49,2,128]{3,2,1,0:T(2,128)(2,1)S(1)} %get-tuple-element.27), channel_id=1, replica_groups=mesh['x'=4,'c'=2,'z'=8,'y'=4] {'z','y'}, dimensions={0} | all-to-all | bytes 1605632 | tf_op jit(solution)/shard_map/all_to_all | solution.py:268
  53.3 0.9 %combine.1 = (f32[128,768]{1,0:T(8,128)S(1)}, bf16[128,768]{1,0:T(8,128)(2,1)S(1)}) custom-call(bf16[32,49,2,128]{3,2,1,0:T(2,128)(2,1)S(1)} %all_to_all.5.got_ref), custom_call_target="tpu_custom_call" | custom-call | tf_op jit(solution)/shard_map/combine/pallas_call | solution.py:270
  54.2 5.7 %collective-permute-start.5 = (bf16[128,768]{1,0:T(8,128)(2,1)S(1)}, bf16[128,768]{1,0:T(8,128)(2,1)S(1)}, u32[]{:S(2)}, u32[]{:S(2)}) collective-permute-start(bf16[128,768]{1,0:T(8,128)(2,1)S(1)} %get-tuple-element.29), channel_id=1, source_target_pairs={{0,32},{32,0},{1,33},{33,1},{2,34},{34,2},{3,35},{35,3},{4,36},{36... | collective-permute-start | bytes 589832 | tf_op jit(solution)/shard_map/ppermute | solution.py:216
  59.9 1.1 %collective-permute-done.5 = bf16[128,768]{1,0:T(8,128)(2,1)S(1)} collective-permute-done((bf16[128,768]{1,0:T(8,128)(2,1)S(1)}, bf16[128,768]{1,0:T(8,128)(2,1)S(1)}, u32[]{:S(2)}, u32[]{:S(2)}) %collective-permute-start.5) | collective-permute-done | bytes 196640 | tf_op jit(solution)/shard_map/ppermute | solution.py:216
  61.0 2.1 %collective-permute-start.6 = (bf16[32,768]{1,0:T(8,128)(2,1)S(1)}, bf16[32,768]{1,0:T(8,128)(2,1)S(1)}, u32[]{:S(2)}, u32[]{:S(2)}) collective-permute-start(bf16[32,768]{1,0:T(8,128)(2,1)S(1)} %get-tuple-element.32), channel_id=1, source_target_pairs={{0,128},{64,192},{128,0},{192,64},{1,129},{65,193},{129,1},{193,65... | collective-permute-start | bytes 147464 | tf_op jit(solution)/shard_map/ppermute | solution.py:286
  63.1 1.2 %collective-permute-start.7 = (bf16[32,768]{1,0:T(8,128)(2,1)S(1)}, bf16[32,768]{1,0:T(8,128)(2,1)S(1)}, u32[]{:S(2)}, u32[]{:S(2)}) collective-permute-start(bf16[32,768]{1,0:T(8,128)(2,1)S(1)} %get-tuple-element.31), channel_id=1, source_target_pairs={{0,64},{64,128},{128,192},{192,0},{1,65},{65,129},{129,193},{193,1... | collective-permute-start | bytes 147464 | tf_op jit(solution)/shard_map/ppermute | solution.py:286
  64.3 1.5 %collective-permute-start.8 = (bf16[32,768]{1,0:T(8,128)(2,1)S(1)}, bf16[32,768]{1,0:T(8,128)(2,1)S(1)}, u32[]{:S(2)}, u32[]{:S(2)}) collective-permute-start(bf16[32,768]{1,0:T(8,128)(2,1)S(1)} %get-tuple-element.30), channel_id=1, source_target_pairs={{0,192},{64,0},{128,64},{192,128},{1,193},{65,1},{129,65},{193,129... | collective-permute-start | bytes 147464 | tf_op jit(solution)/shard_map/ppermute | solution.py:286
  65.8 0.0 collective-permute-done.6.a_ref
  65.8 1.5 %collective-permute-done.7.b_ref = bf16[32,768]{1,0:T(8,128)(2,1)S(1)} collective-permute-done((bf16[32,768]{1,0:T(8,128)(2,1)S(1)}, bf16[32,768]{1,0:T(8,128)(2,1)S(1)}, u32[]{:S(2)}, u32[]{:S(2)}) %collective-permute-start.7) | collective-permute-done | bytes 49184 | tf_op jit(solution)/shard_map/ppermute | solution.py:286
  67.2 0.0 collective-permute-done.8.c_ref
  67.3 0.8 %finish.1 = f32[32,768]{1,0:T(8,128)} custom-call(f32[32,768]{1,0:T(8,128)S(1)} %get-tuple-element.33.own_ref, bf16[32,768]{1,0:T(8,128)(2,1)S(1)} %collective-permute-done.6.a_ref, bf16[32,768]{1,0:T(8,128)(2,1)S(1)} %collective-permute-done.7.b_ref, bf16[32,768]{1,0:T(8,128)(2,1)S(1)} %collective-permute-done.8.c_ref), custom_call_target="tpu_custom_call" | custom-call | tf_op jit(solution)/shard_map/finish/pallas_call | solution.py:290
  (7 shorter events, 0.0 us)
Async XLA Ops:
  0.6 5.3 %copy-start.1 = (s32[8]{0:T(128)S(1)}, s32[8]{0:T(128)}, u32[]{:S(2)}) copy-start(s32[8]{0:T(128)} %rows_ref.3) | copy-start | bytes 100
  0.6 5.3 %copy-start.2 = (s32[8]{0:T(128)S(1)}, s32[8]{0:T(128)}, u32[]{:S(2)}) copy-start(s32[8]{0:T(128)} %labs_ref.3) | copy-start | bytes 100
  0.7 5.2 %copy-start = (bf16[8,256,256]{2,1,0:T(8,128)(2,1)S(1)}, bf16[8,256,256]{2,1,0:T(8,128)(2,1)}, u32[]{:S(2)}) copy-start(bf16[8,256,256]{2,1,0:T(8,128)(2,1)} %vals_ref.3) | copy-start | bytes 3145732
  2.6 5.2 %collective-permute-start = (bf16[256,768]{1,0:T(8,128)(2,1)S(1)}, bf16[256,768]{1,0:T(8,128)(2,1)S(1)}, u32[]{:S(2)}, u32[]{:S(2)}) collective-permute-start(bf16[256,768]{1,0:T(8,128)(2,1)S(1)} %get-tuple-element.19), channel_id=1, source_target_pairs={{0,32},{32,0},{1,33},{33,1},{2,34},{34,2},{3,35},{35,3},{4,36},{36... | collective-permute-start | bytes 1179656 | tf_op jit(solution)/shard_map/ppermute | solution.py:216
  7.8 2.9 %collective-permute-start.1 = (bf16[768,768]{1,0:T(8,128)(2,1)S(1)}, bf16[768,768]{1,0:T(8,128)(2,1)S(1)}, u32[]{:S(2)}, u32[]{:S(2)}) collective-permute-start(bf16[768,768]{1,0:T(8,128)(2,1)S(1)} %get-tuple-element.21), channel_id=1, source_target_pairs={{0,32},{32,0},{1,33},{33,1},{2,34},{34,2},{3,35},{35,3},{4,36},{36... | collective-permute-start | bytes 3538952 | tf_op jit(solution)/shard_map/ppermute | solution.py:216
  7.9 7.6 %collective-permute-start.3 = (bf16[256,768]{1,0:T(8,128)(2,1)S(1)}, bf16[256,768]{1,0:T(8,128)(2,1)S(1)}, u32[]{:S(2)}, u32[]{:S(2)}) collective-permute-start(bf16[256,768]{1,0:T(8,128)(2,1)S(1)} %add_convert_fusion.1), channel_id=1, source_target_pairs={{0,64},{32,224},{64,128},{96,32},{128,192},{160,96},{192,0},{224,1... | collective-permute-start | bytes 1179656 | tf_op jit(solution)/shard_map/ppermute | solution.py:221
  10.9 6.0 %copy-start.3 = (s32[256]{0:T(256)S(1)}, s32[256]{0:T(256)}, u32[]{:S(2)}) copy-start(s32[256]{0:T(256)} %param.9) | copy-start | bytes 3076
  10.9 10.1 %collective-permute-start.2 = (bf16[256,768]{1,0:T(8,128)(2,1)S(1)}, bf16[256,768]{1,0:T(8,128)(2,1)S(1)}, u32[]{:S(2)}, u32[]{:S(2)}) collective-permute-start(bf16[256,768]{1,0:T(8,128)(2,1)S(1)} %add_convert_fusion), channel_id=1, source_target_pairs={{0,192},{32,96},{64,0},{96,160},{128,64},{160,224},{192,128},{224,... | collective-permute-start | bytes 1179656 | tf_op jit(solution)/shard_map/ppermute | solution.py:221
  15.7 7.4 %collective-permute-start.4 = (bf16[256,768]{1,0:T(8,128)(2,1)S(1)}, bf16[256,768]{1,0:T(8,128)(2,1)S(1)}, u32[]{:S(2)}, u32[]{:S(2)}) collective-permute-start(bf16[256,768]{1,0:T(8,128)(2,1)S(1)} %load.1), channel_id=1, source_target_pairs={{0,64},{32,224},{64,128},{96,32},{128,192},{160,96},{192,0},{224,1... | collective-permute-start | bytes 1179656 | tf_op jit(solution)/shard_map/ppermute | solution.py:221
  54.2 6.8 %collective-permute-start.5 = (bf16[128,768]{1,0:T(8,128)(2,1)S(1)}, bf16[128,768]{1,0:T(8,128)(2,1)S(1)}, u32[]{:S(2)}, u32[]{:S(2)}) collective-permute-start(bf16[128,768]{1,0:T(8,128)(2,1)S(1)} %get-tuple-element.29), channel_id=1, source_target_pairs={{0,32},{32,0},{1,33},{33,1},{2,34},{34,2},{3,35},{35,3},{4,36},{36... | collective-permute-start | bytes 589832 | tf_op jit(solution)/shard_map/ppermute | solution.py:216
  61.0 4.8 %collective-permute-start.6 = (bf16[32,768]{1,0:T(8,128)(2,1)S(1)}, bf16[32,768]{1,0:T(8,128)(2,1)S(1)}, u32[]{:S(2)}, u32[]{:S(2)}) collective-permute-start(bf16[32,768]{1,0:T(8,128)(2,1)S(1)} %get-tuple-element.32), channel_id=1, source_target_pairs={{0,128},{64,192},{128,0},{192,64},{1,129},{65,193},{129,1},{193,65... | collective-permute-start | bytes 147464 | tf_op jit(solution)/shard_map/ppermute | solution.py:286
  63.1 4.2 %collective-permute-start.7 = (bf16[32,768]{1,0:T(8,128)(2,1)S(1)}, bf16[32,768]{1,0:T(8,128)(2,1)S(1)}, u32[]{:S(2)}, u32[]{:S(2)}) collective-permute-start(bf16[32,768]{1,0:T(8,128)(2,1)S(1)} %get-tuple-element.31), channel_id=1, source_target_pairs={{0,64},{64,128},{128,192},{192,0},{1,65},{65,129},{129,193},{193,1... | collective-permute-start | bytes 147464 | tf_op jit(solution)/shard_map/ppermute | solution.py:286
  64.3 3.0 %collective-permute-start.8 = (bf16[32,768]{1,0:T(8,128)(2,1)S(1)}, bf16[32,768]{1,0:T(8,128)(2,1)S(1)}, u32[]{:S(2)}, u32[]{:S(2)}) collective-permute-start(bf16[32,768]{1,0:T(8,128)(2,1)S(1)} %get-tuple-element.30), channel_id=1, source_target_pairs={{0,192},{64,0},{128,64},{192,128},{1,193},{65,1},{129,65},{193,129... | collective-permute-start | bytes 147464 | tf_op jit(solution)/shard_map/ppermute | solution.py:286

commit v8 on v7

--- a/solution.py
+++ b/solution.py
@@ -108,7 +108,7 @@
     rank = jnp.sum(earlier.astype(jnp.int32), axis=0, keepdims=True)
     inst = owner // n_lab
     core = (inst + lax.axis_index("c")) % CORES
-    chip = (inst // CORES + chips - lax.axis_index("x")) % chips
+    chip = inst // CORES ^ lax.axis_index("x")
     row = ((core * chips + chip) * n_lab + owner % n_lab) * SLOTS + rank
     place_ref[...] = jnp.where(lax.broadcasted_iota(jnp.int32, (rows, labs), 0) == row, 1.0, 0.0).astype(BF)
     inside_ref[...] = jnp.broadcast_to((ids_down % CL_OWN).astype(F32), inside_ref.shape).astype(BF)
@@ -162,8 +162,8 @@
             away_ref[k * CL_OWN : (k + 1) * CL_OWN, :] = sums.astype(BF)
 
 
-def finish_kernel(own_ref, a_ref, b_ref, c_ref, out_ref):
-    sums = own_ref[...] + a_ref[...].astype(F32) + b_ref[...].astype(F32) + c_ref[...].astype(F32)
+def finish_kernel(own_ref, came_ref, out_ref):
+    sums = own_ref[...] + came_ref[...].astype(F32)
     out_ref[...] = sums * lax.rsqrt(jnp.sum(sums * sums, axis=-1, keepdims=True) + 1e-06)
 
 
@@ -278,24 +278,25 @@
     )(got)
     mate_sums = across(away)
 
-    def cluster_sums(step):
-        part = slice(step * CL_OWN, (step + 1) * CL_OWN)
-        return keep[part] + mate_sums[part].astype(F32)
-
-    sums_came = [
-        lax.ppermute(cluster_sums(step).astype(BF), "x", [(i, (i + step) % chips) for i in range(chips)])
-        for step in (2, 1, 3)
-    ]
+    sums = keep + mate_sums.astype(F32)
+    left = chips
+    while left > 1:
+        left //= 2
+        cut = left * CL_OWN
+        came = lax.ppermute(sums[cut:].astype(BF), "x", [(i, i ^ left) for i in range(chips)])
+        sums = sums[:cut]
+        if left > 1:
+            sums = sums + came.astype(F32)
     block = full((CL_OWN, width))
     centroids = pl.pallas_call(
         finish_kernel,
         grid=(1,),
         out_shape=jax.ShapeDtypeStruct((CL_OWN, width), F32),
-        in_specs=[block] * 4,
+        in_specs=[block] * 2,
         out_specs=block,
         compiler_params=params(),
         name="finish",
-    )(cluster_sums(0), *sums_came)
+    )(sums, came)
     return label_embed, centroids
 
 

time: 69 us -> 71.8 us (1.041)
  the two profiles are of different devices: /device:TPU:1 before, /device:TPU:6 now
where the time goes in v8:
time: 71.8 us; the launch traced here: 71.4 us
  blocking collectives  32.5 us (45%)
  waiting for transfers between devices  21.6 us (30%)
  Pallas kernels  8.21 us (11%)
  starting transfers between devices  7.76 us (11%)
  between operations  0.84 us (1%)
    all_to_all x1, blocking collectives, shards(): got = lax.all_to_all(rows, LAB, 0, 0, tiled=True)  32.5 us
    ppermute x3, waiting for transfers between devices, along(): return lax.ppermute(block, INST, pairs)  10.5 us
    ppermute x2, waiting for transfers between devices, shards(): lax.ppermute(sums[cut:].astype(BF), 'x', [(i, i ^ left) for i in range(ch...  9.63 us
    ppermute x3, starting transfers between devices, along(): return lax.ppermute(block, INST, pairs)  6.34 us
    pallas_call x2, Pallas kernels, later(): pl.pallas_call(functools.partial(later_kernel, jobs), grid=(1,), out_shap...  3.09 us
    pallas_call x1, Pallas kernels, shards(): pl.pallas_call(functools.partial(first_kernel, far_steps), grid=(1,), out...  1.89 us
  transfers between devices with their start and end apart: 8, of which 5 were waited for; matrix products, arithmetic and copies ran while one was open for 0% of the time, Pallas kernels for 5%

profile of v8, /device:TPU:6, one launch (start us, length us, event | category | flops | bytes accessed | tf_op | source)
XLA Modules:
  0.0 71.4 jit_solution(2422826984956615238)
XLA Ops:
  0.7 1.9 %far_away.1 = (bf16[256,768]{1,0:T(8,128)(2,1)S(1)}, bf16[512,768]{1,0:T(8,128)(2,1)S(1)}) custom-call(s32[8]{0:T(128)} %rows_ref.3, s32[8]{0:T(128)} %labs_ref.3, bf16[8,256,256]{2,1,0:T(8,128)(2,1)} %vals_ref.3, bf16[512,768]{1,0:T(8,128)(2,1)} %feat_hbm.1), custom_call_target="tpu_custom_call" | custom-call | flops 100663296 | bytes 2228224 | tf_op jit(solution)/shard_map/far_away/pallas_call | solution.py:189
  2.6 0.1 collective-permute-start
  2.7 0.0 copy-done.1
  2.7 0.0 copy-done.2
  2.7 0.0 copy-done
  2.7 1.7 %far_own.1 = (bf16[256,768]{1,0:T(8,128)(2,1)S(1)}, bf16[768,768]{1,0:T(8,128)(2,1)S(1)}) custom-call(s32[8]{0:T(128)S(1)} %copy-done.1, s32[8]{0:T(128)S(1)} %copy-done.2, bf16[8,256,256]{2,1,0:T(8,128)(2,1)S(1)} %copy-done, bf16[512,768]{1,0:T(8,128)(2,1)S(1)} %get-tuple-element.20.x_ref), custom_call_target="tpu_custom_call" | custom-call | flops 402653184 | bytes 3407872 | tf_op jit(solution)/shard_map/far_own/pallas_call | solution.py:204
  4.4 0.0 collective-permute-done
  4.4 0.1 add_convert_fusion.1
  4.5 0.3 collective-permute-start.1
  4.8 2.5 %collective-permute-start.3 = (bf16[256,768]{1,0:T(8,128)(2,1)S(1)}, bf16[256,768]{1,0:T(8,128)(2,1)S(1)}, u32[]{:S(2)}, u32[]{:S(2)}) collective-permute-start(bf16[256,768]{1,0:T(8,128)(2,1)S(1)} %add_convert_fusion.1), channel_id=1, source_target_pairs={{0,64},{32,224},{64,128},{96,32},{128,192},{160,96},{192,0},{224,1... | collective-permute-start | bytes 1179656 | tf_op jit(solution)/shard_map/ppermute | solution.py:221
  7.3 1.4 %near_own.1.own_ref = bf16[768,768]{1,0:T(8,128)(2,1)S(1)} custom-call(s32[8]{0:T(128)S(1)} %copy-done.1, s32[8]{0:T(128)S(1)} %copy-done.2, bf16[8,256,256]{2,1,0:T(8,128)(2,1)S(1)} %copy-done, bf16[512,768]{1,0:T(8,128)(2,1)S(1)} %get-tuple-element.20.x_ref), custom_call_target="tpu_custom_call" | custom-call | flops 301989888 | bytes 3014656 | tf_op jit(solution)/shard_map/near_own/pallas_call | solution.py:204
  8.7 0.0 collective-permute-done.1.mate_ref
  8.7 0.1 add_convert_fusion
  8.8 0.0 copy-start.3
  8.8 0.1 collective-permute-start.2
  8.9 5.8 %collective-permute-done.3.far_ref = bf16[256,768]{1,0:T(8,128)(2,1)S(1)} collective-permute-done((bf16[256,768]{1,0:T(8,128)(2,1)S(1)}, bf16[256,768]{1,0:T(8,128)(2,1)S(1)}, u32[]{:S(2)}, u32[]{:S(2)}) %collective-permute-start.3) | collective-permute-done | bytes 393248 | tf_op jit(solution)/shard_map/ppermute | solution.py:221
  14.7 0.1 load.1
  14.8 3.8 %collective-permute-start.4 = (bf16[256,768]{1,0:T(8,128)(2,1)S(1)}, bf16[256,768]{1,0:T(8,128)(2,1)S(1)}, u32[]{:S(2)}, u32[]{:S(2)}) collective-permute-start(bf16[256,768]{1,0:T(8,128)(2,1)S(1)} %load.1), channel_id=1, source_target_pairs={{0,64},{32,224},{64,128},{96,32},{128,192},{160,96},{192,0},{224,1... | collective-permute-start | bytes 1179656 | tf_op jit(solution)/shard_map/ppermute | solution.py:221
  18.6 0.4 route.1
  19.0 0.0 collective-permute-done.2
  19.0 0.2 convert_add_fusion.most_ref
  19.2 4.7 %collective-permute-done.4.came_ref = bf16[256,768]{1,0:T(8,128)(2,1)S(1)} collective-permute-done((bf16[256,768]{1,0:T(8,128)(2,1)S(1)}, bf16[256,768]{1,0:T(8,128)(2,1)S(1)}, u32[]{:S(2)}, u32[]{:S(2)}) %collective-permute-start.4) | collective-permute-done | bytes 393248 | tf_op jit(solution)/shard_map/ppermute | solution.py:221
  23.9 1.1 %pack.1 = (f32[256,768]{1,0:T(8,128)}, bf16[32,49,2,128]{3,2,1,0:T(2,128)(2,1)S(1)}) custom-call(f32[256,768]{1,0:T(8,128)S(1)} %convert_add_fusion.most_ref, bf16[256,768]{1,0:T(8,128)(2,1)S(1)} %collective-permute-done.4.came_ref, bf16[512,256]{1,0:T(8,128)(2,1)S(1)} %get-tuple-element.24.place_ref, bf16[256,128]{1,0:T(8,128)(2,1)S(1)} %get-tuple-element.25.inside_ref), custom_call_target="tpu_custom_call" | custom-call | tf_op jit(solution)/shard_map/pack/pallas_call | solution.py:258
  25.0 32.5 %all_to_all.5.got_ref = bf16[32,49,2,128]{3,2,1,0:T(2,128)(2,1)S(1)} all-to-all(bf16[32,49,2,128]{3,2,1,0:T(2,128)(2,1)S(1)} %get-tuple-element.27), channel_id=1, replica_groups=mesh['x'=4,'c'=2,'z'=8,'y'=4] {'z','y'}, dimensions={0} | all-to-all | bytes 1605632 | tf_op jit(solution)/shard_map/all_to_all | solution.py:268
  57.5 0.9 %combine.1 = (f32[128,768]{1,0:T(8,128)S(1)}, bf16[128,768]{1,0:T(8,128)(2,1)S(1)}) custom-call(bf16[32,49,2,128]{3,2,1,0:T(2,128)(2,1)S(1)} %all_to_all.5.got_ref), custom_call_target="tpu_custom_call" | custom-call | tf_op jit(solution)/shard_map/combine/pallas_call | solution.py:270
  58.4 0.1 collective-permute-start.5
  58.5 1.4 %collective-permute-done.5 = bf16[128,768]{1,0:T(8,128)(2,1)S(1)} collective-permute-done((bf16[128,768]{1,0:T(8,128)(2,1)S(1)}, bf16[128,768]{1,0:T(8,128)(2,1)S(1)}, u32[]{:S(2)}, u32[]{:S(2)}) %collective-permute-start.5) | collective-permute-done | bytes 196640 | tf_op jit(solution)/shard_map/ppermute | solution.py:216
  60.0 0.9 %collective-permute-start.6 = (bf16[64,768]{1,0:T(8,128)(2,1)S(1)}, bf16[64,768]{1,0:T(8,128)(2,1)S(1)}, u32[]{:S(2)}, u32[]{:S(2)}) collective-permute-start(bf16[64,768]{1,0:T(8,128)(2,1)S(1)} %slice.49), channel_id=1, source_target_pairs={{0,128},{64,192},{128,0},{192,64},{1,129},{65,193},{129,1},{193,65... | collective-permute-start | bytes 294920 | tf_op jit(solution)/shard_map/ppermute | solution.py:286
  60.9 5.6 %collective-permute-done.6 = bf16[64,768]{1,0:T(8,128)(2,1)S(1)} collective-permute-done((bf16[64,768]{1,0:T(8,128)(2,1)S(1)}, bf16[64,768]{1,0:T(8,128)(2,1)S(1)}, u32[]{:S(2)}, u32[]{:S(2)}) %collective-permute-start.6) | collective-permute-done | bytes 98336 | tf_op jit(solution)/shard_map/ppermute | solution.py:286
  66.5 0.1 collective-permute-start.7
  66.6 4.1 %collective-permute-done.7.came_ref = bf16[32,768]{1,0:T(8,128)(2,1)S(1)} collective-permute-done((bf16[32,768]{1,0:T(8,128)(2,1)S(1)}, bf16[32,768]{1,0:T(8,128)(2,1)S(1)}, u32[]{:S(2)}, u32[]{:S(2)}) %collective-permute-start.7) | collective-permute-done | bytes 49184 | tf_op jit(solution)/shard_map/ppermute | solution.py:286
  70.7 0.7 %finish.1 = f32[32,768]{1,0:T(8,128)} custom-call(f32[32,768]{1,0:T(8,128)S(1)} %slice.40.own_ref, bf16[32,768]{1,0:T(8,128)(2,1)S(1)} %collective-permute-done.7.came_ref), custom_call_target="tpu_custom_call" | custom-call | tf_op jit(solution)/shard_map/finish/pallas_call | solution.py:291
  (9 shorter events, 0.1 us)
Async XLA Ops:
  0.6 2.0 %copy-start.1 = (s32[8]{0:T(128)S(1)}, s32[8]{0:T(128)}, u32[]{:S(2)}) copy-start(s32[8]{0:T(128)} %rows_ref.3) | copy-start | bytes 100
  0.6 2.0 %copy-start.2 = (s32[8]{0:T(128)S(1)}, s32[8]{0:T(128)}, u32[]{:S(2)}) copy-start(s32[8]{0:T(128)} %labs_ref.3) | copy-start | bytes 100
  0.7 2.0 %copy-start = (bf16[8,256,256]{2,1,0:T(8,128)(2,1)S(1)}, bf16[8,256,256]{2,1,0:T(8,128)(2,1)}, u32[]{:S(2)}) copy-start(bf16[8,256,256]{2,1,0:T(8,128)(2,1)} %vals_ref.3) | copy-start | bytes 3145732
  2.6 1.9 %collective-permute-start = (bf16[256,768]{1,0:T(8,128)(2,1)S(1)}, bf16[256,768]{1,0:T(8,128)(2,1)S(1)}, u32[]{:S(2)}, u32[]{:S(2)}) collective-permute-start(bf16[256,768]{1,0:T(8,128)(2,1)S(1)} %get-tuple-element.19), channel_id=1, source_target_pairs={{0,32},{32,0},{1,33},{33,1},{2,34},{34,2},{3,35},{35,3},{4,36},{36... | collective-permute-start | bytes 1179656 | tf_op jit(solution)/shard_map/ppermute | solution.py:216
  4.5 4.2 %collective-permute-start.1 = (bf16[768,768]{1,0:T(8,128)(2,1)S(1)}, bf16[768,768]{1,0:T(8,128)(2,1)S(1)}, u32[]{:S(2)}, u32[]{:S(2)}) collective-permute-start(bf16[768,768]{1,0:T(8,128)(2,1)S(1)} %get-tuple-element.21), channel_id=1, source_target_pairs={{0,32},{32,0},{1,33},{33,1},{2,34},{34,2},{3,35},{35,3},{4,36},{36... | collective-permute-start | bytes 3538952 | tf_op jit(solution)/shard_map/ppermute | solution.py:216
  4.8 9.9 %collective-permute-start.3 = (bf16[256,768]{1,0:T(8,128)(2,1)S(1)}, bf16[256,768]{1,0:T(8,128)(2,1)S(1)}, u32[]{:S(2)}, u32[]{:S(2)}) collective-permute-start(bf16[256,768]{1,0:T(8,128)(2,1)S(1)} %add_convert_fusion.1), channel_id=1, source_target_pairs={{0,64},{32,224},{64,128},{96,32},{128,192},{160,96},{192,0},{224,1... | collective-permute-start | bytes 1179656 | tf_op jit(solution)/shard_map/ppermute | solution.py:221
  8.8 9.8 %copy-start.3 = (s32[256]{0:T(256)S(1)}, s32[256]{0:T(256)}, u32[]{:S(2)}) copy-start(s32[256]{0:T(256)} %param.9) | copy-start | bytes 3076
  8.8 10.1 %collective-permute-start.2 = (bf16[256,768]{1,0:T(8,128)(2,1)S(1)}, bf16[256,768]{1,0:T(8,128)(2,1)S(1)}, u32[]{:S(2)}, u32[]{:S(2)}) collective-permute-start(bf16[256,768]{1,0:T(8,128)(2,1)S(1)} %add_convert_fusion), channel_id=1, source_target_pairs={{0,192},{32,96},{64,0},{96,160},{128,64},{160,224},{192,128},{224,... | collective-permute-start | bytes 1179656 | tf_op jit(solution)/shard_map/ppermute | solution.py:221
  14.8 9.1 %collective-permute-start.4 = (bf16[256,768]{1,0:T(8,128)(2,1)S(1)}, bf16[256,768]{1,0:T(8,128)(2,1)S(1)}, u32[]{:S(2)}, u32[]{:S(2)}) collective-permute-start(bf16[256,768]{1,0:T(8,128)(2,1)S(1)} %load.1), channel_id=1, source_target_pairs={{0,64},{32,224},{64,128},{96,32},{128,192},{160,96},{192,0},{224,1... | collective-permute-start | bytes 1179656 | tf_op jit(solution)/shard_map/ppermute | solution.py:221
  58.4 1.5 %collective-permute-start.5 = (bf16[128,768]{1,0:T(8,128)(2,1)S(1)}, bf16[128,768]{1,0:T(8,128)(2,1)S(1)}, u32[]{:S(2)}, u32[]{:S(2)}) collective-permute-start(bf16[128,768]{1,0:T(8,128)(2,1)S(1)} %get-tuple-element.29), channel_id=1, source_target_pairs={{0,32},{32,0},{1,33},{33,1},{2,34},{34,2},{3,35},{35,3},{4,36},{36... | collective-permute-start | bytes 589832 | tf_op jit(solution)/shard_map/ppermute | solution.py:216
  60.0 6.4 %collective-permute-start.6 = (bf16[64,768]{1,0:T(8,128)(2,1)S(1)}, bf16[64,768]{1,0:T(8,128)(2,1)S(1)}, u32[]{:S(2)}, u32[]{:S(2)}) collective-permute-start(bf16[64,768]{1,0:T(8,128)(2,1)S(1)} %slice.49), channel_id=1, source_target_pairs={{0,128},{64,192},{128,0},{192,64},{1,129},{65,193},{129,1},{193,65... | collective-permute-start | bytes 294920 | tf_op jit(solution)/shard_map/ppermute | solution.py:286
  66.5 4.2 %collective-permute-start.7 = (bf16[32,768]{1,0:T(8,128)(2,1)S(1)}, bf16[32,768]{1,0:T(8,128)(2,1)S(1)}, u32[]{:S(2)}, u32[]{:S(2)}) collective-permute-start(bf16[32,768]{1,0:T(8,128)(2,1)S(1)} %slice.50), channel_id=1, source_target_pairs={{0,64},{64,0},{128,192},{192,128},{1,65},{65,1},{129,193},{193,129... | collective-permute-start | bytes 147464 | tf_op jit(solution)/shard_map/ppermute | solution.py:286

commit v9 on v6

--- a/solution.py
+++ b/solution.py
@@ -78,14 +78,16 @@
 def first_kernel(
     steps, rows_hbm, labs_hbm, vals_hbm, feat_hbm, out_ref, x_ref, rows_ref, labs_ref, vals_ref, feat_ref, sems
 ):
-    feat_in = pltpu.make_async_copy(feat_hbm, feat_ref, sems.at[3])
+    tile = vals_ref.shape[1]
+    halves = [slice(r * tile, (r + 1) * tile) for r in range(RT)]
+    feats = [pltpu.make_async_copy(feat_hbm.at[h], feat_ref.at[h], sems.at[3 + r]) for r, h in enumerate(halves)]
     copies = tiles_in(rows_hbm, labs_hbm, vals_hbm, rows_ref, labs_ref, vals_ref, sems)
-    feat_in.start()
-    for copy in copies:
+    for copy in feats + copies:
         copy.start()
-    feat_in.wait()
-    f = feat_ref[...].astype(F32)
-    x_ref[...] = (f * lax.rsqrt(jnp.sum(f * f, axis=-1, keepdims=True) + 1e-06)).astype(BF)
+    for copy, h in zip(feats, halves):
+        copy.wait()
+        f = feat_ref[h, :].astype(F32)
+        x_ref[h, :] = (f * lax.rsqrt(jnp.sum(f * f, axis=-1, keepdims=True) + 1e-06)).astype(BF)
     for copy in copies:
         copy.wait()
     product(True, steps, rows_ref, labs_ref, vals_ref, x_ref, out_ref)
@@ -96,7 +98,7 @@
         product(other, steps, rows_ref, labs_ref, vals_ref, x_ref, out_ref)
 
 
-def route_kernel(n_lab, ids_ref, place_ref, inside_ref):
+def route_kernel(n_lab, ids_ref, place_ref, beside_ref):
     rows, labs = place_ref.shape
     ids = ids_ref[...]
     down = lax.broadcasted_iota(jnp.int32, (labs, labs), 0)
@@ -108,33 +110,40 @@
     core = owner // n_lab % CORES
     chip = owner // (n_lab * CORES) * n_lab + owner % n_lab
     row = core * (rows // CORES) + chip * SLOTS + rank
-    place_ref[...] = jnp.where(lax.broadcasted_iota(jnp.int32, (rows, labs), 0) == row, 1.0, 0.0).astype(BF)
-    inside_ref[...] = jnp.broadcast_to((ids_down % CL_OWN).astype(F32), inside_ref.shape).astype(BF)
+    place = jnp.where(lax.broadcasted_iota(jnp.int32, (rows, labs), 0) == row, 1.0, 0.0).astype(BF)
+    place_ref[...] = place
+    inside = jnp.broadcast_to((ids_down % CL_OWN).astype(F32), (labs, LANES)).astype(BF)
+    inside = jnp.dot(place, inside, preferred_element_type=F32)
+    half = rows // CORES
+    lane = lax.broadcasted_iota(jnp.int32, (half, LANES), 1)
+    beside_ref[...] = jnp.where(lane < LANES // CORES, inside[:half], inside[half:]).astype(BF)
 
 
 def load_kernel(own_ref, mate_ref, far_ref, out_ref):
     out_ref[...] = (own_ref[...].astype(F32) + mate_ref[...].astype(F32) + far_ref[...].astype(F32)).astype(BF)
 
 
-def pack_kernel(most_ref, came_ref, place_ref, inside_ref, emb_hbm, out_ref, emb_ref, sem):
+def pack_kernel(most_ref, came_ref, place_ref, beside_ref, emb_hbm, out_ref, emb_ref, sems):
     chips, cols = out_ref.shape[0], out_ref.shape[1] // CORES
     rows = chips * SLOTS
-    summed = most_ref[...] + came_ref[...].astype(F32)
-    unit = summed * lax.rsqrt(jnp.sum(summed * summed, axis=-1, keepdims=True) + 1e-06)
-    emb_ref[...] = unit
-    emb_out = pltpu.make_async_copy(emb_ref, emb_hbm, sem)
-    emb_out.start()
-    place = place_ref[...]
-    moved = jnp.dot(place, unit.astype(BF), preferred_element_type=F32).astype(BF)
+    half = emb_ref.shape[0] // 2
+    units, copies = [], []
+    for k in range(2):
+        part = slice(k * half, (k + 1) * half)
+        summed = most_ref[part, :] + came_ref[part, :].astype(F32)
+        unit = summed * lax.rsqrt(jnp.sum(summed * summed, axis=-1, keepdims=True) + 1e-06)
+        emb_ref[part, :] = unit
+        copies.append(pltpu.make_async_copy(emb_ref.at[part], emb_hbm.at[part], sems.at[k]))
+        copies[k].start()
+        units.append(unit.astype(BF))
+    moved = jnp.dot(place_ref[...], jnp.concatenate(units, axis=0), preferred_element_type=F32).astype(BF)
     for core in range(CORES):
         for col in range(cols):
             block = moved[core * rows : (core + 1) * rows, col * LANES : (col + 1) * LANES]
             out_ref[:, core * cols + col] = block.reshape(chips, SLOTS, LANES)
-    inside = jnp.dot(place, inside_ref[...], preferred_element_type=F32)
-    lane = lax.broadcasted_iota(jnp.int32, (rows, LANES), 1)
-    beside = jnp.where(lane < LANES // CORES, inside[:rows], inside[rows:])
-    out_ref[:, CORES * cols] = beside.astype(BF).reshape(chips, SLOTS, LANES)
-    emb_out.wait()
+    out_ref[:, CORES * cols] = beside_ref[...].reshape(chips, SLOTS, LANES)
+    for copy in copies:
+        copy.wait()
 
 
 def combine_kernel(got_ref, mine_ref, other_ref):
@@ -187,7 +196,7 @@
         in_specs=[hbm] * 4,
         out_specs=(full((tile, width)), full((insts, width))),
         scratch_shapes=tile_scratch
-        + [pltpu.VMEM((insts, width), BF), pltpu.SemaphoreType.DMA((4,))],
+        + [pltpu.VMEM((insts, width), BF), pltpu.SemaphoreType.DMA((3 + RT,))],
         compiler_params=params(),
         cost_estimate=product_cost(far_steps),
         name="far_away",
@@ -238,12 +247,12 @@
     )(own, mate, far_came)
     came = along(loaded, 1)
     most = pair(0) + free_came.astype(F32)
-    place, inside = pl.pallas_call(
+    place, beside = pl.pallas_call(
         functools.partial(route_kernel, lax.axis_size(LAB)),
         grid=(1,),
-        out_shape=(jax.ShapeDtypeStruct((SLOTS * owners, labs), BF), jax.ShapeDtypeStruct((labs, LANES), BF)),
+        out_shape=(jax.ShapeDtypeStruct((SLOTS * owners, labs), BF), jax.ShapeDtypeStruct((owners, LANES), BF)),
         in_specs=[full((1, labs))],
-        out_specs=(full((SLOTS * owners, labs)), full((labs, LANES))),
+        out_specs=(full((SLOTS * owners, labs)), full((owners, LANES))),
         compiler_params=params(),
         name="route",
     )(ids.reshape(1, labs))
@@ -253,12 +262,12 @@
         pack_kernel,
         grid=(1,),
         out_shape=(jax.ShapeDtypeStruct((labs, width), F32), jax.ShapeDtypeStruct(message, BF)),
-        in_specs=[block] * 2 + [full((SLOTS * owners, labs)), full((labs, LANES))],
+        in_specs=[block] * 2 + [full((SLOTS * owners, labs)), full((owners, LANES))],
         out_specs=(hbm, full(message)),
-        scratch_shapes=[pltpu.VMEM((labs, width), F32), pltpu.SemaphoreType.DMA],
+        scratch_shapes=[pltpu.VMEM((labs, width), F32), pltpu.SemaphoreType.DMA((2,))],
         compiler_params=params(),
         name="pack",
-    )(most, came, place, inside)
+    )(most, came, place, beside)
     got = lax.all_to_all(rows, ("x",) + LAB, 0, 0, tiled=True)
     sums = jax.ShapeDtypeStruct((CL_OWN, width), F32)
     mine, other = pl.pallas_call(

time: 68.6 us -> 68.7 us (level)
  waiting for transfers between devices: 11 us -> 11.8 us
  transfers between devices with their start and end apart: 6 -> 6, of which waited for: 5 -> 5; matrix products, arithmetic and copies ran while one was open for 0% -> 0% of each run, Pallas kernels for 5% -> 6%
where the time goes in v9:
time: 68.7 us; the launch traced here: 68.4 us
  blocking collectives  36.6 us (53%)
  waiting for transfers between devices  11.8 us (17%)
  starting transfers between devices  11.2 us (16%)
  Pallas kernels  7.7 us (11%)
  between operations  0.74 us (1%)
    all_to_all x1, blocking collectives, shards(): got = lax.all_to_all(rows, ('x',) + LAB, 0, 0, tiled=True)  36.6 us
    ppermute x3, waiting for transfers between devices, along(): return lax.ppermute(block, INST, pairs)  10.2 us
    ppermute x3, starting transfers between devices, across(): return lax.ppermute(block, 'c', [(0, 1), (1, 0)])  9.33 us
    pallas_call x2, Pallas kernels, later(): pl.pallas_call(functools.partial(later_kernel, jobs), grid=(1,), out_shap...  3.18 us
    ppermute x3, starting transfers between devices, along(): return lax.ppermute(block, INST, pairs)  1.87 us
    pallas_call x1, Pallas kernels, shards(): pl.pallas_call(functools.partial(first_kernel, far_steps), grid=(1,), out...  1.63 us
    ppermute x3, waiting for transfers between devices, across(): return lax.ppermute(block, 'c', [(0, 1), (1, 0)])  1.54 us
  transfers between devices with their start and end apart: 6, of which 5 were waited for; matrix products, arithmetic and copies ran while one was open for 0% of the time, Pallas kernels for 6%

profile of v9, /device:TPU:1, one launch (start us, length us, event | category | flops | bytes accessed | tf_op | source)
XLA Modules:
  0.0 68.4 jit_solution(17270421486079572742)
XLA Ops:
  0.6 0.0 copy-start.1
  0.6 0.0 copy-start.2
  0.7 0.0 copy-start
  0.7 1.6 %far_away.1 = (bf16[256,768]{1,0:T(8,128)(2,1)S(1)}, bf16[512,768]{1,0:T(8,128)(2,1)S(1)}) custom-call(s32[8]{0:T(128)} %rows_ref.3, s32[8]{0:T(128)} %labs_ref.3, bf16[8,256,256]{2,1,0:T(8,128)(2,1)} %vals_ref.3, bf16[512,768]{1,0:T(8,128)(2,1)} %feat_hbm.1), custom_call_target="tpu_custom_call" | custom-call | flops 100663296 | bytes 2228224 | tf_op jit(solution)/shard_map/far_away/pallas_call | solution.py:192
  2.3 3.6 %collective-permute-start = (bf16[256,768]{1,0:T(8,128)(2,1)S(1)}, bf16[256,768]{1,0:T(8,128)(2,1)S(1)}, u32[]{:S(2)}, u32[]{:S(2)}) collective-permute-start(bf16[256,768]{1,0:T(8,128)(2,1)S(1)} %get-tuple-element.19), channel_id=1, source_target_pairs={{0,32},{32,0},{1,33},{33,1},{2,34},{34,2},{3,35},{35,3},{4,36},{36... | collective-permute-start | bytes 1179656 | tf_op jit(solution)/shard_map/ppermute | solution.py:219
  5.9 0.0 copy-done.1
  5.9 0.0 copy-done.2
  5.9 0.0 copy-done
  5.9 1.7 %far_own.1 = (bf16[256,768]{1,0:T(8,128)(2,1)S(1)}, bf16[768,768]{1,0:T(8,128)(2,1)S(1)}) custom-call(s32[8]{0:T(128)S(1)} %copy-done.1, s32[8]{0:T(128)S(1)} %copy-done.2, bf16[8,256,256]{2,1,0:T(8,128)(2,1)S(1)} %copy-done, bf16[512,768]{1,0:T(8,128)(2,1)S(1)} %get-tuple-element.20.x_ref), custom_call_target="tpu_custom_call" | custom-call | flops 402653184 | bytes 3407872 | tf_op jit(solution)/shard_map/far_own/pallas_call | solution.py:207
  7.6 0.0 collective-permute-done
  7.6 0.1 add_convert_fusion.1
  7.7 0.4 collective-permute-start.1
  8.1 0.5 collective-permute-start.3
  8.6 1.5 %near_own.1.own_ref = bf16[768,768]{1,0:T(8,128)(2,1)S(1)} custom-call(s32[8]{0:T(128)S(1)} %copy-done.1, s32[8]{0:T(128)S(1)} %copy-done.2, bf16[8,256,256]{2,1,0:T(8,128)(2,1)S(1)} %copy-done, bf16[512,768]{1,0:T(8,128)(2,1)S(1)} %get-tuple-element.20.x_ref), custom_call_target="tpu_custom_call" | custom-call | flops 301989888 | bytes 3014656 | tf_op jit(solution)/shard_map/near_own/pallas_call | solution.py:207
  10.1 0.6 collective-permute-done.1.mate_ref
  10.7 0.1 add_convert_fusion
  10.8 0.0 copy-start.3
  10.8 0.6 collective-permute-start.2
  11.4 4.3 %collective-permute-done.3.far_ref = bf16[256,768]{1,0:T(8,128)(2,1)S(1)} collective-permute-done((bf16[256,768]{1,0:T(8,128)(2,1)S(1)}, bf16[256,768]{1,0:T(8,128)(2,1)S(1)}, u32[]{:S(2)}, u32[]{:S(2)}) %collective-permute-start.3) | collective-permute-done | bytes 393248 | tf_op jit(solution)/shard_map/ppermute | solution.py:224
  15.7 0.1 load.1
  15.9 0.8 %collective-permute-start.4 = (bf16[256,768]{1,0:T(8,128)(2,1)S(1)}, bf16[256,768]{1,0:T(8,128)(2,1)S(1)}, u32[]{:S(2)}, u32[]{:S(2)}) collective-permute-start(bf16[256,768]{1,0:T(8,128)(2,1)S(1)} %load.1), channel_id=1, source_target_pairs={{0,64},{32,224},{64,128},{96,32},{128,192},{160,96},{192,0},{224,1... | collective-permute-start | bytes 1179656 | tf_op jit(solution)/shard_map/ppermute | solution.py:224
  16.7 0.0 copy-done.3
  16.7 0.5 route.1
  17.1 3.7 %collective-permute-done.2 = bf16[256,768]{1,0:T(8,128)(2,1)S(1)} collective-permute-done((bf16[256,768]{1,0:T(8,128)(2,1)S(1)}, bf16[256,768]{1,0:T(8,128)(2,1)S(1)}, u32[]{:S(2)}, u32[]{:S(2)}) %collective-permute-start.2) | collective-permute-done | bytes 393248 | tf_op jit(solution)/shard_map/ppermute | solution.py:224
  20.9 0.2 convert_add_fusion.most_ref
  21.0 2.2 %collective-permute-done.4.came_ref = bf16[256,768]{1,0:T(8,128)(2,1)S(1)} collective-permute-done((bf16[256,768]{1,0:T(8,128)(2,1)S(1)}, bf16[256,768]{1,0:T(8,128)(2,1)S(1)}, u32[]{:S(2)}, u32[]{:S(2)}) %collective-permute-start.4) | collective-permute-done | bytes 393248 | tf_op jit(solution)/shard_map/ppermute | solution.py:224
  23.2 1.0 %pack.1 = (f32[256,768]{1,0:T(8,128)}, bf16[128,13,2,128]{3,2,1,0:T(2,128)(2,1)S(1)}) custom-call(f32[256,768]{1,0:T(8,128)S(1)} %convert_add_fusion.most_ref, bf16[256,768]{1,0:T(8,128)(2,1)S(1)} %collective-permute-done.4.came_ref, bf16[512,256]{1,0:T(8,128)(2,1)S(1)} %get-tuple-element.24.place_ref, bf16[256,128]{1,0:T(8,128)(2,1)S(1)} %get-tuple-element.25.beside_ref), custom_call_target="tpu_custom_call" | custom-call | tf_op jit(solution)/shard_map/pack/pallas_call | solution.py:261
  24.2 36.6 %all_to_all.5.got_ref = bf16[128,13,2,128]{3,2,1,0:T(2,128)(2,1)S(1)} all-to-all(bf16[128,13,2,128]{3,2,1,0:T(2,128)(2,1)S(1)} %get-tuple-element.27), channel_id=1, replica_groups=mesh['x'=4,'c'=2,'z'=8,'y'=4] {'x','z','y'}, dimensions={0} | all-to-all | bytes 1703936 | tf_op jit(solution)/shard_map/all_to_all | solution.py:271
  60.9 0.5 combine.1
  61.4 5.3 %collective-permute-start.5 = (f32[32,768]{1,0:T(8,128)S(1)}, f32[32,768]{1,0:T(8,128)S(1)}, u32[]{:S(2)}, u32[]{:S(2)}) collective-permute-start(f32[32,768]{1,0:T(8,128)S(1)} %get-tuple-element.29), channel_id=1, source_target_pairs={{0,32},{32,0},{1,33},{33,1},{2,34},{34,2},{3,35},{35,3},{4,36},{36... | collective-permute-start | bytes 294920 | tf_op jit(solution)/shard_map/ppermute | solution.py:219
  66.7 0.9 %collective-permute-done.5.mate_ref = f32[32,768]{1,0:T(8,128)S(1)} collective-permute-done((f32[32,768]{1,0:T(8,128)S(1)}, f32[32,768]{1,0:T(8,128)S(1)}, u32[]{:S(2)}, u32[]{:S(2)}) %collective-permute-start.5) | collective-permute-done | bytes 98336 | tf_op jit(solution)/shard_map/ppermute | solution.py:219
  67.7 0.7 %finish.1 = f32[32,768]{1,0:T(8,128)} custom-call(f32[32,768]{1,0:T(8,128)S(1)} %get-tuple-element.28.mine_ref, f32[32,768]{1,0:T(8,128)S(1)} %collective-permute-done.5.mate_ref), custom_call_target="tpu_custom_call" | custom-call | tf_op jit(solution)/shard_map/finish/pallas_call | solution.py:282
Async XLA Ops:
  0.6 5.3 %copy-start.1 = (s32[8]{0:T(128)S(1)}, s32[8]{0:T(128)}, u32[]{:S(2)}) copy-start(s32[8]{0:T(128)} %rows_ref.3) | copy-start | bytes 100
  0.6 5.3 %copy-start.2 = (s32[8]{0:T(128)S(1)}, s32[8]{0:T(128)}, u32[]{:S(2)}) copy-start(s32[8]{0:T(128)} %labs_ref.3) | copy-start | bytes 100
  0.7 5.3 %copy-start = (bf16[8,256,256]{2,1,0:T(8,128)(2,1)S(1)}, bf16[8,256,256]{2,1,0:T(8,128)(2,1)}, u32[]{:S(2)}) copy-start(bf16[8,256,256]{2,1,0:T(8,128)(2,1)} %vals_ref.3) | copy-start | bytes 3145732
  2.3 5.3 %collective-permute-start = (bf16[256,768]{1,0:T(8,128)(2,1)S(1)}, bf16[256,768]{1,0:T(8,128)(2,1)S(1)}, u32[]{:S(2)}, u32[]{:S(2)}) collective-permute-start(bf16[256,768]{1,0:T(8,128)(2,1)S(1)} %get-tuple-element.19), channel_id=1, source_target_pairs={{0,32},{32,0},{1,33},{33,1},{2,34},{34,2},{3,35},{35,3},{4,36},{36... | collective-permute-start | bytes 1179656 | tf_op jit(solution)/shard_map/ppermute | solution.py:219
  7.7 2.9 %collective-permute-start.1 = (bf16[768,768]{1,0:T(8,128)(2,1)S(1)}, bf16[768,768]{1,0:T(8,128)(2,1)S(1)}, u32[]{:S(2)}, u32[]{:S(2)}) collective-permute-start(bf16[768,768]{1,0:T(8,128)(2,1)S(1)} %get-tuple-element.21), channel_id=1, source_target_pairs={{0,32},{32,0},{1,33},{33,1},{2,34},{34,2},{3,35},{35,3},{4,36},{36... | collective-permute-start | bytes 3538952 | tf_op jit(solution)/shard_map/ppermute | solution.py:219
  8.1 7.6 %collective-permute-start.3 = (bf16[256,768]{1,0:T(8,128)(2,1)S(1)}, bf16[256,768]{1,0:T(8,128)(2,1)S(1)}, u32[]{:S(2)}, u32[]{:S(2)}) collective-permute-start(bf16[256,768]{1,0:T(8,128)(2,1)S(1)} %add_convert_fusion.1), channel_id=1, source_target_pairs={{0,64},{32,224},{64,128},{96,32},{128,192},{160,96},{192,0},{224,1... | collective-permute-start | bytes 1179656 | tf_op jit(solution)/shard_map/ppermute | solution.py:224
  10.8 5.9 %copy-start.3 = (s32[256]{0:T(256)S(1)}, s32[256]{0:T(256)}, u32[]{:S(2)}) copy-start(s32[256]{0:T(256)} %param.9) | copy-start | bytes 3076
  10.8 10.1 %collective-permute-start.2 = (bf16[256,768]{1,0:T(8,128)(2,1)S(1)}, bf16[256,768]{1,0:T(8,128)(2,1)S(1)}, u32[]{:S(2)}, u32[]{:S(2)}) collective-permute-start(bf16[256,768]{1,0:T(8,128)(2,1)S(1)} %add_convert_fusion), channel_id=1, source_target_pairs={{0,192},{32,96},{64,0},{96,160},{128,64},{160,224},{192,128},{224,... | collective-permute-start | bytes 1179656 | tf_op jit(solution)/shard_map/ppermute | solution.py:224
  15.9 7.3 %collective-permute-start.4 = (bf16[256,768]{1,0:T(8,128)(2,1)S(1)}, bf16[256,768]{1,0:T(8,128)(2,1)S(1)}, u32[]{:S(2)}, u32[]{:S(2)}) collective-permute-start(bf16[256,768]{1,0:T(8,128)(2,1)S(1)} %load.1), channel_id=1, source_target_pairs={{0,64},{32,224},{64,128},{96,32},{128,192},{160,96},{192,0},{224,1... | collective-permute-start | bytes 1179656 | tf_op jit(solution)/shard_map/ppermute | solution.py:224
  61.4 6.3 %collective-permute-start.5 = (f32[32,768]{1,0:T(8,128)S(1)}, f32[32,768]{1,0:T(8,128)S(1)}, u32[]{:S(2)}, u32[]{:S(2)}) collective-permute-start(f32[32,768]{1,0:T(8,128)S(1)} %get-tuple-element.29), channel_id=1, source_target_pairs={{0,32},{32,0},{1,33},{33,1},{2,34},{34,2},{3,35},{35,3},{4,36},{36... | collective-permute-start | bytes 294920 | tf_op jit(solution)/shard_map/ppermute | solution.py:219

commit v10 on v9

--- a/solution.py
+++ b/solution.py
@@ -76,7 +76,7 @@
 
 
 def first_kernel(
-    steps, rows_hbm, labs_hbm, vals_hbm, feat_hbm, out_ref, x_ref, rows_ref, labs_ref, vals_ref, feat_ref, sems
+    steps, rows_hbm, labs_hbm, vals_hbm, feat_hbm, out_ref, x_ref, vals_ref, rows_ref, labs_ref, feat_ref, sems
 ):
     tile = vals_ref.shape[1]
     halves = [slice(r * tile, (r + 1) * tile) for r in range(RT)]
@@ -179,7 +179,7 @@
     cols = width // LANES
     smem = pl.BlockSpec(memory_space=pltpu.MemorySpace.SMEM)
     hbm = pl.BlockSpec(memory_space=pltpu.MemorySpace.HBM)
-    tile_scratch = [pltpu.SMEM((tiles,), jnp.int32)] * 2 + [pltpu.VMEM(tile_values.shape, BF)]
+    tile_scratch = [pltpu.SMEM((tiles,), jnp.int32)] * 2
     far_steps, near_steps = (2,), (0, 1, -1)
 
     def product_cost(steps):
@@ -189,12 +189,16 @@
             transcendentals=0,
         )
 
-    far_away, normed = pl.pallas_call(
+    far_away, normed, tiles_held = pl.pallas_call(
         functools.partial(first_kernel, far_steps),
         grid=(1,),
-        out_shape=(jax.ShapeDtypeStruct((tile, width), BF), jax.ShapeDtypeStruct((insts, width), BF)),
+        out_shape=(
+            jax.ShapeDtypeStruct((tile, width), BF),
+            jax.ShapeDtypeStruct((insts, width), BF),
+            jax.ShapeDtypeStruct(tile_values.shape, BF),
+        ),
         in_specs=[hbm] * 4,
-        out_specs=(full((tile, width)), full((insts, width))),
+        out_specs=(full((tile, width)), full((insts, width)), full(tile_values.shape)),
         scratch_shapes=tile_scratch
         + [pltpu.VMEM((insts, width), BF), pltpu.SemaphoreType.DMA((3 + RT,))],
         compiler_params=params(),
@@ -213,7 +217,7 @@
             compiler_params=params(),
             cost_estimate=product_cost(sum((steps for _, steps in jobs), ())),
             name=name,
-        )(tile_rows, tile_labels, tile_values, x)
+        )(tile_rows, tile_labels, tiles_held, x)
 
     def across(block):
         return lax.ppermute(block, "c", [(0, 1), (1, 0)])

time: 68.7 us -> 68.8 us (level)
  starting transfers between devices: 11.2 us -> 9.26 us
  blocking collectives: 36.6 us -> 37.7 us
  waiting for transfers between devices: 11.8 us -> 12.8 us
    ppermute x3, starting transfers between devices: 9.33 us -> 7.87 us  [across(): return lax.ppermute(block, 'c', [(0, 1), (1, 0)])]
    all_to_all x1, blocking collectives: 36.6 us -> 37.7 us  [shards(): got = lax.all_to_all(rows, ('x',) + LAB, 0, 0, tiled=True)]
    ppermute x3, waiting for transfers between devices: 1.54 us -> 2.27 us  [across(): return lax.ppermute(block, 'c', [(0, 1), (1, 0)])]
  transfers between devices with their start and end apart: 6 -> 6, of which waited for: 5 -> 5; matrix products, arithmetic and copies ran while one was open for 0% -> 0% of each run, Pallas kernels for 6% -> 5%
where the time goes in v10:
time: 68.8 us; the launch traced here: 68.6 us
  blocking collectives  37.7 us (55%)
  waiting for transfers between devices  12.8 us (19%)
  starting transfers between devices  9.26 us (13%)
  Pallas kernels  7.82 us (11%)
  between operations  0.74 us (1%)
    all_to_all x1, blocking collectives, shards(): got = lax.all_to_all(rows, ('x',) + LAB, 0, 0, tiled=True)  37.7 us
    ppermute x3, waiting for transfers between devices, along(): return lax.ppermute(block, INST, pairs)  10.5 us
    ppermute x3, starting transfers between devices, across(): return lax.ppermute(block, 'c', [(0, 1), (1, 0)])  7.87 us
    pallas_call x2, Pallas kernels, later(): pl.pallas_call(functools.partial(later_kernel, jobs), grid=(1,), out_shap...  3.01 us
    ppermute x3, waiting for transfers between devices, across(): return lax.ppermute(block, 'c', [(0, 1), (1, 0)])  2.27 us
    pallas_call x1, Pallas kernels, shards(): pl.pallas_call(functools.partial(first_kernel, far_steps), grid=(1,), out...  1.92 us
    ppermute x3, starting transfers between devices, along(): return lax.ppermute(block, INST, pairs)  1.38 us
  transfers between devices with their start and end apart: 6, of which 5 were waited for; matrix products, arithmetic and copies ran while one was open for 0% of the time, Pallas kernels for 5%

profile of v10, /device:TPU:1, one launch (start us, length us, event | category | flops | bytes accessed | tf_op | source)
XLA Modules:
  0.0 68.6 jit_solution(8831857530054967704)
XLA Ops:
  0.6 0.0 copy-start.1
  0.6 0.0 copy-start
  0.7 1.9 %far_away.1 = (bf16[256,768]{1,0:T(8,128)(2,1)S(1)}, bf16[512,768]{1,0:T(8,128)(2,1)S(1)}, bf16[8,256,256]{2,1,0:T(8,128)(2,1)S(1)}) custom-call(s32[8]{0:T(128)} %rows_ref.3, s32[8]{0:T(128)} %labs_ref.3, bf16[8,256,256]{2,1,0:T(8,128)(2,1)} %vals_hbm.1, bf16[512,768]{1,0:T(8,128)(2,1)} %feat_hbm.1), custom_call_target="tpu_custom_call" | custom-call | flops 100663296 | bytes 2228224 | tf_op jit(solution)/shard_map/far_away/pallas_call | solution.py:192
  2.6 3.2 %collective-permute-start = (bf16[256,768]{1,0:T(8,128)(2,1)S(1)}, bf16[256,768]{1,0:T(8,128)(2,1)S(1)}, u32[]{:S(2)}, u32[]{:S(2)}) collective-permute-start(bf16[256,768]{1,0:T(8,128)(2,1)S(1)} %get-tuple-element.21), channel_id=1, source_target_pairs={{0,32},{32,0},{1,33},{33,1},{2,34},{34,2},{3,35},{35,3},{4,36},{36... | collective-permute-start | bytes 1179656 | tf_op jit(solution)/shard_map/ppermute | solution.py:223
  5.8 0.0 copy-done.1
  5.8 0.0 copy-done
  5.8 2.0 %far_own.1 = (bf16[256,768]{1,0:T(8,128)(2,1)S(1)}, bf16[768,768]{1,0:T(8,128)(2,1)S(1)}) custom-call(s32[8]{0:T(128)S(1)} %copy-done, s32[8]{0:T(128)S(1)} %copy-done.1, bf16[8,256,256]{2,1,0:T(8,128)(2,1)S(1)} %get-tuple-element.17.vals_ref, bf16[512,768]{1,0:T(8,128)(2,1)S(1)} %get-tuple-element.22.x_ref), custom_call_target="tpu_custom_call" | custom-call | flops 402653184 | bytes 3407872 | tf_op jit(solution)/shard_map/far_own/pallas_call | solution.py:211
  7.8 0.0 collective-permute-done
  7.8 0.1 add_convert_fusion.1
  7.9 0.1 collective-permute-start.1
  8.0 0.5 collective-permute-start.3
  8.5 1.0 %near_own.1.own_ref = bf16[768,768]{1,0:T(8,128)(2,1)S(1)} custom-call(s32[8]{0:T(128)S(1)} %copy-done, s32[8]{0:T(128)S(1)} %copy-done.1, bf16[8,256,256]{2,1,0:T(8,128)(2,1)S(1)} %get-tuple-element.17.vals_ref, bf16[512,768]{1,0:T(8,128)(2,1)S(1)} %get-tuple-element.22.x_ref), custom_call_target="tpu_custom_call" | custom-call | flops 301989888 | bytes 3014656 | tf_op jit(solution)/shard_map/near_own/pallas_call | solution.py:211
  9.5 1.3 %collective-permute-done.1.mate_ref = bf16[768,768]{1,0:T(8,128)(2,1)S(1)} collective-permute-done((bf16[768,768]{1,0:T(8,128)(2,1)S(1)}, bf16[768,768]{1,0:T(8,128)(2,1)S(1)}, u32[]{:S(2)}, u32[]{:S(2)}) %collective-permute-start.1) | collective-permute-done | bytes 1179680 | tf_op jit(solution)/shard_map/ppermute | solution.py:223
  10.9 0.1 add_convert_fusion
  11.0 0.0 copy-start.2
  11.0 0.1 collective-permute-start.2
  11.1 4.6 %collective-permute-done.3.far_ref = bf16[256,768]{1,0:T(8,128)(2,1)S(1)} collective-permute-done((bf16[256,768]{1,0:T(8,128)(2,1)S(1)}, bf16[256,768]{1,0:T(8,128)(2,1)S(1)}, u32[]{:S(2)}, u32[]{:S(2)}) %collective-permute-start.3) | collective-permute-done | bytes 393248 | tf_op jit(solution)/shard_map/ppermute | solution.py:228
  15.6 0.1 load.1
  15.8 0.8 %collective-permute-start.4 = (bf16[256,768]{1,0:T(8,128)(2,1)S(1)}, bf16[256,768]{1,0:T(8,128)(2,1)S(1)}, u32[]{:S(2)}, u32[]{:S(2)}) collective-permute-start(bf16[256,768]{1,0:T(8,128)(2,1)S(1)} %load.1), channel_id=1, source_target_pairs={{0,64},{32,224},{64,128},{96,32},{128,192},{160,96},{192,0},{224,1... | collective-permute-start | bytes 1179656 | tf_op jit(solution)/shard_map/ppermute | solution.py:228
  16.6 0.0 copy-done.2
  16.6 0.5 route.1
  17.1 4.0 %collective-permute-done.2 = bf16[256,768]{1,0:T(8,128)(2,1)S(1)} collective-permute-done((bf16[256,768]{1,0:T(8,128)(2,1)S(1)}, bf16[256,768]{1,0:T(8,128)(2,1)S(1)}, u32[]{:S(2)}, u32[]{:S(2)}) %collective-permute-start.2) | collective-permute-done | bytes 393248 | tf_op jit(solution)/shard_map/ppermute | solution.py:228
  21.0 0.1 convert_add_fusion.most_ref
  21.2 2.0 %collective-permute-done.4.came_ref = bf16[256,768]{1,0:T(8,128)(2,1)S(1)} collective-permute-done((bf16[256,768]{1,0:T(8,128)(2,1)S(1)}, bf16[256,768]{1,0:T(8,128)(2,1)S(1)}, u32[]{:S(2)}, u32[]{:S(2)}) %collective-permute-start.4) | collective-permute-done | bytes 393248 | tf_op jit(solution)/shard_map/ppermute | solution.py:228
  23.2 1.0 %pack.1 = (f32[256,768]{1,0:T(8,128)}, bf16[128,13,2,128]{3,2,1,0:T(2,128)(2,1)S(1)}) custom-call(f32[256,768]{1,0:T(8,128)S(1)} %convert_add_fusion.most_ref, bf16[256,768]{1,0:T(8,128)(2,1)S(1)} %collective-permute-done.4.came_ref, bf16[512,256]{1,0:T(8,128)(2,1)S(1)} %get-tuple-element.26.place_ref, bf16[256,128]{1,0:T(8,128)(2,1)S(1)} %get-tuple-element.27.beside_ref), custom_call_target="tpu_custom_call" | custom-call | tf_op jit(solution)/shard_map/pack/pallas_call | solution.py:265
  24.2 37.7 %all_to_all.5.got_ref = bf16[128,13,2,128]{3,2,1,0:T(2,128)(2,1)S(1)} all-to-all(bf16[128,13,2,128]{3,2,1,0:T(2,128)(2,1)S(1)} %get-tuple-element.29), channel_id=1, replica_groups=mesh['x'=4,'c'=2,'z'=8,'y'=4] {'x','z','y'}, dimensions={0} | all-to-all | bytes 1703936 | tf_op jit(solution)/shard_map/all_to_all | solution.py:275
  61.9 0.5 combine.1
  62.4 4.5 %collective-permute-start.5 = (f32[32,768]{1,0:T(8,128)S(1)}, f32[32,768]{1,0:T(8,128)S(1)}, u32[]{:S(2)}, u32[]{:S(2)}) collective-permute-start(f32[32,768]{1,0:T(8,128)S(1)} %get-tuple-element.31), channel_id=1, source_target_pairs={{0,32},{32,0},{1,33},{33,1},{2,34},{34,2},{3,35},{35,3},{4,36},{36... | collective-permute-start | bytes 294920 | tf_op jit(solution)/shard_map/ppermute | solution.py:223
  66.9 0.9 %collective-permute-done.5.mate_ref = f32[32,768]{1,0:T(8,128)S(1)} collective-permute-done((f32[32,768]{1,0:T(8,128)S(1)}, f32[32,768]{1,0:T(8,128)S(1)}, u32[]{:S(2)}, u32[]{:S(2)}) %collective-permute-start.5) | collective-permute-done | bytes 98336 | tf_op jit(solution)/shard_map/ppermute | solution.py:223
  67.9 0.7 %finish.1 = f32[32,768]{1,0:T(8,128)} custom-call(f32[32,768]{1,0:T(8,128)S(1)} %get-tuple-element.30.mine_ref, f32[32,768]{1,0:T(8,128)S(1)} %collective-permute-done.5.mate_ref), custom_call_target="tpu_custom_call" | custom-call | tf_op jit(solution)/shard_map/finish/pallas_call | solution.py:286
Async XLA Ops:
  0.6 5.2 %copy-start.1 = (s32[8]{0:T(128)S(1)}, s32[8]{0:T(128)}, u32[]{:S(2)}) copy-start(s32[8]{0:T(128)} %labs_ref.3) | copy-start | bytes 100
  0.6 5.2 %copy-start = (s32[8]{0:T(128)S(1)}, s32[8]{0:T(128)}, u32[]{:S(2)}) copy-start(s32[8]{0:T(128)} %rows_ref.3) | copy-start | bytes 100
  2.6 5.2 %collective-permute-start = (bf16[256,768]{1,0:T(8,128)(2,1)S(1)}, bf16[256,768]{1,0:T(8,128)(2,1)S(1)}, u32[]{:S(2)}, u32[]{:S(2)}) collective-permute-start(bf16[256,768]{1,0:T(8,128)(2,1)S(1)} %get-tuple-element.21), channel_id=1, source_target_pairs={{0,32},{32,0},{1,33},{33,1},{2,34},{34,2},{3,35},{35,3},{4,36},{36... | collective-permute-start | bytes 1179656 | tf_op jit(solution)/shard_map/ppermute | solution.py:223
  7.9 2.9 %collective-permute-start.1 = (bf16[768,768]{1,0:T(8,128)(2,1)S(1)}, bf16[768,768]{1,0:T(8,128)(2,1)S(1)}, u32[]{:S(2)}, u32[]{:S(2)}) collective-permute-start(bf16[768,768]{1,0:T(8,128)(2,1)S(1)} %get-tuple-element.23), channel_id=1, source_target_pairs={{0,32},{32,0},{1,33},{33,1},{2,34},{34,2},{3,35},{35,3},{4,36},{36... | collective-permute-start | bytes 3538952 | tf_op jit(solution)/shard_map/ppermute | solution.py:223
  8.0 7.6 %collective-permute-start.3 = (bf16[256,768]{1,0:T(8,128)(2,1)S(1)}, bf16[256,768]{1,0:T(8,128)(2,1)S(1)}, u32[]{:S(2)}, u32[]{:S(2)}) collective-permute-start(bf16[256,768]{1,0:T(8,128)(2,1)S(1)} %add_convert_fusion.1), channel_id=1, source_target_pairs={{0,64},{32,224},{64,128},{96,32},{128,192},{160,96},{192,0},{224,1... | collective-permute-start | bytes 1179656 | tf_op jit(solution)/shard_map/ppermute | solution.py:228
  11.0 5.6 %copy-start.2 = (s32[256]{0:T(256)S(1)}, s32[256]{0:T(256)}, u32[]{:S(2)}) copy-start(s32[256]{0:T(256)} %param.9) | copy-start | bytes 3076
  11.0 10.1 %collective-permute-start.2 = (bf16[256,768]{1,0:T(8,128)(2,1)S(1)}, bf16[256,768]{1,0:T(8,128)(2,1)S(1)}, u32[]{:S(2)}, u32[]{:S(2)}) collective-permute-start(bf16[256,768]{1,0:T(8,128)(2,1)S(1)} %add_convert_fusion), channel_id=1, source_target_pairs={{0,192},{32,96},{64,0},{96,160},{128,64},{160,224},{192,128},{224,... | collective-permute-start | bytes 1179656 | tf_op jit(solution)/shard_map/ppermute | solution.py:228
  15.8 7.4 %collective-permute-start.4 = (bf16[256,768]{1,0:T(8,128)(2,1)S(1)}, bf16[256,768]{1,0:T(8,128)(2,1)S(1)}, u32[]{:S(2)}, u32[]{:S(2)}) collective-permute-start(bf16[256,768]{1,0:T(8,128)(2,1)S(1)} %load.1), channel_id=1, source_target_pairs={{0,64},{32,224},{64,128},{96,32},{128,192},{160,96},{192,0},{224,1... | collective-permute-start | bytes 1179656 | tf_op jit(solution)/shard_map/ppermute | solution.py:228
  62.4 5.5 %collective-permute-start.5 = (f32[32,768]{1,0:T(8,128)S(1)}, f32[32,768]{1,0:T(8,128)S(1)}, u32[]{:S(2)}, u32[]{:S(2)}) collective-permute-start(f32[32,768]{1,0:T(8,128)S(1)} %get-tuple-element.31), channel_id=1, source_target_pairs={{0,32},{32,0},{1,33},{33,1},{2,34},{34,2},{3,35},{35,3},{4,36},{36... | collective-permute-start | bytes 294920 | tf_op jit(solution)/shard_map/ppermute | solution.py:223

commit v11 on v10

--- a/solution.py
+++ b/solution.py
@@ -123,27 +123,24 @@
     out_ref[...] = (own_ref[...].astype(F32) + mate_ref[...].astype(F32) + far_ref[...].astype(F32)).astype(BF)
 
 
-def pack_kernel(most_ref, came_ref, place_ref, beside_ref, emb_hbm, out_ref, emb_ref, sems):
+def pack_kernel(most_ref, came_ref, place_ref, beside_ref, emb_ref, out_ref):
     chips, cols = out_ref.shape[0], out_ref.shape[1] // CORES
     rows = chips * SLOTS
-    half = emb_ref.shape[0] // 2
-    units, copies = [], []
-    for k in range(2):
-        part = slice(k * half, (k + 1) * half)
-        summed = most_ref[part, :] + came_ref[part, :].astype(F32)
-        unit = summed * lax.rsqrt(jnp.sum(summed * summed, axis=-1, keepdims=True) + 1e-06)
-        emb_ref[part, :] = unit
-        copies.append(pltpu.make_async_copy(emb_ref.at[part], emb_hbm.at[part], sems.at[k]))
-        copies[k].start()
-        units.append(unit.astype(BF))
-    moved = jnp.dot(place_ref[...], jnp.concatenate(units, axis=0), preferred_element_type=F32).astype(BF)
+    summed = most_ref[...] + came_ref[...].astype(F32)
+    unit = summed * lax.rsqrt(jnp.sum(summed * summed, axis=-1, keepdims=True) + 1e-06)
+    emb_ref[...] = unit
+    moved = jnp.dot(place_ref[...], unit.astype(BF), preferred_element_type=F32).astype(BF)
     for core in range(CORES):
         for col in range(cols):
             block = moved[core * rows : (core + 1) * rows, col * LANES : (col + 1) * LANES]
             out_ref[:, core * cols + col] = block.reshape(chips, SLOTS, LANES)
     out_ref[:, CORES * cols] = beside_ref[...].reshape(chips, SLOTS, LANES)
-    for copy in copies:
-        copy.wait()
+
+
+def emit_kernel(unit_ref, out_hbm, sem):
+    copy = pltpu.make_async_copy(unit_ref, out_hbm, sem)
+    copy.start()
+    copy.wait()
 
 
 def combine_kernel(got_ref, mine_ref, other_ref):
@@ -262,13 +259,12 @@
     )(ids.reshape(1, labs))
     block = full((tile, width))
     message = (owners // CORES, CORES * cols + 1, SLOTS, LANES)
-    label_embed, rows = pl.pallas_call(
+    unit, rows = pl.pallas_call(
         pack_kernel,
         grid=(1,),
         out_shape=(jax.ShapeDtypeStruct((labs, width), F32), jax.ShapeDtypeStruct(message, BF)),
         in_specs=[block] * 2 + [full((SLOTS * owners, labs)), full((owners, LANES))],
-        out_specs=(hbm, full(message)),
-        scratch_shapes=[pltpu.VMEM((labs, width), F32), pltpu.SemaphoreType.DMA((2,))],
+        out_specs=(full((labs, width)), full(message)),
         compiler_params=params(),
         name="pack",
     )(most, came, place, beside)
@@ -283,6 +279,17 @@
         compiler_params=params(),
         name="combine",
     )(got)
+    other, unit = lax.optimization_barrier((other, unit))
+    label_embed = pl.pallas_call(
+        emit_kernel,
+        grid=(1,),
+        out_shape=jax.ShapeDtypeStruct((labs, width), F32),
+        in_specs=[full((labs, width))],
+        out_specs=hbm,
+        scratch_shapes=[pltpu.SemaphoreType.DMA],
+        compiler_params=params(),
+        name="emit",
+    )(unit)
     centroids = pl.pallas_call(
         finish_kernel,
         grid=(1,),

time: 68.8 us -> 68.6 us (level)
  waiting for transfers between devices: 12.8 us -> 11.1 us
    ppermute x3, waiting for transfers between devices: 2.27 us -> 1.05 us  [across(): return lax.ppermute(block, 'c', [(0, 1), (1, 0)])]
    pallas_call x0 -> x1, Pallas kernels: none -> 0.89 us  [shards(): pl.pallas_call(emit_kernel, grid=(1,), out_shape=jax.ShapeDtypeStruct((la...]
    ppermute x3, starting transfers between devices: 1.38 us -> 2.12 us  [along(): return lax.ppermute(block, INST, pairs)]
  transfers between devices with their start and end apart: 6 -> 6, of which waited for: 5 -> 4; matrix products, arithmetic and copies ran while one was open for 0% -> 0% of each run, Pallas kernels for 5% -> 6%
where the time goes in v11:
time: 68.6 us; the launch traced here: 68.5 us
  blocking collectives  38.2 us (56%)
  waiting for transfers between devices  11.1 us (16%)
  starting transfers between devices  9.67 us (14%)
  Pallas kernels  8.37 us (12%)
  between operations  0.74 us (1%)
    all_to_all x1, blocking collectives, shards(): got = lax.all_to_all(rows, ('x',) + LAB, 0, 0, tiled=True)  38.2 us
    ppermute x3, waiting for transfers between devices, along(): return lax.ppermute(block, INST, pairs)  10.1 us
    ppermute x3, starting transfers between devices, across(): return lax.ppermute(block, 'c', [(0, 1), (1, 0)])  7.55 us
    pallas_call x2, Pallas kernels, later(): pl.pallas_call(functools.partial(later_kernel, jobs), grid=(1,), out_shap...  2.82 us
    ppermute x3, starting transfers between devices, along(): return lax.ppermute(block, INST, pairs)  2.12 us
    pallas_call x1, Pallas kernels, shards(): pl.pallas_call(functools.partial(first_kernel, far_steps), grid=(1,), out...  1.92 us
  transfers between devices with their start and end apart: 6, of which 4 were waited for; matrix products, arithmetic and copies ran while one was open for 0% of the time, Pallas kernels for 6%

profile of v11, /device:TPU:1, one launch (start us, length us, event | category | flops | bytes accessed | tf_op | source)
XLA Modules:
  0.0 68.5 jit_solution(13704754992983280208)
XLA Ops:
  0.6 0.0 copy-start.1
  0.6 0.0 copy-start
  0.7 1.9 %far_away.1 = (bf16[256,768]{1,0:T(8,128)(2,1)S(1)}, bf16[512,768]{1,0:T(8,128)(2,1)S(1)}, bf16[8,256,256]{2,1,0:T(8,128)(2,1)S(1)}) custom-call(s32[8]{0:T(128)} %rows_ref.3, s32[8]{0:T(128)} %labs_ref.3, bf16[8,256,256]{2,1,0:T(8,128)(2,1)} %vals_hbm.1, bf16[512,768]{1,0:T(8,128)(2,1)} %feat_hbm.1), custom_call_target="tpu_custom_call" | custom-call | flops 100663296 | bytes 2228224 | tf_op jit(solution)/shard_map/far_away/pallas_call | solution.py:189
  2.6 3.2 %collective-permute-start = (bf16[256,768]{1,0:T(8,128)(2,1)S(1)}, bf16[256,768]{1,0:T(8,128)(2,1)S(1)}, u32[]{:S(2)}, u32[]{:S(2)}) collective-permute-start(bf16[256,768]{1,0:T(8,128)(2,1)S(1)} %get-tuple-element.23), channel_id=1, source_target_pairs={{0,32},{32,0},{1,33},{33,1},{2,34},{34,2},{3,35},{35,3},{4,36},{36... | collective-permute-start | bytes 1179656 | tf_op jit(solution)/shard_map/ppermute | solution.py:220
  5.8 0.0 copy-done.1
  5.8 0.0 copy-done
  5.8 1.8 %far_own.1 = (bf16[256,768]{1,0:T(8,128)(2,1)S(1)}, bf16[768,768]{1,0:T(8,128)(2,1)S(1)}) custom-call(s32[8]{0:T(128)S(1)} %copy-done, s32[8]{0:T(128)S(1)} %copy-done.1, bf16[8,256,256]{2,1,0:T(8,128)(2,1)S(1)} %get-tuple-element.19.vals_ref, bf16[512,768]{1,0:T(8,128)(2,1)S(1)} %get-tuple-element.24.x_ref), custom_call_target="tpu_custom_call" | custom-call | flops 402653184 | bytes 3407872 | tf_op jit(solution)/shard_map/far_own/pallas_call | solution.py:208
  7.6 0.0 collective-permute-done
  7.6 0.1 add_convert_fusion.1
  7.8 0.1 collective-permute-start.1
  7.9 0.8 %collective-permute-start.3 = (bf16[256,768]{1,0:T(8,128)(2,1)S(1)}, bf16[256,768]{1,0:T(8,128)(2,1)S(1)}, u32[]{:S(2)}, u32[]{:S(2)}) collective-permute-start(bf16[256,768]{1,0:T(8,128)(2,1)S(1)} %add_convert_fusion.1), channel_id=1, source_target_pairs={{0,64},{32,224},{64,128},{96,32},{128,192},{160,96},{192,0},{224,1... | collective-permute-start | bytes 1179656 | tf_op jit(solution)/shard_map/ppermute | solution.py:225
  8.7 1.0 %near_own.1.own_ref = bf16[768,768]{1,0:T(8,128)(2,1)S(1)} custom-call(s32[8]{0:T(128)S(1)} %copy-done, s32[8]{0:T(128)S(1)} %copy-done.1, bf16[8,256,256]{2,1,0:T(8,128)(2,1)S(1)} %get-tuple-element.19.vals_ref, bf16[512,768]{1,0:T(8,128)(2,1)S(1)} %get-tuple-element.24.x_ref), custom_call_target="tpu_custom_call" | custom-call | flops 301989888 | bytes 3014656 | tf_op jit(solution)/shard_map/near_own/pallas_call | solution.py:208
  9.7 1.0 %collective-permute-done.1.mate_ref = bf16[768,768]{1,0:T(8,128)(2,1)S(1)} collective-permute-done((bf16[768,768]{1,0:T(8,128)(2,1)S(1)}, bf16[768,768]{1,0:T(8,128)(2,1)S(1)}, u32[]{:S(2)}, u32[]{:S(2)}) %collective-permute-start.1) | collective-permute-done | bytes 1179680 | tf_op jit(solution)/shard_map/ppermute | solution.py:220
  10.7 0.1 add_convert_fusion
  10.8 0.0 copy-start.2
  10.8 0.2 collective-permute-start.2
  11.0 4.5 %collective-permute-done.3.far_ref = bf16[256,768]{1,0:T(8,128)(2,1)S(1)} collective-permute-done((bf16[256,768]{1,0:T(8,128)(2,1)S(1)}, bf16[256,768]{1,0:T(8,128)(2,1)S(1)}, u32[]{:S(2)}, u32[]{:S(2)}) %collective-permute-start.3) | collective-permute-done | bytes 393248 | tf_op jit(solution)/shard_map/ppermute | solution.py:225
  15.5 0.1 load.1
  15.6 1.1 %collective-permute-start.4 = (bf16[256,768]{1,0:T(8,128)(2,1)S(1)}, bf16[256,768]{1,0:T(8,128)(2,1)S(1)}, u32[]{:S(2)}, u32[]{:S(2)}) collective-permute-start(bf16[256,768]{1,0:T(8,128)(2,1)S(1)} %load.1), channel_id=1, source_target_pairs={{0,64},{32,224},{64,128},{96,32},{128,192},{160,96},{192,0},{224,1... | collective-permute-start | bytes 1179656 | tf_op jit(solution)/shard_map/ppermute | solution.py:225
  16.7 0.0 copy-done.2
  16.7 0.5 route.1
  17.2 3.7 %collective-permute-done.2 = bf16[256,768]{1,0:T(8,128)(2,1)S(1)} collective-permute-done((bf16[256,768]{1,0:T(8,128)(2,1)S(1)}, bf16[256,768]{1,0:T(8,128)(2,1)S(1)}, u32[]{:S(2)}, u32[]{:S(2)}) %collective-permute-start.2) | collective-permute-done | bytes 393248 | tf_op jit(solution)/shard_map/ppermute | solution.py:225
  20.9 0.2 convert_add_fusion.most_ref
  21.0 1.9 %collective-permute-done.4.came_ref = bf16[256,768]{1,0:T(8,128)(2,1)S(1)} collective-permute-done((bf16[256,768]{1,0:T(8,128)(2,1)S(1)}, bf16[256,768]{1,0:T(8,128)(2,1)S(1)}, u32[]{:S(2)}, u32[]{:S(2)}) %collective-permute-start.4) | collective-permute-done | bytes 393248 | tf_op jit(solution)/shard_map/ppermute | solution.py:225
  23.0 0.9 %pack.1 = (f32[256,768]{1,0:T(8,128)S(1)}, bf16[128,13,2,128]{3,2,1,0:T(2,128)(2,1)S(1)}) custom-call(f32[256,768]{1,0:T(8,128)S(1)} %convert_add_fusion.most_ref, bf16[256,768]{1,0:T(8,128)(2,1)S(1)} %collective-permute-done.4.came_ref, bf16[512,256]{1,0:T(8,128)(2,1)S(1)} %get-tuple-element.28.place_ref, bf16[256,128]{1,0:T(8,128)(2,1)S(1)} %get-tuple-element.29.beside_ref), custom_call_target="tpu_custom_call" | custom-call | tf_op jit(solution)/shard_map/pack/pallas_call | solution.py:262
  23.9 38.2 %all_to_all.5.got_ref = bf16[128,13,2,128]{3,2,1,0:T(2,128)(2,1)S(1)} all-to-all(bf16[128,13,2,128]{3,2,1,0:T(2,128)(2,1)S(1)} %get-tuple-element.30), channel_id=1, replica_groups=mesh['x'=4,'c'=2,'z'=8,'y'=4] {'x','z','y'}, dimensions={0} | all-to-all | bytes 1703936 | tf_op jit(solution)/shard_map/all_to_all | solution.py:271
  62.1 0.5 combine.1
  62.6 4.2 %collective-permute-start.5 = (f32[32,768]{1,0:T(8,128)S(1)}, f32[32,768]{1,0:T(8,128)S(1)}, u32[]{:S(2)}, u32[]{:S(2)}) collective-permute-start(f32[32,768]{1,0:T(8,128)S(1)} %get-tuple-element.35), channel_id=1, source_target_pairs={{0,32},{32,0},{1,33},{33,1},{2,34},{34,2},{3,35},{35,3},{4,36},{36... | collective-permute-start | bytes 294920 | tf_op jit(solution)/shard_map/ppermute | solution.py:220
  66.8 0.9 %emit.1 = f32[256,768]{1,0:T(8,128)} custom-call(f32[256,768]{1,0:T(8,128)S(1)} %get-tuple-element.33.unit_ref), custom_call_target="tpu_custom_call" | custom-call | tf_op jit(solution)/shard_map/emit/pallas_call | solution.py:283
  67.7 0.1 collective-permute-done.5.mate_ref
  67.8 0.7 %finish.1 = f32[32,768]{1,0:T(8,128)} custom-call(f32[32,768]{1,0:T(8,128)S(1)} %get-tuple-element.34.mine_ref, f32[32,768]{1,0:T(8,128)S(1)} %collective-permute-done.5.mate_ref), custom_call_target="tpu_custom_call" | custom-call | tf_op jit(solution)/shard_map/finish/pallas_call | solution.py:293
Async XLA Ops:
  0.6 5.2 %copy-start.1 = (s32[8]{0:T(128)S(1)}, s32[8]{0:T(128)}, u32[]{:S(2)}) copy-start(s32[8]{0:T(128)} %labs_ref.3) | copy-start | bytes 100
  0.6 5.2 %copy-start = (s32[8]{0:T(128)S(1)}, s32[8]{0:T(128)}, u32[]{:S(2)}) copy-start(s32[8]{0:T(128)} %rows_ref.3) | copy-start | bytes 100
  2.6 5.1 %collective-permute-start = (bf16[256,768]{1,0:T(8,128)(2,1)S(1)}, bf16[256,768]{1,0:T(8,128)(2,1)S(1)}, u32[]{:S(2)}, u32[]{:S(2)}) collective-permute-start(bf16[256,768]{1,0:T(8,128)(2,1)S(1)} %get-tuple-element.23), channel_id=1, source_target_pairs={{0,32},{32,0},{1,33},{33,1},{2,34},{34,2},{3,35},{35,3},{4,36},{36... | collective-permute-start | bytes 1179656 | tf_op jit(solution)/shard_map/ppermute | solution.py:220
  7.8 2.9 %collective-permute-start.1 = (bf16[768,768]{1,0:T(8,128)(2,1)S(1)}, bf16[768,768]{1,0:T(8,128)(2,1)S(1)}, u32[]{:S(2)}, u32[]{:S(2)}) collective-permute-start(bf16[768,768]{1,0:T(8,128)(2,1)S(1)} %get-tuple-element.25), channel_id=1, source_target_pairs={{0,32},{32,0},{1,33},{33,1},{2,34},{34,2},{3,35},{35,3},{4,36},{36... | collective-permute-start | bytes 3538952 | tf_op jit(solution)/shard_map/ppermute | solution.py:220
  7.9 7.6 %collective-permute-start.3 = (bf16[256,768]{1,0:T(8,128)(2,1)S(1)}, bf16[256,768]{1,0:T(8,128)(2,1)S(1)}, u32[]{:S(2)}, u32[]{:S(2)}) collective-permute-start(bf16[256,768]{1,0:T(8,128)(2,1)S(1)} %add_convert_fusion.1), channel_id=1, source_target_pairs={{0,64},{32,224},{64,128},{96,32},{128,192},{160,96},{192,0},{224,1... | collective-permute-start | bytes 1179656 | tf_op jit(solution)/shard_map/ppermute | solution.py:225
  10.8 6.0 %copy-start.2 = (s32[256]{0:T(256)S(1)}, s32[256]{0:T(256)}, u32[]{:S(2)}) copy-start(s32[256]{0:T(256)} %param.9) | copy-start | bytes 3076
  10.8 10.1 %collective-permute-start.2 = (bf16[256,768]{1,0:T(8,128)(2,1)S(1)}, bf16[256,768]{1,0:T(8,128)(2,1)S(1)}, u32[]{:S(2)}, u32[]{:S(2)}) collective-permute-start(bf16[256,768]{1,0:T(8,128)(2,1)S(1)} %add_convert_fusion), channel_id=1, source_target_pairs={{0,192},{32,96},{64,0},{96,160},{128,64},{160,224},{192,128},{224,... | collective-permute-start | bytes 1179656 | tf_op jit(solution)/shard_map/ppermute | solution.py:225
  15.6 7.4 %collective-permute-start.4 = (bf16[256,768]{1,0:T(8,128)(2,1)S(1)}, bf16[256,768]{1,0:T(8,128)(2,1)S(1)}, u32[]{:S(2)}, u32[]{:S(2)}) collective-permute-start(bf16[256,768]{1,0:T(8,128)(2,1)S(1)} %load.1), channel_id=1, source_target_pairs={{0,64},{32,224},{64,128},{96,32},{128,192},{160,96},{192,0},{224,1... | collective-permute-start | bytes 1179656 | tf_op jit(solution)/shard_map/ppermute | solution.py:225
  62.6 5.1 %collective-permute-start.5 = (f32[32,768]{1,0:T(8,128)S(1)}, f32[32,768]{1,0:T(8,128)S(1)}, u32[]{:S(2)}, u32[]{:S(2)}) collective-permute-start(f32[32,768]{1,0:T(8,128)S(1)} %get-tuple-element.35), channel_id=1, source_target_pairs={{0,32},{32,0},{1,33},{33,1},{2,34},{34,2},{3,35},{35,3},{4,36},{36... | collective-permute-start | bytes 294920 | tf_op jit(solution)/shard_map/ppermute | solution.py:220

commit v12 on v10

--- a/solution.py
+++ b/solution.py
@@ -162,11 +162,11 @@
         sums.append(both[core * part : core * part + CL_OWN])
     first = lax.axis_index("c") == 0
     mine_ref[...] = jnp.where(first, sums[0], sums[1])
-    other_ref[...] = jnp.where(first, sums[1], sums[0])
+    other_ref[...] = jnp.where(first, sums[1], sums[0]).astype(BF)
 
 
 def finish_kernel(mine_ref, mate_ref, out_ref):
-    sums = mine_ref[...] + mate_ref[...]
+    sums = mine_ref[...] + mate_ref[...].astype(F32)
     out_ref[...] = sums * lax.rsqrt(jnp.sum(sums * sums, axis=-1, keepdims=True) + 1e-06)
 
 
@@ -277,7 +277,7 @@
     mine, other = pl.pallas_call(
         combine_kernel,
         grid=(1,),
-        out_shape=(sums, sums),
+        out_shape=(sums, jax.ShapeDtypeStruct(sums.shape, BF)),
         in_specs=[full(message)],
         out_specs=(full(sums.shape), full(sums.shape)),
         compiler_params=params(),

time: 68.8 us -> 68.4 us (level)
  starting transfers between devices: 9.26 us -> 11.9 us
  waiting for transfers between devices: 12.8 us -> 10.8 us
  blocking collectives: 37.7 us -> 36.7 us
    ppermute x3, starting transfers between devices: 1.38 us -> 2.75 us  [along(): return lax.ppermute(block, INST, pairs)]
    ppermute x3, waiting for transfers between devices: 2.27 us -> 0.96 us  [across(): return lax.ppermute(block, 'c', [(0, 1), (1, 0)])]
    ppermute x3, starting transfers between devices: 7.87 us -> 9.13 us  [across(): return lax.ppermute(block, 'c', [(0, 1), (1, 0)])]
    all_to_all x1, blocking collectives: 37.7 us -> 36.7 us  [shards(): got = lax.all_to_all(rows, ('x',) + LAB, 0, 0, tiled=True)]
    ppermute x3, waiting for transfers between devices: 10.5 us -> 9.8 us  [along(): return lax.ppermute(block, INST, pairs)]
where the time goes in v12:
time: 68.4 us; the launch traced here: 68.2 us
  blocking collectives  36.7 us (54%)
  starting transfers between devices  11.9 us (17%)
  waiting for transfers between devices  10.8 us (16%)
  Pallas kernels  7.81 us (11%)
  between operations  0.73 us (1%)
    all_to_all x1, blocking collectives, shards(): got = lax.all_to_all(rows, ('x',) + LAB, 0, 0, tiled=True)  36.7 us
    ppermute x3, waiting for transfers between devices, along(): return lax.ppermute(block, INST, pairs)  9.8 us
    ppermute x3, starting transfers between devices, across(): return lax.ppermute(block, 'c', [(0, 1), (1, 0)])  9.13 us
    pallas_call x2, Pallas kernels, later(): pl.pallas_call(functools.partial(later_kernel, jobs), grid=(1,), out_shap...  3 us
    ppermute x3, starting transfers between devices, along(): return lax.ppermute(block, INST, pairs)  2.75 us
    pallas_call x1, Pallas kernels, shards(): pl.pallas_call(functools.partial(first_kernel, far_steps), grid=(1,), out...  1.92 us
  transfers between devices with their start and end apart: 6, of which 5 were waited for; matrix products, arithmetic and copies ran while one was open for 0% of the time, Pallas kernels for 5%

profile of v12, /device:TPU:1, one launch (start us, length us, event | category | flops | bytes accessed | tf_op | source)
XLA Modules:
  0.0 68.2 jit_solution(1241220681112216622)
XLA Ops:
  0.6 0.0 copy-start.1
  0.6 0.0 copy-start
  0.7 1.9 %far_away.1 = (bf16[256,768]{1,0:T(8,128)(2,1)S(1)}, bf16[512,768]{1,0:T(8,128)(2,1)S(1)}, bf16[8,256,256]{2,1,0:T(8,128)(2,1)S(1)}) custom-call(s32[8]{0:T(128)} %rows_ref.3, s32[8]{0:T(128)} %labs_ref.3, bf16[8,256,256]{2,1,0:T(8,128)(2,1)} %vals_hbm.1, bf16[512,768]{1,0:T(8,128)(2,1)} %feat_hbm.1), custom_call_target="tpu_custom_call" | custom-call | flops 100663296 | bytes 2228224 | tf_op jit(solution)/shard_map/far_away/pallas_call | solution.py:192
  2.6 3.2 %collective-permute-start = (bf16[256,768]{1,0:T(8,128)(2,1)S(1)}, bf16[256,768]{1,0:T(8,128)(2,1)S(1)}, u32[]{:S(2)}, u32[]{:S(2)}) collective-permute-start(bf16[256,768]{1,0:T(8,128)(2,1)S(1)} %get-tuple-element.21), channel_id=1, source_target_pairs={{0,32},{32,0},{1,33},{33,1},{2,34},{34,2},{3,35},{35,3},{4,36},{36... | collective-permute-start | bytes 1179656 | tf_op jit(solution)/shard_map/ppermute | solution.py:223
  5.8 0.0 copy-done.1
  5.8 0.0 copy-done
  5.8 1.4 %far_own.1 = (bf16[256,768]{1,0:T(8,128)(2,1)S(1)}, bf16[768,768]{1,0:T(8,128)(2,1)S(1)}) custom-call(s32[8]{0:T(128)S(1)} %copy-done, s32[8]{0:T(128)S(1)} %copy-done.1, bf16[8,256,256]{2,1,0:T(8,128)(2,1)S(1)} %get-tuple-element.17.vals_ref, bf16[512,768]{1,0:T(8,128)(2,1)S(1)} %get-tuple-element.22.x_ref), custom_call_target="tpu_custom_call" | custom-call | flops 402653184 | bytes 3407872 | tf_op jit(solution)/shard_map/far_own/pallas_call | solution.py:211
  7.3 0.0 collective-permute-done
  7.3 0.1 add_convert_fusion.1
  7.4 0.5 collective-permute-start.1
  7.9 0.8 %collective-permute-start.3 = (bf16[256,768]{1,0:T(8,128)(2,1)S(1)}, bf16[256,768]{1,0:T(8,128)(2,1)S(1)}, u32[]{:S(2)}, u32[]{:S(2)}) collective-permute-start(bf16[256,768]{1,0:T(8,128)(2,1)S(1)} %add_convert_fusion.1), channel_id=1, source_target_pairs={{0,64},{32,224},{64,128},{96,32},{128,192},{160,96},{192,0},{224,1... | collective-permute-start | bytes 1179656 | tf_op jit(solution)/shard_map/ppermute | solution.py:228
  8.7 1.6 %near_own.1.own_ref = bf16[768,768]{1,0:T(8,128)(2,1)S(1)} custom-call(s32[8]{0:T(128)S(1)} %copy-done, s32[8]{0:T(128)S(1)} %copy-done.1, bf16[8,256,256]{2,1,0:T(8,128)(2,1)S(1)} %get-tuple-element.17.vals_ref, bf16[512,768]{1,0:T(8,128)(2,1)S(1)} %get-tuple-element.22.x_ref), custom_call_target="tpu_custom_call" | custom-call | flops 301989888 | bytes 3014656 | tf_op jit(solution)/shard_map/near_own/pallas_call | solution.py:211
  10.3 0.1 collective-permute-done.1.mate_ref
  10.3 0.1 add_convert_fusion
  10.4 0.0 copy-start.2
  10.5 0.7 %collective-permute-start.2 = (bf16[256,768]{1,0:T(8,128)(2,1)S(1)}, bf16[256,768]{1,0:T(8,128)(2,1)S(1)}, u32[]{:S(2)}, u32[]{:S(2)}) collective-permute-start(bf16[256,768]{1,0:T(8,128)(2,1)S(1)} %add_convert_fusion), channel_id=1, source_target_pairs={{0,192},{32,96},{64,0},{96,160},{128,64},{160,224},{192,128},{224,... | collective-permute-start | bytes 1179656 | tf_op jit(solution)/shard_map/ppermute | solution.py:228
  11.2 4.2 %collective-permute-done.3.far_ref = bf16[256,768]{1,0:T(8,128)(2,1)S(1)} collective-permute-done((bf16[256,768]{1,0:T(8,128)(2,1)S(1)}, bf16[256,768]{1,0:T(8,128)(2,1)S(1)}, u32[]{:S(2)}, u32[]{:S(2)}) %collective-permute-start.3) | collective-permute-done | bytes 393248 | tf_op jit(solution)/shard_map/ppermute | solution.py:228
  15.4 0.1 load.1
  15.6 1.2 %collective-permute-start.4 = (bf16[256,768]{1,0:T(8,128)(2,1)S(1)}, bf16[256,768]{1,0:T(8,128)(2,1)S(1)}, u32[]{:S(2)}, u32[]{:S(2)}) collective-permute-start(bf16[256,768]{1,0:T(8,128)(2,1)S(1)} %load.1), channel_id=1, source_target_pairs={{0,64},{32,224},{64,128},{96,32},{128,192},{160,96},{192,0},{224,1... | collective-permute-start | bytes 1179656 | tf_op jit(solution)/shard_map/ppermute | solution.py:228
  16.8 0.0 copy-done.2
  16.8 0.5 route.1
  17.2 3.3 %collective-permute-done.2 = bf16[256,768]{1,0:T(8,128)(2,1)S(1)} collective-permute-done((bf16[256,768]{1,0:T(8,128)(2,1)S(1)}, bf16[256,768]{1,0:T(8,128)(2,1)S(1)}, u32[]{:S(2)}, u32[]{:S(2)}) %collective-permute-start.2) | collective-permute-done | bytes 393248 | tf_op jit(solution)/shard_map/ppermute | solution.py:228
  20.5 0.1 convert_add_fusion.most_ref
  20.6 2.3 %collective-permute-done.4.came_ref = bf16[256,768]{1,0:T(8,128)(2,1)S(1)} collective-permute-done((bf16[256,768]{1,0:T(8,128)(2,1)S(1)}, bf16[256,768]{1,0:T(8,128)(2,1)S(1)}, u32[]{:S(2)}, u32[]{:S(2)}) %collective-permute-start.4) | collective-permute-done | bytes 393248 | tf_op jit(solution)/shard_map/ppermute | solution.py:228
  22.9 1.0 %pack.1 = (f32[256,768]{1,0:T(8,128)}, bf16[128,13,2,128]{3,2,1,0:T(2,128)(2,1)S(1)}) custom-call(f32[256,768]{1,0:T(8,128)S(1)} %convert_add_fusion.most_ref, bf16[256,768]{1,0:T(8,128)(2,1)S(1)} %collective-permute-done.4.came_ref, bf16[512,256]{1,0:T(8,128)(2,1)S(1)} %get-tuple-element.26.place_ref, bf16[256,128]{1,0:T(8,128)(2,1)S(1)} %get-tuple-element.27.beside_ref), custom_call_target="tpu_custom_call" | custom-call | tf_op jit(solution)/shard_map/pack/pallas_call | solution.py:265
  24.0 36.7 %all_to_all.5.got_ref = bf16[128,13,2,128]{3,2,1,0:T(2,128)(2,1)S(1)} all-to-all(bf16[128,13,2,128]{3,2,1,0:T(2,128)(2,1)S(1)} %get-tuple-element.29), channel_id=1, replica_groups=mesh['x'=4,'c'=2,'z'=8,'y'=4] {'x','z','y'}, dimensions={0} | all-to-all | bytes 1703936 | tf_op jit(solution)/shard_map/all_to_all | solution.py:275
  60.7 0.5 combine.1
  61.2 5.4 %collective-permute-start.5 = (bf16[32,768]{1,0:T(8,128)(2,1)S(1)}, bf16[32,768]{1,0:T(8,128)(2,1)S(1)}, u32[]{:S(2)}, u32[]{:S(2)}) collective-permute-start(bf16[32,768]{1,0:T(8,128)(2,1)S(1)} %get-tuple-element.31), channel_id=1, source_target_pairs={{0,32},{32,0},{1,33},{33,1},{2,34},{34,2},{3,35},{35,3},{4,36},{36... | collective-permute-start | bytes 147464 | tf_op jit(solution)/shard_map/ppermute | solution.py:223
  66.6 0.9 %collective-permute-done.5.mate_ref = bf16[32,768]{1,0:T(8,128)(2,1)S(1)} collective-permute-done((bf16[32,768]{1,0:T(8,128)(2,1)S(1)}, bf16[32,768]{1,0:T(8,128)(2,1)S(1)}, u32[]{:S(2)}, u32[]{:S(2)}) %collective-permute-start.5) | collective-permute-done | bytes 49184 | tf_op jit(solution)/shard_map/ppermute | solution.py:223
  67.5 0.7 %finish.1 = f32[32,768]{1,0:T(8,128)} custom-call(f32[32,768]{1,0:T(8,128)S(1)} %get-tuple-element.30.mine_ref, bf16[32,768]{1,0:T(8,128)(2,1)S(1)} %collective-permute-done.5.mate_ref), custom_call_target="tpu_custom_call" | custom-call | tf_op jit(solution)/shard_map/finish/pallas_call | solution.py:286
Async XLA Ops:
  0.6 5.2 %copy-start.1 = (s32[8]{0:T(128)S(1)}, s32[8]{0:T(128)}, u32[]{:S(2)}) copy-start(s32[8]{0:T(128)} %labs_ref.3) | copy-start | bytes 100
  0.6 5.2 %copy-start = (s32[8]{0:T(128)S(1)}, s32[8]{0:T(128)}, u32[]{:S(2)}) copy-start(s32[8]{0:T(128)} %rows_ref.3) | copy-start | bytes 100
  2.6 4.7 %collective-permute-start = (bf16[256,768]{1,0:T(8,128)(2,1)S(1)}, bf16[256,768]{1,0:T(8,128)(2,1)S(1)}, u32[]{:S(2)}, u32[]{:S(2)}) collective-permute-start(bf16[256,768]{1,0:T(8,128)(2,1)S(1)} %get-tuple-element.21), channel_id=1, source_target_pairs={{0,32},{32,0},{1,33},{33,1},{2,34},{34,2},{3,35},{35,3},{4,36},{36... | collective-permute-start | bytes 1179656 | tf_op jit(solution)/shard_map/ppermute | solution.py:223
  7.4 3.0 %collective-permute-start.1 = (bf16[768,768]{1,0:T(8,128)(2,1)S(1)}, bf16[768,768]{1,0:T(8,128)(2,1)S(1)}, u32[]{:S(2)}, u32[]{:S(2)}) collective-permute-start(bf16[768,768]{1,0:T(8,128)(2,1)S(1)} %get-tuple-element.23), channel_id=1, source_target_pairs={{0,32},{32,0},{1,33},{33,1},{2,34},{34,2},{3,35},{35,3},{4,36},{36... | collective-permute-start | bytes 3538952 | tf_op jit(solution)/shard_map/ppermute | solution.py:223
  7.9 7.6 %collective-permute-start.3 = (bf16[256,768]{1,0:T(8,128)(2,1)S(1)}, bf16[256,768]{1,0:T(8,128)(2,1)S(1)}, u32[]{:S(2)}, u32[]{:S(2)}) collective-permute-start(bf16[256,768]{1,0:T(8,128)(2,1)S(1)} %add_convert_fusion.1), channel_id=1, source_target_pairs={{0,64},{32,224},{64,128},{96,32},{128,192},{160,96},{192,0},{224,1... | collective-permute-start | bytes 1179656 | tf_op jit(solution)/shard_map/ppermute | solution.py:228
  10.4 6.3 %copy-start.2 = (s32[256]{0:T(256)S(1)}, s32[256]{0:T(256)}, u32[]{:S(2)}) copy-start(s32[256]{0:T(256)} %param.9) | copy-start | bytes 3076
  10.5 10.0 %collective-permute-start.2 = (bf16[256,768]{1,0:T(8,128)(2,1)S(1)}, bf16[256,768]{1,0:T(8,128)(2,1)S(1)}, u32[]{:S(2)}, u32[]{:S(2)}) collective-permute-start(bf16[256,768]{1,0:T(8,128)(2,1)S(1)} %add_convert_fusion), channel_id=1, source_target_pairs={{0,192},{32,96},{64,0},{96,160},{128,64},{160,224},{192,128},{224,... | collective-permute-start | bytes 1179656 | tf_op jit(solution)/shard_map/ppermute | solution.py:228
  15.6 7.3 %collective-permute-start.4 = (bf16[256,768]{1,0:T(8,128)(2,1)S(1)}, bf16[256,768]{1,0:T(8,128)(2,1)S(1)}, u32[]{:S(2)}, u32[]{:S(2)}) collective-permute-start(bf16[256,768]{1,0:T(8,128)(2,1)S(1)} %load.1), channel_id=1, source_target_pairs={{0,64},{32,224},{64,128},{96,32},{128,192},{160,96},{192,0},{224,1... | collective-permute-start | bytes 1179656 | tf_op jit(solution)/shard_map/ppermute | solution.py:228
  61.2 6.3 %collective-permute-start.5 = (bf16[32,768]{1,0:T(8,128)(2,1)S(1)}, bf16[32,768]{1,0:T(8,128)(2,1)S(1)}, u32[]{:S(2)}, u32[]{:S(2)}) collective-permute-start(bf16[32,768]{1,0:T(8,128)(2,1)S(1)} %get-tuple-element.31), channel_id=1, source_target_pairs={{0,32},{32,0},{1,33},{33,1},{2,34},{34,2},{3,35},{35,3},{4,36},{36... | collective-permute-start | bytes 147464 | tf_op jit(solution)/shard_map/ppermute | solution.py:223
